TPU v7x, 256 devices: a whole 4x4x8 slice. The times are simulated.
256 devices in a mesh: trial: 8 (over y_hi, x), dp: 8 (over z), tensor: 4 (over y_lo, core).
Axes of the slice: x: 4, y: 4 (y_hi: 2, y_lo: 2; y = y_hi * 2 + y_lo), z: 8, core: 2. Of those that a mesh axis runs over, the one named last changes fastest.
Arguments:
- residual_rows: bfloat16 [32768, 8192], P(('trial', 'dp', 'tensor'))
- input_norm_weight: float32 [8192], replicated, may hold values from 0.25 to 1.75
- trial_row_index: int32 [8, 4096], P(None, 'dp'), may hold values from 0 to 127, as said below
- keyvalue_weight: bfloat16 [8192, 2048], P('tensor'), may hold values from -0.0625 to 0.0625
- adapter_down_weight: bfloat16 [8, 8192, 128], P('trial', 'tensor'), may hold values from -0.0625 to 0.0625
- adapter_up_weight: bfloat16 [8, 64, 2048], P('trial'), may hold values from -0.75 to 0.75
- keyvalue_gradient: bfloat16 [8, 4096, 2048], P('trial', ('dp', 'tensor')), may hold values from -6 to 6
Outputs:
- keyvalue_output: float32 [8, 4096, 2048], P('trial', ('dp', 'tensor'))
- grad_a: float32 [8, 128, 8192], P('trial', 'dp', 'tensor')
- grad_b: float32 [8, 64, 2048], P('trial', None, ('dp', 'tensor'))
Inputs may be any that keep to these rules, and one draw needn't show every extreme that they name: `trial_row_index`: within each trial, each index of dp and each block of 16 consecutive tokens taken from one source device, the rows named are distinct.
All inputs are finite; a program needn't handle non-finite values.
Results may differ from a plain program's by a relative error of at most 0.0041.
Values may be sent and summed in bfloat16 or wider, within the bound.
A program may use at most 64 MiB of HBM per device.

v0:
```python
import jax
import jax.numpy as jnp
from jax import lax
from jax.sharding import PartitionSpec as P

adapter_scale = 2.0
norm_eps = 1e-05


def shards(
    residual_rows,
    input_norm_weight,
    trial_row_index,
    keyvalue_weight,
    adapter_down_weight,
    adapter_up_weight,
    keyvalue_gradient,
):
    trials = lax.axis_size("trial")
    tensors = lax.axis_size("tensor")
    tok_dev = trial_row_index.shape[1]
    select = tok_dev // (trials * tensors)
    normed_input = keyvalue_weight.shape[0]
    kv_width = keyvalue_weight.shape[1]
    keyvalue_half = kv_width // 2
    rank_index = adapter_up_weight.shape[1]
    highest_precision = lax.Precision.HIGHEST
    wide = residual_rows.astype(jnp.float32)
    msq = jnp.mean(wide * wide, axis=1, keepdims=True)
    normed = (wide * lax.rsqrt(msq + norm_eps) * input_norm_weight[None, :]).astype(jnp.bfloat16)
    source = lax.axis_index("trial") * tensors + lax.axis_index("tensor")
    picks = lax.dynamic_slice_in_dim(trial_row_index, source * select, select, 1)
    chosen = jnp.take(normed, picks.reshape(-1), axis=0)
    chosen = chosen.reshape(trials, select, tensors, normed_input).transpose(0, 2, 1, 3)
    arrived = lax.all_to_all(
        chosen.reshape(trials * tensors, select, normed_input),
        ("trial", "tensor"),
        split_axis=0,
        concat_axis=0,
        tiled=True,
    )
    rows = arrived.reshape(tok_dev, normed_input)
    down_weight = adapter_down_weight[0]
    keyval = jnp.dot(rows, keyvalue_weight, preferred_element_type=jnp.float32)
    ranks = jnp.dot(rows, down_weight, preferred_element_type=jnp.float32)
    summed = lax.psum_scatter(
        jnp.concatenate([keyval, ranks], axis=1), "tensor", scatter_dimension=0, tiled=True
    )
    frozen_output_local = summed[:, :kv_width]
    local_rank_rows = summed[:, kv_width:]
    up_weight = adapter_up_weight[0].astype(jnp.float32)
    adapter_key = jnp.dot(
        local_rank_rows[:, :rank_index], up_weight[:, :keyvalue_half], precision=highest_precision
    )
    adapter_value = jnp.dot(
        local_rank_rows[:, rank_index:], up_weight[:, keyvalue_half:], precision=highest_precision
    )
    keyvalue_output = frozen_output_local + adapter_scale * jnp.concatenate(
        [adapter_key, adapter_value], axis=1
    )
    grad_in = keyvalue_gradient[0].astype(jnp.float32)
    key_gradient_full = jnp.dot(
        grad_in[:, :keyvalue_half], up_weight[:, :keyvalue_half].T, precision=highest_precision
    )
    value_gradient_full = jnp.dot(
        grad_in[:, keyvalue_half:], up_weight[:, keyvalue_half:].T, precision=highest_precision
    )
    rank_gradient = (
        adapter_scale * jnp.concatenate([key_gradient_full, value_gradient_full], axis=1)
    ).astype(jnp.bfloat16)
    every_rank = lax.all_gather(rank_gradient, "tensor", axis=0, tiled=True)
    grad_a_term = lax.dot_general(
        every_rank, rows, (((0,), (0,)), ((), ())), preferred_element_type=jnp.float32
    )
    grad_a = lax.psum_scatter(grad_a_term, "dp", scatter_dimension=0, tiled=True)
    key_down_gradient = jnp.dot(
        local_rank_rows[:, :rank_index].T, grad_in[:, :keyvalue_half], precision=highest_precision
    )
    value_down_gradient = jnp.dot(
        local_rank_rows[:, rank_index:].T, grad_in[:, keyvalue_half:], precision=highest_precision
    )
    up_gradient_term = adapter_scale * jnp.concatenate(
        [key_down_gradient, value_down_gradient], axis=1
    )
    grad_b = lax.psum_scatter(up_gradient_term, ("dp", "tensor"), scatter_dimension=1, tiled=True)
    return (keyvalue_output[None], grad_a[None], grad_b[None])


def solution(mesh):
    return jax.shard_map(
        shards,
        mesh=mesh,
        in_specs=(
            P(("trial", "dp", "tensor"), None),
            P(),
            P(None, "dp"),
            P("tensor", None),
            P("trial", "tensor", None),
            P("trial", None, None),
            P("trial", ("dp", "tensor"), None),
        ),
        out_specs=(
            P("trial", ("dp", "tensor"), None),
            P("trial", "dp", "tensor"),
            P("trial", None, ("dp", "tensor")),
        ),
        check_vma=False,
    )
```

profile of v0, /device:TPU:1, one launch (start us, length us, event | category | flops | bytes accessed | tf_op | source)
XLA Modules:
  0.0 282.0 jit_solution(9549503070303807925)
XLA Ops:
  7.2 2.1 fusion
  9.4 0.8 compare_and_fusion
  10.3 2.2 fusion.2
  12.4 3.2 %gather_fusion = bf16[128,8192]{1,0:T(8,128)(2,1)} fusion(bf16[128,8192]{1,0:T(8,128)(2,1)S(1)} %fusion.2, s32[1024]{0:T(1024)S(1)} %pad_clamp_fusion), kind=kCustom, calls=%fused_computation | custom fusion | bytes 4194816 | tf_op jit(solution)/shard_map/jit(_take)/gather | solution.py:33
  15.6 3.3 %gather.7 = bf16[8,16,4,2048]{3,2,1,0:T(4,128)(2,1)S(1)} reshape(bf16[128,8192]{1,0:T(8,128)(2,1)} %gather_fusion) | data formatting | bytes 4194304 | tf_op jit(solution)/shard_map/jit(_take)/gather | solution.py:33
  19.0 2.4 copy_select_fusion
  21.4 37.5 %all_to_all.5 = bf16[32,16,2048]{2,1,0:T(8,128)(2,1)S(1)} all-to-all(bf16[32,16,2048]{2,1,0:T(8,128)(2,1)S(1)} %bitcast.25), channel_id=1, replica_groups=mesh['trial'=8,'dp'=8,'tensor'=4] {'trial','tensor'}, dimensions={0} | all-to-all | bytes 4194304 | tf_op jit(solution)/shard_map/all_to_all | solution.py:35
  58.9 0.7 fusion.4
  59.6 6.9 %fusion.26 = f32[512,2048]{1,0:T(8,128)S(1)} fusion(bf16[512,2048]{1,0:T(8,128)(2,1)S(1)} %bitcast.23, bf16[2048,2048]{1,0:T(8,128)(2,1)} %param.10), kind=kOutput, calls=%fused_computation.41 | convolution fusion | flops 4294967296 | bytes 14680064 | tf_op jit(solution)/shard_map/dot_general | solution.py:44
  66.5 2.4 pad_maximum_fusion
  68.9 49.4 %reduce-scatter.6.cloned.1.call-done = f32[128,2176]{1,0:T(8,128)} async-done(((f32[512,2176]{1,0:T(8,128)}), f32[128,2176]{1,0:T(8,128)}) %reduce-scatter.6.cloned.1.call-update) | async-done | bytes 1114128 | tf_op jit(solution)/shard_map/reduce_scatter | solution.py:46
  118.4 1.2 fusion.10
  119.5 1.3 fusion.6
  120.9 1.4 copy.16
  122.3 1.2 fusion.12
  123.5 1.2 fusion.8
  124.6 5.7 %all_gather.3 = bf16[512,128]{0,1:T(8,128)(2,1)S(1)} all-gather(bf16[128,128]{0,1:T(8,128)(2,1)S(1)} %fusion.20), channel_id=1, replica_groups=mesh['trial'=8,'dp'=8,'tensor'=4] {'tensor'}, dimensions={0}, use_global_device_ids=true | all-gather | bytes 163840 | tf_op jit(solution)/shard_map/all_gather | solution.py:71
  130.3 1.4 fusion.27
  131.8 1.3 fusion.15
  133.1 1.2 fusion.18
  134.3 1.1 fusion.3
  135.5 100.6 %reduce-scatter.10.cloned.1.call-done = f32[64,64]{1,0:T(8,128)} async-done(((f32[2048,64]{1,0:T(8,128)}), f32[64,64]{1,0:T(8,128)}) %reduce-scatter.10.cloned.1.call-update) | async-done | bytes 16400
  236.0 1.5 copy.17
  237.5 38.0 %reduce-scatter.8.cloned.1.call-done = f32[16,2048]{1,0:T(8,128)} async-done(((f32[128,2048]{1,0:T(8,128)}), f32[16,2048]{1,0:T(8,128)}) %reduce-scatter.8.cloned.1.call-update) | async-done | bytes 131088 | tf_op jit(solution)/shard_map/reduce_scatter | solution.py:75
  (22 shorter events, 0.3 us)
Async XLA Ops:
  7.2 51.7 %copy-start = (bf16[1,2048,128]{2,1,0:T(8,128)(2,1)S(1)}, bf16[1,2048,128]{2,1,0:T(8,128)(2,1)}, u32[]{:S(2)}) copy-start(bf16[1,2048,128]{2,1,0:T(8,128)(2,1)} %param.11) | copy-start | bytes 1572868
  7.2 3.1 %copy-start.4 = (f32[8192]{0:T(1024)S(1)}, f32[8192]{0:T(1024)}, u32[]{:S(2)}) copy-start(f32[8192]{0:T(1024)} %param.8) | copy-start | bytes 98308
  7.2 111.2 %reduce-scatter.6.cloned.1.call-start = ((), (), s32[]{:S(2)}) async-start(), calls=%async_computation.4 | async-start | bytes 5570560 | tf_op jit(solution)/shard_map/reduce_scatter | solution.py:46
  68.9 49.5 %copy-start.2 = (bf16[1,128,2048]{2,1,0:T(8,128)(2,1)S(1)}, bf16[1,128,2048]{2,1,0:T(8,128)(2,1)}, u32[]{:S(2)}) copy-start(bf16[1,128,2048]{2,1,0:T(8,128)(2,1)} %param.13) | copy-start | bytes 1572868
  68.9 167.1 %reduce-scatter.10.cloned.1.call-start = ((), (), s32[]{:S(2)}) async-start(), calls=%async_computation.6 | async-start | bytes 1081344
  119.5 2.8 copy-start.3
  122.2 153.2 %reduce-scatter.8.cloned.1.call-start = ((), (), s32[]{:S(2)}) async-start(), calls=%async_computation.5 | async-start | bytes 1179648 | tf_op jit(solution)/shard_map/reduce_scatter | solution.py:75
  131.7 2.6 copy-start.1
Sparse Core Ops, SparseCore 0:
  69.0 49.2 reduce-scatter.5
  122.4 113.6 reduce-scatter.9
  239.3 36.1 reduce-scatter.7
where the time goes:
time: 286 us; the launch traced here: 282 us
  waiting for transfers between devices  188 us (66%)
  blocking collectives  43.2 us (15%)
  matrix products  16.3 us (6%)
  between operations  13.9 us (5%)
  other arithmetic  11.1 us (4%)
  local copies, waits for them, and re-layouts  9.43 us (3%)
    unnamed x4, waiting for transfers between devices  101 us
    reduce_scatter x1, waiting for transfers between devices, shards(): lax.psum_scatter(jnp.concatenate([keyval, ranks], axis=1), 'tensor', scat...  49.4 us
    reduce_scatter x1, waiting for transfers between devices, shards(): lax.psum_scatter(grad_a_term, 'dp', scatter_dimension=0, tiled=True)  38 us
    all_to_all x1, blocking collectives, shards(): lax.all_to_all(chosen.reshape(trials * tensors, select, normed_input), ('...  37.5 us
    dot_general x1, matrix products, shards(): keyval = jnp.dot(rows, keyvalue_weight, preferred_element_type=jnp.float32)  6.89 us
    gather x2, local copies, waits for them, and re-layouts, shards(): chosen = jnp.take(normed, picks.reshape(-1), axis=0)  6.51 us
  transfers between devices with their start and end apart: 3, of which 3 were waited for; matrix products, arithmetic and copies ran while one was open for 3% of the time, Pallas kernels for 0%

commit v1 on v0

v1 whole, which is shorter than its diff:
```python
import jax
import jax.numpy as jnp
from jax import lax
from jax.sharding import PartitionSpec as P

adapter_scale = 2.0
norm_eps = 1e-05


def shards(
    residual_rows,
    input_norm_weight,
    trial_row_index,
    keyvalue_weight,
    adapter_down_weight,
    adapter_up_weight,
    keyvalue_gradient,
):
    trials = lax.axis_size("trial")
    tensors = lax.axis_size("tensor")
    dps = lax.axis_size("dp")
    tok_dev = trial_row_index.shape[1]
    select = tok_dev // (trials * tensors)
    normed_input = keyvalue_weight.shape[0]
    kv_width = keyvalue_weight.shape[1]
    keyvalue_half = kv_width // 2
    rank_index = adapter_up_weight.shape[1]
    pool_dev = residual_rows.shape[0]
    highest_precision = lax.Precision.HIGHEST

    source = lax.axis_index("trial") * tensors + lax.axis_index("tensor")
    picks = lax.dynamic_slice_in_dim(trial_row_index, source * select, select, 1).reshape(-1)
    onehot = (picks[:, None] == jnp.arange(pool_dev, dtype=jnp.int32)[None, :]).astype(jnp.bfloat16)
    wide = jnp.dot(onehot, residual_rows, preferred_element_type=jnp.float32)
    msq = jnp.mean(wide * wide, axis=1, keepdims=True)
    chosen = (wide * lax.rsqrt(msq + norm_eps) * input_norm_weight[None, :]).astype(jnp.bfloat16)
    chosen = chosen.reshape(trials, select, tensors, normed_input).transpose(0, 2, 1, 3)
    arrived = lax.all_to_all(
        chosen.reshape(trials * tensors, select, normed_input),
        ("trial", "tensor"),
        split_axis=0,
        concat_axis=0,
        tiled=True,
    )
    rows = arrived.reshape(tok_dev, normed_input)

    up_weight = adapter_up_weight[0].astype(jnp.float32)
    grad_in = keyvalue_gradient[0].astype(jnp.float32)
    key_gradient_full = jnp.dot(
        grad_in[:, :keyvalue_half], up_weight[:, :keyvalue_half].T, precision=highest_precision
    )
    value_gradient_full = jnp.dot(
        grad_in[:, keyvalue_half:], up_weight[:, keyvalue_half:].T, precision=highest_precision
    )
    rank_gradient = (
        adapter_scale * jnp.concatenate([key_gradient_full, value_gradient_full], axis=1)
    ).astype(jnp.bfloat16)
    every_rank = lax.all_gather(rank_gradient, "tensor", axis=0, tiled=True)
    grad_a_term = lax.dot_general(
        every_rank, rows, (((0,), (0,)), ((), ())), preferred_element_type=jnp.float32
    )

    down_weight = adapter_down_weight[0]
    keyval = jnp.dot(rows, keyvalue_weight, preferred_element_type=jnp.float32)
    ranks = jnp.dot(rows, down_weight, preferred_element_type=jnp.float32)
    summed = lax.psum_scatter(
        jnp.concatenate([keyval, ranks], axis=1), "tensor", scatter_dimension=0, tiled=True
    )
    frozen_output_local = summed[:, :kv_width]
    local_rank_rows = summed[:, kv_width:]
    adapter_key = jnp.dot(
        local_rank_rows[:, :rank_index], up_weight[:, :keyvalue_half], precision=highest_precision
    )
    adapter_value = jnp.dot(
        local_rank_rows[:, rank_index:], up_weight[:, keyvalue_half:], precision=highest_precision
    )
    keyvalue_output = frozen_output_local + adapter_scale * jnp.concatenate(
        [adapter_key, adapter_value], axis=1
    )

    grad_a = lax.psum_scatter(grad_a_term, "dp", scatter_dimension=0, tiled=True)

    key_down_gradient = jnp.dot(
        local_rank_rows[:, :rank_index].T, grad_in[:, :keyvalue_half], precision=highest_precision
    )
    value_down_gradient = jnp.dot(
        local_rank_rows[:, rank_index:].T, grad_in[:, keyvalue_half:], precision=highest_precision
    )
    up_gradient_term = adapter_scale * jnp.concatenate(
        [key_down_gradient, value_down_gradient], axis=1
    )
    width = up_gradient_term.shape[1] // (dps * tensors)
    up_gradient_term = (
        up_gradient_term.reshape(rank_index, dps, tensors, width)
        .transpose(0, 2, 1, 3)
        .reshape(rank_index, dps * tensors * width)
    )
    grad_b = lax.psum_scatter(up_gradient_term, "tensor", scatter_dimension=1, tiled=True)
    grad_b = lax.psum_scatter(grad_b, "dp", scatter_dimension=1, tiled=True)
    return (keyvalue_output[None], grad_a[None], grad_b[None])


def solution(mesh):
    return jax.shard_map(
        shards,
        mesh=mesh,
        in_specs=(
            P(("trial", "dp", "tensor"), None),
            P(),
            P(None, "dp"),
            P("tensor", None),
            P("trial", "tensor", None),
            P("trial", None, None),
            P("trial", ("dp", "tensor"), None),
        ),
        out_specs=(
            P("trial", ("dp", "tensor"), None),
            P("trial", "dp", "tensor"),
            P("trial", None, ("dp", "tensor")),
        ),
        check_vma=False,
    )
```

time: 286 us -> 230 us (0.80)
  waiting for transfers between devices: 188 us -> 129 us
  other arithmetic: 11.1 us -> 5.7 us
  local copies, waits for them, and re-layouts: 9.43 us -> 14.6 us
    unnamed x4 -> x5, waiting for transfers between devices: 101 us -> 26 us
    reduce_scatter x0 -> x1, waiting for transfers between devices: none -> 13.9 us  [shards(): lax.psum_scatter(up_gradient_term, 'tensor', scatter_dimension=1, tiled=T...]
    reshape x1 -> x3, local copies, waits for them, and re-layouts: 0.08 us -> 8.41 us  [the longest x2 7.26 us: shards(): chosen.reshape(trials, select, tensors, normed_input).transpose(0, 2, 1, 3)]
    gather x2 -> x0, local copies, waits for them, and re-layouts: 6.51 us -> none  [shards(): chosen = jnp.take(normed, picks.reshape(-1), axis=0)]
  transfers between devices with their start and end apart: 3 -> 4, of which waited for: 3 -> 4; matrix products, arithmetic and copies ran while one was open for 3% -> 5% of each run, Pallas kernels for 0% -> 0%
where the time goes in v1:
time: 230 us; the launch traced here: 225 us
  waiting for transfers between devices  129 us (56%)
  blocking collectives  43.3 us (19%)
  matrix products  18.9 us (8%)
  local copies, waits for them, and re-layouts  14.6 us (6%)
  between operations  13.9 us (6%)
  other arithmetic  5.7 us (2%)
    reduce_scatter x1, waiting for transfers between devices, shards(): lax.psum_scatter(jnp.concatenate([keyval, ranks], axis=1), 'tensor', scat...  49.4 us
    reduce_scatter x1, waiting for transfers between devices, shards(): lax.psum_scatter(grad_a_term, 'dp', scatter_dimension=0, tiled=True)  39.4 us
    all_to_all x1, blocking collectives, shards(): lax.all_to_all(chosen.reshape(trials * tensors, select, normed_input), ('...  37.6 us
    unnamed x5, waiting for transfers between devices  26 us
    reduce_scatter x1, waiting for transfers between devices, shards(): lax.psum_scatter(up_gradient_term, 'tensor', scatter_dimension=1, tiled=T...  13.9 us
    reshape x2, local copies, waits for them, and re-layouts, shards(): chosen.reshape(trials, select, tensors, normed_input).transpose(0, 2, 1, 3)  7.26 us
    dot_general x1, matrix products, shards(): keyval = jnp.dot(rows, keyvalue_weight, preferred_element_type=jnp.float32)  6.88 us
    all_gather x1, blocking collectives, shards(): every_rank = lax.all_gather(rank_gradient, 'tensor', axis=0, tiled=True)  5.69 us
  transfers between devices with their start and end apart: 4, of which 4 were waited for; matrix products, arithmetic and copies ran while one was open for 5% of the time, Pallas kernels for 0%

profile of v1, /device:TPU:1, one launch (start us, length us, event | category | flops | bytes accessed | tf_op | source)
XLA Modules:
  0.0 225.3 jit_solution(2438023686047598556)
XLA Ops:
  7.2 0.9 constant_dynamic-slice_fusion
  8.8 0.8 multiply_reduce_fusion
  9.6 1.8 multiply_convert_fusion
  11.5 4.5 %reshape.31 = bf16[8,16,4,2048]{3,2,1,0:T(4,128)(2,1)} reshape(bf16[128,8192]{1,0:T(8,128)(2,1)} %multiply_convert_fusion) | data formatting | bytes 4194304 | tf_op jit(solution)/shard_map/reshape | solution.py:37
  16.0 2.8 %copy.15 = bf16[8,16,4,2048]{3,1,2,0:T(8,128)(2,1)S(1)} copy(bf16[8,16,4,2048]{3,2,1,0:T(4,128)(2,1)} %reshape.31) | data formatting | bytes 4194304 | tf_op jit(solution)/shard_map/reshape | solution.py:37
  18.8 37.6 %all_to_all.5 = bf16[32,16,2048]{2,1,0:T(8,128)(2,1)S(1)} all-to-all(bf16[32,16,2048]{2,1,0:T(8,128)(2,1)S(1)} %bitcast.28), channel_id=1, replica_groups=mesh['trial'=8,'dp'=8,'tensor'=4] {'trial','tensor'}, dimensions={0} | all-to-all | bytes 4194304 | tf_op jit(solution)/shard_map/all_to_all | solution.py:38
  57.7 6.9 %fusion.25 = f32[512,2048]{1,0:T(8,128)S(1)} fusion(bf16[512,2048]{1,0:T(8,128)(2,1)S(1)} %bitcast.26, bf16[2048,2048]{1,0:T(8,128)(2,1)} %param.10), kind=kOutput, calls=%fused_computation.35 | convolution fusion | flops 4294967296 | bytes 14680064 | tf_op jit(solution)/shard_map/dot_general | solution.py:64
  64.6 2.4 %pad_maximum_fusion = f32[512,2176]{1,0:T(8,128)} fusion(f32[512,128]{1,0:T(8,128)S(1)} %fusion.2, f32[512,2048]{1,0:T(8,128)S(1)} %fusion.25), kind=kLoop, calls=%fused_computation | loop fusion | flops 1114112 | bytes 8912896 | tf_op jit(solution)/shard_map/concatenate | solution.py:67
  67.0 49.4 %reduce-scatter.7.cloned.1.call-done = f32[128,2176]{1,0:T(8,128)} async-done(((f32[512,2176]{1,0:T(8,128)}), f32[128,2176]{1,0:T(8,128)}) %reduce-scatter.7.cloned.1.call-update) | async-done | bytes 1114128 | tf_op jit(solution)/shard_map/reduce_scatter | solution.py:66
  116.5 1.2 fusion.8
  118.0 1.4 fusion.4
  120.1 1.2 reshape.34
  121.4 1.2 fusion.10
  122.5 1.2 fusion.6
  123.7 5.7 %all_gather.3 = bf16[512,128]{0,1:T(8,128)(2,1)S(1)} all-gather(bf16[128,128]{0,1:T(8,128)(2,1)S(1)} %fusion.18), channel_id=1, replica_groups=mesh['trial'=8,'dp'=8,'tensor'=4] {'tensor'}, dimensions={0}, use_global_device_ids=true | all-gather | bytes 163840 | tf_op jit(solution)/shard_map/all_gather | solution.py:58
  129.4 13.9 %reduce-scatter.11.cloned.1.call-done = f32[64,512]{1,0:T(8,128)} async-done(((f32[64,2048]{1,0:T(8,128)}), f32[64,512]{1,0:T(8,128)}) %reduce-scatter.11.cloned.1.call-update) | async-done | bytes 131088 | tf_op jit(solution)/shard_map/reduce_scatter | solution.py:98
  143.3 1.7 copy.19
  145.1 3.1 %fusion.26 = f32[128,2048]{1,0:T(8,128)} fusion(bf16[512,128]{0,1:T(8,128)(2,1)S(1)} %all_gather.3, bf16[512,2048]{1,0:T(8,128)(2,1)} %bitcast.27), kind=kOutput, calls=%fused_computation.36 | convolution fusion | flops 268435456 | bytes 3276800 | tf_op jit(solution)/shard_map/dot_general | solution.py:59
  148.2 1.3 fusion.13
  149.6 1.3 fusion.16
  150.8 1.1 fusion
  152.0 26.0 %reduce-scatter.13.cloned.1.call-done = f32[64,64]{1,0:T(8,128)} async-done(((f32[512,64]{1,0:T(8,128)}), f32[64,64]{1,0:T(8,128)}) %reduce-scatter.13.cloned.1.call-update) | async-done | bytes 16400
  177.9 1.5 copy.20
  179.4 39.4 %reduce-scatter.9.cloned.1.call-done = f32[16,2048]{1,0:T(8,128)} async-done(((f32[128,2048]{1,0:T(8,128)}), f32[16,2048]{1,0:T(8,128)}) %reduce-scatter.9.cloned.1.call-update) | async-done | bytes 131088 | tf_op jit(solution)/shard_map/reduce_scatter | solution.py:81
  (30 shorter events, 3.4 us)
Async XLA Ops:
  7.2 1.6 copy-start
  7.2 109.3 %reduce-scatter.7.cloned.1.call-start = ((), (), s32[]{:S(2)}) async-start(), calls=%async_computation.5 | async-start | bytes 5570560 | tf_op jit(solution)/shard_map/reduce_scatter | solution.py:66
  8.8 0.8 copy-start.6
  18.7 37.6 %copy-start.4 = (bf16[1,2048,128]{2,1,0:T(8,128)(2,1)S(1)}, bf16[1,2048,128]{2,1,0:T(8,128)(2,1)}, u32[]{:S(2)}) copy-start(bf16[1,2048,128]{2,1,0:T(8,128)(2,1)} %param.11) | copy-start | bytes 1572868
  56.4 1.3 copy-start.1
  67.0 49.5 %copy-start.3 = (bf16[1,128,2048]{2,1,0:T(8,128)(2,1)S(1)}, bf16[1,128,2048]{2,1,0:T(8,128)(2,1)}, u32[]{:S(2)}) copy-start(bf16[1,128,2048]{2,1,0:T(8,128)(2,1)} %param.13) | copy-start | bytes 1572868
  67.0 76.3 %reduce-scatter.11.cloned.1.call-start = ((), (), s32[]{:S(2)}) async-start(), calls=%async_computation.7 | async-start | bytes 655360 | tf_op jit(solution)/shard_map/reduce_scatter | solution.py:98
  120.1 1.3 copy-start.5
  121.3 56.6 %reduce-scatter.13.cloned.1.call-start = ((), (), s32[]{:S(2)}) async-start(), calls=%async_computation.8 | async-start | bytes 294912
  145.1 3.2 %copy-start.2 = (f32[128,2176]{1,0:T(8,128)S(1)}, f32[128,2176]{1,0:T(8,128)}, u32[]{:S(2)}) copy-start(f32[128,2176]{1,0:T(8,128)} %reduce-scatter.7.cloned.1.call-done) | copy-start | bytes 3342340
  145.1 73.8 %reduce-scatter.9.cloned.1.call-start = ((), (), s32[]{:S(2)}) async-start(), calls=%async_computation.6 | async-start | bytes 1179648 | tf_op jit(solution)/shard_map/reduce_scatter | solution.py:81
Sparse Core Ops, SparseCore 0:
  67.1 49.2 reduce-scatter.6
  121.4 21.8 reduce-scatter.10
  145.8 32.0 reduce-scatter.12
  181.0 37.7 reduce-scatter.8

commit v2 on v1

--- a/solution.py
+++ b/solution.py
@@ -1,10 +1,61 @@
+import functools
+
 import jax
 import jax.numpy as jnp
 from jax import lax
+from jax.experimental import pallas as pl
+from jax.experimental.pallas import tpu as pltpu
 from jax.sharding import PartitionSpec as P
+
+MESH = pl.DeviceIdType.MESH
 
 adapter_scale = 2.0
 norm_eps = 1e-05
+
+
+def _exchange_sum_kernel(n, group_index, device_of, x_ref, o_ref, recv, send_sems, recv_sems):
+    me = group_index()
+    barrier = pltpu.get_barrier_semaphore()
+    for shift in range(1, n):
+        pl.semaphore_signal(
+            barrier, inc=1, device_id=device_of(lax.rem(me + shift, n)), device_id_type=MESH
+        )
+    pl.semaphore_wait(barrier, n - 1)
+    copies = []
+    for shift in range(1, n):
+        target = lax.rem(me + shift, n)
+        copy = pltpu.make_async_remote_copy(
+            src_ref=x_ref.at[target],
+            dst_ref=recv.at[shift],
+            send_sem=send_sems.at[shift],
+            recv_sem=recv_sems.at[shift],
+            device_id=device_of(target),
+            device_id_type=MESH,
+        )
+        copy.start()
+        copies.append(copy)
+    o_ref[...] = x_ref[me]
+    for shift, copy in zip(range(1, n), copies):
+        copy.wait_recv()
+        o_ref[...] += recv[shift]
+    for copy in copies:
+        copy.wait_send()
+
+
+def exchange_sum(x, n, group_index, device_of, collective_id):
+    chunk = x.shape[1:]
+    return pl.pallas_call(
+        functools.partial(_exchange_sum_kernel, n, group_index, device_of),
+        out_shape=jax.ShapeDtypeStruct(chunk, x.dtype),
+        in_specs=[pl.BlockSpec(memory_space=pltpu.VMEM)],
+        out_specs=pl.BlockSpec(memory_space=pltpu.VMEM),
+        scratch_shapes=[
+            pltpu.VMEM((n,) + chunk, x.dtype),
+            pltpu.SemaphoreType.DMA((n,)),
+            pltpu.SemaphoreType.DMA((n,)),
+        ],
+        compiler_params=pltpu.CompilerParams(collective_id=collective_id, has_side_effects=True),
+    )(x)
 
 
 def shards(
@@ -78,7 +129,13 @@
         [adapter_key, adapter_value], axis=1
     )
 
-    grad_a = lax.psum_scatter(grad_a_term, "dp", scatter_dimension=0, tiled=True)
+    grad_a = exchange_sum(
+        grad_a_term.reshape(dps, grad_a_term.shape[0] // dps, grad_a_term.shape[1]),
+        dps,
+        lambda: lax.axis_index("dp"),
+        lambda j: (lax.axis_index("trial"), j, lax.axis_index("tensor")),
+        0,
+    )
 
     key_down_gradient = jnp.dot(
         local_rank_rows[:, :rank_index].T, grad_in[:, :keyvalue_half], precision=highest_precision
@@ -89,14 +146,15 @@
     up_gradient_term = adapter_scale * jnp.concatenate(
         [key_down_gradient, value_down_gradient], axis=1
     )
-    width = up_gradient_term.shape[1] // (dps * tensors)
-    up_gradient_term = (
-        up_gradient_term.reshape(rank_index, dps, tensors, width)
-        .transpose(0, 2, 1, 3)
-        .reshape(rank_index, dps * tensors * width)
+    members = dps * tensors
+    width = up_gradient_term.shape[1] // members
+    grad_b = exchange_sum(
+        up_gradient_term.reshape(rank_index, members, width).transpose(1, 0, 2),
+        members,
+        lambda: lax.axis_index("dp") * tensors + lax.axis_index("tensor"),
+        lambda g: (lax.axis_index("trial"), g // tensors, lax.rem(g, tensors)),
+        1,
     )
-    grad_b = lax.psum_scatter(up_gradient_term, "tensor", scatter_dimension=1, tiled=True)
-    grad_b = lax.psum_scatter(grad_b, "dp", scatter_dimension=1, tiled=True)
     return (keyvalue_output[None], grad_a[None], grad_b[None])
 
 

time: 230 us -> 165 us (0.72); the launches traced: 225 us -> 164 us
  waiting for transfers between devices: 129 us -> 5.74 us
  Pallas kernels: 0 us -> 65.1 us
    pallas_call x0 -> x2, Pallas kernels: none -> 65.1 us  [exchange_sum(): pl.pallas_call(functools.partial(_exchange_sum_kernel, n, group_index, de...]
    reduce_scatter x2 -> x0, waiting for transfers between devices: 53.3 us -> none  [the longest x1 39.4 us: shards(): lax.psum_scatter(grad_a_term, 'dp', scatter_dimension=0, tiled=True)]
    reduce_scatter x1, waiting for transfers between devices: 49.4 us -> 5.72 us  [shards(): lax.psum_scatter(jnp.concatenate([keyval, ranks], axis=1), 'tensor', scat...]
    unnamed x5 -> x1, waiting for transfers between devices: 26 us -> 0.02 us
  transfers between devices with their start and end apart: 4 -> 1, of which waited for: 4 -> 1; matrix products, arithmetic and copies ran while one was open for 5% -> 2% of each run, Pallas kernels for 0% -> 20%
where the time goes in v2:
time: 165 us; the launch traced here: 164 us
  Pallas kernels  65.1 us (39%)
  blocking collectives  43.6 us (26%)
  matrix products  16.9 us (10%)
  between operations  14.2 us (9%)
  local copies, waits for them, and re-layouts  12.4 us (8%)
  other arithmetic  6.46 us (4%)
  waiting for transfers between devices  5.74 us (3%)
    pallas_call x2, Pallas kernels, exchange_sum(): pl.pallas_call(functools.partial(_exchange_sum_kernel, n, group_index, de...  65.1 us
    all_to_all x1, blocking collectives, shards(): lax.all_to_all(chosen.reshape(trials * tensors, select, normed_input), ('...  37.6 us
    reshape x2, local copies, waits for them, and re-layouts, shards(): chosen.reshape(trials, select, tensors, normed_input).transpose(0, 2, 1, 3)  7.27 us
    dot_general x1, matrix products, shards(): keyval = jnp.dot(rows, keyvalue_weight, preferred_element_type=jnp.float32)  6.88 us
    all_gather x1, blocking collectives, shards(): every_rank = lax.all_gather(rank_gradient, 'tensor', axis=0, tiled=True)  6.02 us
    reduce_scatter x1, waiting for transfers between devices, shards(): lax.psum_scatter(jnp.concatenate([keyval, ranks], axis=1), 'tensor', scat...  5.72 us
    unnamed x22, local copies, waits for them, and re-layouts  3.56 us
  transfers between devices with their start and end apart: 1, of which 1 were waited for; matrix products, arithmetic and copies ran while one was open for 2% of the time, Pallas kernels for 20%

profile of v2, /device:TPU:1, one launch (start us, length us, event | category | flops | bytes accessed | tf_op | source)
XLA Modules:
  0.0 164.5 jit_solution(10426868055032276068)
XLA Ops:
  7.2 0.9 constant_dynamic-slice_fusion
  8.8 0.8 multiply_reduce_fusion
  9.6 1.8 %multiply_convert_fusion = bf16[128,8192]{1,0:T(8,128)(2,1)} fusion(f32[128,8192]{1,0:T(8,128)S(1)} %get-tuple-element.4, f32[8192]{0:T(1024)S(1)} %copy-done.9, f32[128]{0:T(128)S(1)} %add_rsqrt_fusion), kind=kLoop, calls=%fused_computation.1 | loop fusion | flops 3145728 | bytes 6324736 | tf_op jit(solution)/shard_map/convert_element_type | solution.py:87
  11.5 4.5 %reshape.30 = bf16[8,16,4,2048]{3,2,1,0:T(4,128)(2,1)} reshape(bf16[128,8192]{1,0:T(8,128)(2,1)} %multiply_convert_fusion) | data formatting | bytes 4194304 | tf_op jit(solution)/shard_map/reshape | solution.py:88
  16.0 2.8 %copy.11 = bf16[8,16,4,2048]{3,1,2,0:T(8,128)(2,1)S(1)} copy(bf16[8,16,4,2048]{3,2,1,0:T(4,128)(2,1)} %reshape.30) | data formatting | bytes 4194304 | tf_op jit(solution)/shard_map/reshape | solution.py:88
  18.8 37.6 %all_to_all.5 = bf16[32,16,2048]{2,1,0:T(8,128)(2,1)S(1)} all-to-all(bf16[32,16,2048]{2,1,0:T(8,128)(2,1)S(1)} %bitcast.29), channel_id=1, replica_groups=mesh['trial'=8,'dp'=8,'tensor'=4] {'trial','tensor'}, dimensions={0} | all-to-all | bytes 4194304 | tf_op jit(solution)/shard_map/all_to_all | solution.py:89
  56.4 0.7 fusion.2
  57.1 0.6 copy-done.1
  57.7 6.9 %fusion.25 = f32[512,2048]{1,0:T(8,128)S(1)} fusion(bf16[512,2048]{1,0:T(8,128)(2,1)S(1)} %bitcast.27, bf16[2048,2048]{1,0:T(8,128)(2,1)} %param.10), kind=kOutput, calls=%fused_computation.35 | convolution fusion | flops 4294967296 | bytes 14680064 | tf_op jit(solution)/shard_map/dot_general | solution.py:115
  64.6 2.4 %pad_maximum_fusion = f32[512,2176]{1,0:T(8,128)} fusion(f32[512,128]{1,0:T(8,128)S(1)} %fusion.2, f32[512,2048]{1,0:T(8,128)S(1)} %fusion.25), kind=kLoop, calls=%fused_computation | loop fusion | flops 1114112 | bytes 8912896 | tf_op jit(solution)/shard_map/concatenate | solution.py:118
  67.0 1.0 copy-done.4
  68.5 6.0 %all_gather.3 = bf16[512,128]{0,1:T(8,128)(2,1)S(1)} all-gather(bf16[128,128]{0,1:T(8,128)(2,1)S(1)} %fusion.18), channel_id=1, replica_groups=mesh['trial'=8,'dp'=8,'tensor'=4] {'tensor'}, dimensions={0}, use_global_device_ids=true | all-gather | bytes 163840 | tf_op jit(solution)/shard_map/all_gather | solution.py:109
  74.5 3.0 %fusion.26.x_ref = f32[8,16,2048]{2,1,0:T(8,128)} fusion(bf16[8,16,512]{2,1,0:T(8,128)(2,1)S(1)} %bitcast.30, bf16[512,2048,1]{1,0,2:T(8,128)(2,1)} %bitcast.28), kind=kOutput, calls=%fused_computation.36 | convolution fusion | flops 268435456 | bytes 3276800 | tf_op jit(solution)/shard_map/dot_general | solution.py:110
  77.6 33.2 %shard_map.94 = f32[16,2048]{1,0:T(8,128)} custom-call(f32[8,16,2048]{2,1,0:T(8,128)} %fusion.26.x_ref), custom_call_target="tpu_custom_call" | custom-call | tf_op jit(solution)/shard_map/pallas_call | solution.py:47
  110.7 5.7 %reduce-scatter.2.cloned.1.call-done = f32[128,2176]{1,0:T(8,128)} async-done(((f32[512,2176]{1,0:T(8,128)}), f32[128,2176]{1,0:T(8,128)}) %reduce-scatter.2.cloned.1.call-update) | async-done | bytes 1114128 | tf_op jit(solution)/shard_map/reduce_scatter | solution.py:117
  116.5 1.2 fusion.8
  117.9 1.4 fusion.4
  119.7 1.1 fusion.1.x_ref
  120.8 31.9 %shard_map.95 = f32[64,64]{1,0:T(8,128)} custom-call(f32[32,64,64]{2,1,0:T(8,128)} %fusion.1.x_ref), custom_call_target="tpu_custom_call" | custom-call | tf_op jit(solution)/shard_map/pallas_call | solution.py:47
  152.7 1.3 fusion.13
  154.0 1.2 fusion.16
  155.2 1.1 fusion
  156.3 0.7 copy.18
  157.0 0.6 copy.19
  (29 shorter events, 1.8 us)
Async XLA Ops:
  7.2 1.6 copy-start
  7.2 109.3 %reduce-scatter.2.cloned.1.call-start = ((), (), s32[]{:S(2)}) async-start(), calls=%async_computation.2 | async-start | bytes 5570560 | tf_op jit(solution)/shard_map/reduce_scatter | solution.py:117
  8.8 0.8 copy-start.9
  18.8 37.6 %copy-start.5 = (bf16[1,2048,128]{2,1,0:T(8,128)(2,1)S(1)}, bf16[1,2048,128]{2,1,0:T(8,128)(2,1)}, u32[]{:S(2)}) copy-start(bf16[1,2048,128]{2,1,0:T(8,128)(2,1)} %param.11) | copy-start | bytes 1572868
  56.4 1.3 copy-start.1
  67.0 1.0 copy-start.4
  67.0 1.1 copy-start.6
  119.5 33.2 %copy-start.7 = (bf16[1,64,2048]{2,1,0:T(8,128)(2,1)S(1)}, bf16[1,64,2048]{2,1,0:T(8,128)(2,1)}, u32[]{:S(2)}) copy-start(bf16[1,64,2048]{2,1,0:T(8,128)(2,1)} %param.12) | copy-start | bytes 786436
  120.8 34.4 %copy-start.2 = (f32[128,2176]{1,0:T(8,128)S(1)}, f32[128,2176]{1,0:T(8,128)}, u32[]{:S(2)}) copy-start(f32[128,2176]{1,0:T(8,128)} %reduce-scatter.2.cloned.1.call-done) | copy-start | bytes 3342340
  153.9 2.4 %copy-start.3 = (f32[16,2048]{1,0:T(8,128)S(1)}, f32[16,2048]{1,0:T(8,128)}, u32[]{:S(2)}) copy-start(f32[16,2048]{1,0:T(8,128)} %shard_map.94) | copy-start | bytes 393220
  153.9 3.0 %copy-start.8 = (f32[64,64]{1,0:T(8,128)S(1)}, f32[64,64]{1,0:T(8,128)}, u32[]{:S(2)}) copy-start(f32[64,64]{1,0:T(8,128)} %shard_map.95) | copy-start | bytes 49156
Sparse Core Ops, SparseCore 0:
  67.1 49.2 reduce-scatter.1

commit v3 on v2

--- a/solution.py
+++ b/solution.py
@@ -53,6 +53,74 @@
             pltpu.VMEM((n,) + chunk, x.dtype),
             pltpu.SemaphoreType.DMA((n,)),
             pltpu.SemaphoreType.DMA((n,)),
+        ],
+        compiler_params=pltpu.CompilerParams(collective_id=collective_id, has_side_effects=True),
+    )(x)
+
+
+def _two_stage_sum_kernel(n1, n2, x_ref, o_ref, stage, recv1, recv2, sems):
+    me1 = lax.axis_index("tensor")
+    me2 = lax.axis_index("dp")
+    trial = lax.axis_index("trial")
+    first = lambda j: (trial, me2, j)
+    second = lambda j: (trial, j, me1)
+    barrier = pltpu.get_barrier_semaphore()
+    for shift in range(1, n1):
+        pl.semaphore_signal(barrier, inc=1, device_id=first(lax.rem(me1 + shift, n1)), device_id_type=MESH)
+    for shift in range(1, n2):
+        pl.semaphore_signal(barrier, inc=1, device_id=second(lax.rem(me2 + shift, n2)), device_id_type=MESH)
+    pl.semaphore_wait(barrier, n1 + n2 - 2)
+    copies = []
+    for shift in range(1, n1):
+        target = lax.rem(me1 + shift, n1)
+        copy = pltpu.make_async_remote_copy(
+            src_ref=x_ref.at[target],
+            dst_ref=recv1.at[shift],
+            send_sem=sems.at[0, shift],
+            recv_sem=sems.at[1, shift],
+            device_id=first(target),
+            device_id_type=MESH,
+        )
+        copy.start()
+        copies.append(copy)
+    stage[...] = x_ref[me1]
+    for shift, copy in zip(range(1, n1), copies):
+        copy.wait_recv()
+        stage[...] += recv1[shift]
+    copies2 = []
+    for shift in range(1, n2):
+        target = lax.rem(me2 + shift, n2)
+        copy = pltpu.make_async_remote_copy(
+            src_ref=stage.at[target],
+            dst_ref=recv2.at[shift],
+            send_sem=sems.at[2, shift],
+            recv_sem=sems.at[3, shift],
+            device_id=second(target),
+            device_id_type=MESH,
+        )
+        copy.start()
+        copies2.append(copy)
+    o_ref[...] = stage[me2]
+    for shift, copy in zip(range(1, n2), copies2):
+        copy.wait_recv()
+        o_ref[...] += recv2[shift]
+    for copy in copies + copies2:
+        copy.wait_send()
+
+
+def two_stage_sum(x, collective_id):
+    n1, n2 = x.shape[0], x.shape[1]
+    chunk = x.shape[2:]
+    return pl.pallas_call(
+        functools.partial(_two_stage_sum_kernel, n1, n2),
+        out_shape=jax.ShapeDtypeStruct(chunk, x.dtype),
+        in_specs=[pl.BlockSpec(memory_space=pltpu.VMEM)],
+        out_specs=pl.BlockSpec(memory_space=pltpu.VMEM),
+        scratch_shapes=[
+            pltpu.VMEM((n2,) + chunk, x.dtype),
+            pltpu.VMEM((n1, n2) + chunk, x.dtype),
+            pltpu.VMEM((n2,) + chunk, x.dtype),
+            pltpu.SemaphoreType.DMA((4, max(n1, n2))),
         ],
         compiler_params=pltpu.CompilerParams(collective_id=collective_id, has_side_effects=True),
     )(x)
@@ -146,14 +214,9 @@
     up_gradient_term = adapter_scale * jnp.concatenate(
         [key_down_gradient, value_down_gradient], axis=1
     )
-    members = dps * tensors
-    width = up_gradient_term.shape[1] // members
-    grad_b = exchange_sum(
-        up_gradient_term.reshape(rank_index, members, width).transpose(1, 0, 2),
-        members,
-        lambda: lax.axis_index("dp") * tensors + lax.axis_index("tensor"),
-        lambda g: (lax.axis_index("trial"), g // tensors, lax.rem(g, tensors)),
-        1,
+    width = up_gradient_term.shape[1] // (dps * tensors)
+    grad_b = two_stage_sum(
+        up_gradient_term.reshape(rank_index, dps, tensors, width).transpose(2, 1, 0, 3), 1
     )
     return (keyvalue_output[None], grad_a[None], grad_b[None])
 

time: 165 us -> 158 us (0.958)
  Pallas kernels: 65.1 us -> 57.8 us
    pallas_call x2 -> x1, Pallas kernels: 65.1 us -> 33.2 us  [exchange_sum(): pl.pallas_call(functools.partial(_exchange_sum_kernel, n, group_index, de...]
    pallas_call x0 -> x1, Pallas kernels: none -> 24.6 us  [two_stage_sum(): pl.pallas_call(functools.partial(_two_stage_sum_kernel, n1, n2), out_shap...]
  transfers between devices with their start and end apart: 1 -> 1, of which waited for: 1 -> 1; matrix products, arithmetic and copies ran while one was open for 2% -> 2% of each run, Pallas kernels for 20% -> 21%
where the time goes in v3:
time: 158 us
  Pallas kernels  57.8 us (37%)
  blocking collectives  43.6 us (28%)
  matrix products  16.9 us (11%)
  between operations  14.2 us (9%)
  local copies, waits for them, and re-layouts  12.8 us (8%)
  other arithmetic  6.46 us (4%)
  waiting for transfers between devices  5.74 us (4%)
    all_to_all x1, blocking collectives, shards(): lax.all_to_all(chosen.reshape(trials * tensors, select, normed_input), ('...  37.6 us
    pallas_call x1, Pallas kernels, exchange_sum(): pl.pallas_call(functools.partial(_exchange_sum_kernel, n, group_index, de...  33.2 us
    pallas_call x1, Pallas kernels, two_stage_sum(): pl.pallas_call(functools.partial(_two_stage_sum_kernel, n1, n2), out_shap...  24.6 us
    reshape x2, local copies, waits for them, and re-layouts, shards(): chosen.reshape(trials, select, tensors, normed_input).transpose(0, 2, 1, 3)  7.27 us
    dot_general x1, matrix products, shards(): keyval = jnp.dot(rows, keyvalue_weight, preferred_element_type=jnp.float32)  6.88 us
    all_gather x1, blocking collectives, shards(): every_rank = lax.all_gather(rank_gradient, 'tensor', axis=0, tiled=True)  6.02 us
    reduce_scatter x1, waiting for transfers between devices, shards(): lax.psum_scatter(jnp.concatenate([keyval, ranks], axis=1), 'tensor', scat...  5.72 us
    unnamed x22, local copies, waits for them, and re-layouts  3.56 us
  transfers between devices with their start and end apart: 1, of which 1 were waited for; matrix products, arithmetic and copies ran while one was open for 2% of the time, Pallas kernels for 21%

profile of v3, /device:TPU:1, one launch (start us, length us, event | category | flops | bytes accessed | tf_op | source)
XLA Modules:
  0.0 157.6 jit_solution(16244620134017010820)
XLA Ops:
  7.2 0.9 constant_dynamic-slice_fusion
  8.8 0.8 multiply_reduce_fusion
  9.6 1.8 %multiply_convert_fusion = bf16[128,8192]{1,0:T(8,128)(2,1)} fusion(f32[128,8192]{1,0:T(8,128)S(1)} %get-tuple-element.4, f32[8192]{0:T(1024)S(1)} %copy-done.9, f32[128]{0:T(128)S(1)} %add_rsqrt_fusion), kind=kLoop, calls=%fused_computation.1 | loop fusion | flops 3145728 | bytes 6324736 | tf_op jit(solution)/shard_map/convert_element_type | solution.py:155
  11.5 4.5 %reshape.30 = bf16[8,16,4,2048]{3,2,1,0:T(4,128)(2,1)} reshape(bf16[128,8192]{1,0:T(8,128)(2,1)} %multiply_convert_fusion) | data formatting | bytes 4194304 | tf_op jit(solution)/shard_map/reshape | solution.py:156
  16.0 2.8 %copy.11 = bf16[8,16,4,2048]{3,1,2,0:T(8,128)(2,1)S(1)} copy(bf16[8,16,4,2048]{3,2,1,0:T(4,128)(2,1)} %reshape.30) | data formatting | bytes 4194304 | tf_op jit(solution)/shard_map/reshape | solution.py:156
  18.8 37.6 %all_to_all.5 = bf16[32,16,2048]{2,1,0:T(8,128)(2,1)S(1)} all-to-all(bf16[32,16,2048]{2,1,0:T(8,128)(2,1)S(1)} %bitcast.29), channel_id=1, replica_groups=mesh['trial'=8,'dp'=8,'tensor'=4] {'trial','tensor'}, dimensions={0} | all-to-all | bytes 4194304 | tf_op jit(solution)/shard_map/all_to_all | solution.py:157
  56.4 0.7 fusion.2
  57.1 0.6 copy-done.1
  57.7 6.9 %fusion.25 = f32[512,2048]{1,0:T(8,128)S(1)} fusion(bf16[512,2048]{1,0:T(8,128)(2,1)S(1)} %bitcast.27, bf16[2048,2048]{1,0:T(8,128)(2,1)} %param.10), kind=kOutput, calls=%fused_computation.35 | convolution fusion | flops 4294967296 | bytes 14680064 | tf_op jit(solution)/shard_map/dot_general | solution.py:183
  64.6 2.4 %pad_maximum_fusion = f32[512,2176]{1,0:T(8,128)} fusion(f32[512,128]{1,0:T(8,128)S(1)} %fusion.2, f32[512,2048]{1,0:T(8,128)S(1)} %fusion.25), kind=kLoop, calls=%fused_computation | loop fusion | flops 1114112 | bytes 8912896 | tf_op jit(solution)/shard_map/concatenate | solution.py:186
  67.0 1.0 copy-done.4
  68.5 6.0 %all_gather.3 = bf16[512,128]{0,1:T(8,128)(2,1)S(1)} all-gather(bf16[128,128]{0,1:T(8,128)(2,1)S(1)} %fusion.18), channel_id=1, replica_groups=mesh['trial'=8,'dp'=8,'tensor'=4] {'tensor'}, dimensions={0}, use_global_device_ids=true | all-gather | bytes 163840 | tf_op jit(solution)/shard_map/all_gather | solution.py:177
  74.5 3.0 %fusion.26.x_ref = f32[8,16,2048]{2,1,0:T(8,128)} fusion(bf16[8,16,512]{2,1,0:T(8,128)(2,1)S(1)} %bitcast.30, bf16[512,2048,1]{1,0,2:T(8,128)(2,1)} %bitcast.28), kind=kOutput, calls=%fused_computation.36 | convolution fusion | flops 268435456 | bytes 3276800 | tf_op jit(solution)/shard_map/dot_general | solution.py:178
  77.6 33.2 %shard_map.94 = f32[16,2048]{1,0:T(8,128)} custom-call(f32[8,16,2048]{2,1,0:T(8,128)} %fusion.26.x_ref), custom_call_target="tpu_custom_call" | custom-call | tf_op jit(solution)/shard_map/pallas_call | solution.py:47
  110.7 5.7 %reduce-scatter.2.cloned.1.call-done = f32[128,2176]{1,0:T(8,128)} async-done(((f32[512,2176]{1,0:T(8,128)}), f32[128,2176]{1,0:T(8,128)}) %reduce-scatter.2.cloned.1.call-update) | async-done | bytes 1114128 | tf_op jit(solution)/shard_map/reduce_scatter | solution.py:185
  116.5 1.2 fusion.8
  118.2 1.4 fusion.4
  120.1 1.1 fusion.1.x_ref
  121.2 24.6 %shard_map.95 = f32[64,64]{1,0:T(8,128)} custom-call(f32[4,8,64,64]{3,2,1,0:T(8,128)} %fusion.1.x_ref), custom_call_target="tpu_custom_call" | custom-call | tf_op jit(solution)/shard_map/pallas_call | solution.py:114
  145.8 1.3 fusion.13
  147.1 1.2 fusion.16
  148.3 1.1 fusion
  149.5 0.7 copy.18
  150.1 0.6 copy.19
  (29 shorter events, 2.3 us)
Async XLA Ops:
  7.2 1.6 %copy-start = (bf16[128,8192]{1,0:T(8,128)(2,1)S(1)}, bf16[128,8192]{1,0:T(8,128)(2,1)}, u32[]{:S(2)}) copy-start(bf16[128,8192]{1,0:T(8,128)(2,1)} %param.7) | copy-start | bytes 6291460
  7.2 109.3 %reduce-scatter.2.cloned.1.call-start = ((), (), s32[]{:S(2)}) async-start(), calls=%async_computation.2 | async-start | bytes 5570560 | tf_op jit(solution)/shard_map/reduce_scatter | solution.py:185
  8.8 0.8 copy-start.9
  18.8 37.6 %copy-start.5 = (bf16[1,2048,128]{2,1,0:T(8,128)(2,1)S(1)}, bf16[1,2048,128]{2,1,0:T(8,128)(2,1)}, u32[]{:S(2)}) copy-start(bf16[1,2048,128]{2,1,0:T(8,128)(2,1)} %param.11) | copy-start | bytes 1572868
  56.4 1.3 copy-start.1
  67.0 1.0 copy-start.4
  67.0 1.1 copy-start.6
  119.9 25.9 %copy-start.7 = (bf16[1,64,2048]{2,1,0:T(8,128)(2,1)S(1)}, bf16[1,64,2048]{2,1,0:T(8,128)(2,1)}, u32[]{:S(2)}) copy-start(bf16[1,64,2048]{2,1,0:T(8,128)(2,1)} %param.12) | copy-start | bytes 786436
  121.2 27.2 %copy-start.2 = (f32[128,2176]{1,0:T(8,128)S(1)}, f32[128,2176]{1,0:T(8,128)}, u32[]{:S(2)}) copy-start(f32[128,2176]{1,0:T(8,128)} %reduce-scatter.2.cloned.1.call-done) | copy-start | bytes 3342340
  147.1 2.4 %copy-start.3 = (f32[16,2048]{1,0:T(8,128)S(1)}, f32[16,2048]{1,0:T(8,128)}, u32[]{:S(2)}) copy-start(f32[16,2048]{1,0:T(8,128)} %shard_map.94) | copy-start | bytes 393220
  147.1 3.0 %copy-start.8 = (f32[64,64]{1,0:T(8,128)S(1)}, f32[64,64]{1,0:T(8,128)}, u32[]{:S(2)}) copy-start(f32[64,64]{1,0:T(8,128)} %shard_map.95) | copy-start | bytes 49156
Sparse Core Ops, SparseCore 0:
  67.1 49.2 reduce-scatter.1

commit v4 on v3

--- a/solution.py
+++ b/solution.py
@@ -121,6 +121,62 @@
             pltpu.VMEM((n1, n2) + chunk, x.dtype),
             pltpu.VMEM((n2,) + chunk, x.dtype),
             pltpu.SemaphoreType.DMA((4, max(n1, n2))),
+        ],
+        compiler_params=pltpu.CompilerParams(collective_id=collective_id, has_side_effects=True),
+    )(x)
+
+
+def _scatter_rows_kernel(trials, tensors, select, x_ref, o_ref, landed, send_sems, recv_sems):
+    n = trials * tensors
+    width = o_ref.shape[1]
+    me = lax.axis_index("trial") * tensors + lax.axis_index("tensor")
+    dp = lax.axis_index("dp")
+    member = lambda g: (g // tensors, dp, lax.rem(g, tensors))
+    barrier = pltpu.get_barrier_semaphore()
+    for shift in range(1, n):
+        pl.semaphore_signal(barrier, inc=1, device_id=member(lax.rem(me + shift, n)), device_id_type=MESH)
+    pl.semaphore_wait(barrier, n - 1)
+    copies = []
+    for shift in range(1, n):
+        target = lax.rem(me + shift, n)
+        copy = pltpu.make_async_remote_copy(
+            src_ref=x_ref.at[
+                pl.ds(pl.multiple_of((target // tensors) * select, select), select),
+                pl.ds(pl.multiple_of(lax.rem(target, tensors) * width, width), width),
+            ],
+            dst_ref=landed.at[pl.ds(pl.multiple_of(me * select, select), select)],
+            send_sem=send_sems.at[shift],
+            recv_sem=recv_sems.at[shift],
+            device_id=member(target),
+            device_id_type=MESH,
+        )
+        copy.start()
+        copies.append(copy)
+    own = pl.ds(pl.multiple_of(me * select, select), select)
+    o_ref[own, :] = x_ref[
+        pl.ds(pl.multiple_of(lax.axis_index("trial") * select, select), select),
+        pl.ds(pl.multiple_of(lax.axis_index("tensor") * width, width), width),
+    ]
+    for shift, copy in zip(range(1, n), copies):
+        copy.wait_recv()
+        source = pl.ds(pl.multiple_of(lax.rem(me + n - shift, n) * select, select), select)
+        o_ref[source, :] = landed[source, :]
+    for copy in copies:
+        copy.wait_send()
+
+
+def scatter_rows(x, trials, tensors, select, collective_id):
+    width = x.shape[1] // tensors
+    rows = trials * tensors * select
+    return pl.pallas_call(
+        functools.partial(_scatter_rows_kernel, trials, tensors, select),
+        out_shape=jax.ShapeDtypeStruct((rows, width), x.dtype),
+        in_specs=[pl.BlockSpec(memory_space=pltpu.VMEM)],
+        out_specs=pl.BlockSpec(memory_space=pltpu.VMEM),
+        scratch_shapes=[
+            pltpu.VMEM((rows, width), x.dtype),
+            pltpu.SemaphoreType.DMA((trials * tensors,)),
+            pltpu.SemaphoreType.DMA((trials * tensors,)),
         ],
         compiler_params=pltpu.CompilerParams(collective_id=collective_id, has_side_effects=True),
     )(x)
@@ -153,15 +209,7 @@
     wide = jnp.dot(onehot, residual_rows, preferred_element_type=jnp.float32)
     msq = jnp.mean(wide * wide, axis=1, keepdims=True)
     chosen = (wide * lax.rsqrt(msq + norm_eps) * input_norm_weight[None, :]).astype(jnp.bfloat16)
-    chosen = chosen.reshape(trials, select, tensors, normed_input).transpose(0, 2, 1, 3)
-    arrived = lax.all_to_all(
-        chosen.reshape(trials * tensors, select, normed_input),
-        ("trial", "tensor"),
-        split_axis=0,
-        concat_axis=0,
-        tiled=True,
-    )
-    rows = arrived.reshape(tok_dev, normed_input)
+    rows = scatter_rows(chosen, trials, tensors, select, 2)
 
     up_weight = adapter_up_weight[0].astype(jnp.float32)
     grad_in = keyvalue_gradient[0].astype(jnp.float32)

time: 158 us -> 161 us (1.019)
  Pallas kernels: 57.8 us -> 101 us
  blocking collectives: 43.6 us -> 9.35 us
  local copies, waits for them, and re-layouts: 12.8 us -> 4.96 us
  matrix products: 16.9 us -> 18.6 us
    pallas_call x0 -> x1, Pallas kernels: none -> 43.7 us  [scatter_rows(): pl.pallas_call(functools.partial(_scatter_rows_kernel, trials, tensors, s...]
    all_to_all x1 -> x0, blocking collectives: 37.6 us -> none  [shards(): lax.all_to_all(chosen.reshape(trials * tensors, select, normed_input), ('...]
    reshape x2 -> x0, local copies, waits for them, and re-layouts: 7.27 us -> none  [shards(): chosen.reshape(trials, select, tensors, normed_input).transpose(0, 2, 1, 3)]
    all_gather x1, blocking collectives: 6.02 us -> 9.35 us  [shards(): every_rank = lax.all_gather(rank_gradient, 'tensor', axis=0, tiled=True)]
    dot_general x1, matrix products: 0.71 us -> 2.44 us  [shards(): ranks = jnp.dot(rows, down_weight, preferred_element_type=jnp.float32)]
where the time goes in v4:
time: 161 us
  Pallas kernels  101 us (63%)
  matrix products  18.6 us (12%)
  between operations  14.2 us (9%)
  blocking collectives  9.35 us (6%)
  other arithmetic  6.54 us (4%)
  waiting for transfers between devices  5.76 us (4%)
  local copies, waits for them, and re-layouts  4.96 us (3%)
    pallas_call x1, Pallas kernels, scatter_rows(): pl.pallas_call(functools.partial(_scatter_rows_kernel, trials, tensors, s...  43.7 us
    pallas_call x1, Pallas kernels, exchange_sum(): pl.pallas_call(functools.partial(_exchange_sum_kernel, n, group_index, de...  33.2 us
    pallas_call x1, Pallas kernels, two_stage_sum(): pl.pallas_call(functools.partial(_two_stage_sum_kernel, n1, n2), out_shap...  24.6 us
    all_gather x1, blocking collectives, shards(): every_rank = lax.all_gather(rank_gradient, 'tensor', axis=0, tiled=True)  9.35 us
    dot_general x1, matrix products, shards(): keyval = jnp.dot(rows, keyvalue_weight, preferred_element_type=jnp.float32)  6.89 us
    reduce_scatter x1, waiting for transfers between devices, shards(): lax.psum_scatter(jnp.concatenate([keyval, ranks], axis=1), 'tensor', scat...  5.74 us
  transfers between devices with their start and end apart: 1, of which 1 were waited for; matrix products, arithmetic and copies ran while one was open for 2% of the time, Pallas kernels for 21%

profile of v4, /device:TPU:1, one launch (start us, length us, event | category | flops | bytes accessed | tf_op | source)
XLA Modules:
  0.0 161.0 jit_solution(3666569485990764440)
XLA Ops:
  7.2 0.9 constant_dynamic-slice_fusion
  8.2 0.6 copy-done
  8.8 0.8 multiply_reduce_fusion
  9.6 1.8 %multiply_convert_fusion.x_ref = bf16[128,8192]{1,0:T(8,128)(2,1)} fusion(f32[128,8192]{1,0:T(8,128)S(1)} %get-tuple-element.4, f32[8192]{0:T(1024)S(1)} %copy-done.9, f32[128]{0:T(128)S(1)} %add_rsqrt_fusion), kind=kLoop, calls=%fused_computation.1 | loop fusion | flops 3145728 | bytes 6324736 | tf_op jit(solution)/shard_map/convert_element_type | solution.py:211
  11.5 43.7 %shard_map.94 = bf16[512,2048]{1,0:T(8,128)(2,1)} custom-call(bf16[128,8192]{1,0:T(8,128)(2,1)} %multiply_convert_fusion.x_ref), custom_call_target="tpu_custom_call" | custom-call | tf_op jit(solution)/shard_map/pallas_call | solution.py:171
  55.2 2.4 %fusion.2 = f32[512,128]{1,0:T(8,128)S(1)} fusion(bf16[512,2048]{1,0:T(8,128)(2,1)} %shard_map.94, bf16[1,2048,128]{2,1,0:T(8,128)(2,1)S(1)} %copy-done.5), kind=kOutput, calls=%fused_computation.8 | convolution fusion | flops 268435456 | bytes 2883584 | tf_op jit(solution)/shard_map/dot_general | solution.py:232
  57.6 6.9 %fusion.25 = f32[512,2048]{1,0:T(8,128)S(1)} fusion(bf16[512,2048]{1,0:T(8,128)(2,1)S(1)} %copy-done.1, bf16[2048,2048]{1,0:T(8,128)(2,1)} %param.10), kind=kOutput, calls=%fused_computation.35 | convolution fusion | flops 4294967296 | bytes 14680064 | tf_op jit(solution)/shard_map/dot_general | solution.py:231
  64.5 2.4 %pad_maximum_fusion = f32[512,2176]{1,0:T(8,128)} fusion(f32[512,128]{1,0:T(8,128)S(1)} %fusion.2, f32[512,2048]{1,0:T(8,128)S(1)} %fusion.25), kind=kLoop, calls=%fused_computation | loop fusion | flops 1114112 | bytes 8912896 | tf_op jit(solution)/shard_map/concatenate | solution.py:234
  66.9 1.0 copy-done.4
  68.6 9.3 %all_gather.3 = bf16[512,128]{1,0:T(8,128)(2,1)S(1)} all-gather(bf16[128,128]{1,0:T(8,128)(2,1)S(1)} %fusion.18), channel_id=1, replica_groups=mesh['trial'=8,'dp'=8,'tensor'=4] {'tensor'}, dimensions={0}, use_global_device_ids=true | all-gather | bytes 163840 | tf_op jit(solution)/shard_map/all_gather | solution.py:225
  77.9 3.0 %fusion.26 = f32[128,2048]{1,0:T(8,128)} fusion(bf16[512,128]{1,0:T(8,128)(2,1)S(1)} %all_gather.3, bf16[512,2048]{1,0:T(8,128)(2,1)} %shard_map.94), kind=kOutput, calls=%fused_computation.36 | convolution fusion | flops 268435456 | bytes 3276800 | tf_op jit(solution)/shard_map/dot_general | solution.py:226
  80.9 33.2 %shard_map.95 = f32[16,2048]{1,0:T(8,128)} custom-call(f32[8,16,2048]{2,1,0:T(8,128)} %bitcast.18), custom_call_target="tpu_custom_call" | custom-call | tf_op jit(solution)/shard_map/pallas_call | solution.py:47
  114.1 5.7 %reduce-scatter.2.cloned.1.call-done = f32[128,2176]{1,0:T(8,128)} async-done(((f32[512,2176]{1,0:T(8,128)}), f32[128,2176]{1,0:T(8,128)}) %reduce-scatter.2.cloned.1.call-update) | async-done | bytes 1114128 | tf_op jit(solution)/shard_map/reduce_scatter | solution.py:233
  119.9 1.2 fusion.8
  121.0 0.3 concatenate.20
  121.6 1.4 fusion.4
  122.9 0.3 concatenate.21
  123.5 1.1 fusion.1.x_ref
  124.6 24.6 %shard_map.96 = f32[64,64]{1,0:T(8,128)} custom-call(f32[4,8,64,64]{3,2,1,0:T(8,128)} %fusion.1.x_ref), custom_call_target="tpu_custom_call" | custom-call | tf_op jit(solution)/shard_map/pallas_call | solution.py:114
  149.2 1.3 fusion.13
  150.5 1.2 fusion.16
  151.7 1.1 fusion
  152.9 0.7 copy.17
  153.5 0.6 copy.18
  (27 shorter events, 1.1 us)
Async XLA Ops:
  7.2 1.6 %copy-start = (bf16[128,8192]{1,0:T(8,128)(2,1)S(1)}, bf16[128,8192]{1,0:T(8,128)(2,1)}, u32[]{:S(2)}) copy-start(bf16[128,8192]{1,0:T(8,128)(2,1)} %param.7) | copy-start | bytes 6291460
  7.2 112.7 %reduce-scatter.2.cloned.1.call-start = ((), (), s32[]{:S(2)}) async-start(), calls=%async_computation.1 | async-start | bytes 5570560 | tf_op jit(solution)/shard_map/reduce_scatter | solution.py:233
  8.8 0.8 copy-start.9
  11.5 43.7 %copy-start.5 = (bf16[1,2048,128]{2,1,0:T(8,128)(2,1)S(1)}, bf16[1,2048,128]{2,1,0:T(8,128)(2,1)}, u32[]{:S(2)}) copy-start(bf16[1,2048,128]{2,1,0:T(8,128)(2,1)} %param.11) | copy-start | bytes 1572868
  55.2 2.5 %copy-start.1 = (bf16[512,2048]{1,0:T(8,128)(2,1)S(1)}, bf16[512,2048]{1,0:T(8,128)(2,1)}, u32[]{:S(2)}) copy-start(bf16[512,2048]{1,0:T(8,128)(2,1)} %shard_map.94) | copy-start | bytes 6291460
  66.9 1.0 copy-start.4
  66.9 1.1 copy-start.6
  123.3 25.9 %copy-start.7 = (bf16[1,64,2048]{2,1,0:T(8,128)(2,1)S(1)}, bf16[1,64,2048]{2,1,0:T(8,128)(2,1)}, u32[]{:S(2)}) copy-start(bf16[1,64,2048]{2,1,0:T(8,128)(2,1)} %param.12) | copy-start | bytes 786436
  124.6 27.1 %copy-start.2 = (f32[128,2176]{1,0:T(8,128)S(1)}, f32[128,2176]{1,0:T(8,128)}, u32[]{:S(2)}) copy-start(f32[128,2176]{1,0:T(8,128)} %reduce-scatter.2.cloned.1.call-done) | copy-start | bytes 3342340
  150.5 2.4 %copy-start.3 = (f32[16,2048]{1,0:T(8,128)S(1)}, f32[16,2048]{1,0:T(8,128)}, u32[]{:S(2)}) copy-start(f32[16,2048]{1,0:T(8,128)} %shard_map.95) | copy-start | bytes 393220
  150.5 3.0 %copy-start.8 = (f32[64,64]{1,0:T(8,128)S(1)}, f32[64,64]{1,0:T(8,128)}, u32[]{:S(2)}) copy-start(f32[64,64]{1,0:T(8,128)} %shard_map.96) | copy-start | bytes 49156
Sparse Core Ops, SparseCore 0:
  67.1 52.7 reduce-scatter.1

commit v5 on v3

--- a/solution.py
+++ b/solution.py
@@ -11,51 +11,6 @@
 
 adapter_scale = 2.0
 norm_eps = 1e-05
-
-
-def _exchange_sum_kernel(n, group_index, device_of, x_ref, o_ref, recv, send_sems, recv_sems):
-    me = group_index()
-    barrier = pltpu.get_barrier_semaphore()
-    for shift in range(1, n):
-        pl.semaphore_signal(
-            barrier, inc=1, device_id=device_of(lax.rem(me + shift, n)), device_id_type=MESH
-        )
-    pl.semaphore_wait(barrier, n - 1)
-    copies = []
-    for shift in range(1, n):
-        target = lax.rem(me + shift, n)
-        copy = pltpu.make_async_remote_copy(
-            src_ref=x_ref.at[target],
-            dst_ref=recv.at[shift],
-            send_sem=send_sems.at[shift],
-            recv_sem=recv_sems.at[shift],
-            device_id=device_of(target),
-            device_id_type=MESH,
-        )
-        copy.start()
-        copies.append(copy)
-    o_ref[...] = x_ref[me]
-    for shift, copy in zip(range(1, n), copies):
-        copy.wait_recv()
-        o_ref[...] += recv[shift]
-    for copy in copies:
-        copy.wait_send()
-
-
-def exchange_sum(x, n, group_index, device_of, collective_id):
-    chunk = x.shape[1:]
-    return pl.pallas_call(
-        functools.partial(_exchange_sum_kernel, n, group_index, device_of),
-        out_shape=jax.ShapeDtypeStruct(chunk, x.dtype),
-        in_specs=[pl.BlockSpec(memory_space=pltpu.VMEM)],
-        out_specs=pl.BlockSpec(memory_space=pltpu.VMEM),
-        scratch_shapes=[
-            pltpu.VMEM((n,) + chunk, x.dtype),
-            pltpu.SemaphoreType.DMA((n,)),
-            pltpu.SemaphoreType.DMA((n,)),
-        ],
-        compiler_params=pltpu.CompilerParams(collective_id=collective_id, has_side_effects=True),
-    )(x)
 
 
 def _two_stage_sum_kernel(n1, n2, x_ref, o_ref, stage, recv1, recv2, sems):
@@ -126,6 +81,59 @@
     )(x)
 
 
+def _tensor_sum_kernel(n, kv_ref, rk_ref, own_kv_ref, own_rk_ref, kv_out, rk_out, recv_kv, recv_rk, sems):
+    me = lax.axis_index("tensor")
+    member = lambda j: (lax.axis_index("trial"), lax.axis_index("dp"), j)
+    barrier = pltpu.get_barrier_semaphore()
+    for shift in range(1, n):
+        pl.semaphore_signal(barrier, inc=1, device_id=member(lax.rem(me + shift, n)), device_id_type=MESH)
+    pl.semaphore_wait(barrier, n - 1)
+    copies = []
+    for shift in range(1, n):
+        target = lax.rem(me + shift, n)
+        for which, (src_ref, dst_ref) in enumerate(((kv_ref, recv_kv), (rk_ref, recv_rk))):
+            copy = pltpu.make_async_remote_copy(
+                src_ref=src_ref.at[target],
+                dst_ref=dst_ref.at[shift],
+                send_sem=sems.at[2 * which, shift],
+                recv_sem=sems.at[2 * which + 1, shift],
+                device_id=member(target),
+                device_id_type=MESH,
+            )
+            copy.start()
+            copies.append(copy)
+    kv_out[...] = own_kv_ref[...]
+    rk_out[...] = own_rk_ref[...]
+    for shift in range(1, n):
+        kv_copy, rk_copy = copies[2 * shift - 2], copies[2 * shift - 1]
+        rk_copy.wait_recv()
+        rk_out[...] += recv_rk[shift]
+        kv_copy.wait_recv()
+        kv_out[...] += recv_kv[shift].astype(jnp.float32)
+    for copy in copies:
+        copy.wait_send()
+
+
+def tensor_sum(kv, rk, own_kv, own_rk, collective_id):
+    n = kv.shape[0]
+    vmem = pl.BlockSpec(memory_space=pltpu.VMEM)
+    return pl.pallas_call(
+        functools.partial(_tensor_sum_kernel, n),
+        out_shape=(
+            jax.ShapeDtypeStruct(own_kv.shape, jnp.float32),
+            jax.ShapeDtypeStruct(own_rk.shape, jnp.float32),
+        ),
+        in_specs=[vmem] * 4,
+        out_specs=(vmem, vmem),
+        scratch_shapes=[
+            pltpu.VMEM(kv.shape, kv.dtype),
+            pltpu.VMEM(rk.shape, rk.dtype),
+            pltpu.SemaphoreType.DMA((4, n)),
+        ],
+        compiler_params=pltpu.CompilerParams(collective_id=collective_id, has_side_effects=True),
+    )(kv, rk, own_kv, own_rk)
+
+
 def shards(
     residual_rows,
     input_norm_weight,
@@ -182,11 +190,15 @@
     down_weight = adapter_down_weight[0]
     keyval = jnp.dot(rows, keyvalue_weight, preferred_element_type=jnp.float32)
     ranks = jnp.dot(rows, down_weight, preferred_element_type=jnp.float32)
-    summed = lax.psum_scatter(
-        jnp.concatenate([keyval, ranks], axis=1), "tensor", scatter_dimension=0, tiled=True
-    )
-    frozen_output_local = summed[:, :kv_width]
-    local_rank_rows = summed[:, kv_width:]
+    block = tok_dev // tensors
+    mine = lax.axis_index("tensor") * block
+    frozen_output_local, local_rank_rows = tensor_sum(
+        keyval.astype(jnp.bfloat16).reshape(tensors, block, kv_width),
+        ranks.reshape(tensors, block, ranks.shape[1]),
+        lax.dynamic_slice_in_dim(keyval, mine, block, 0),
+        lax.dynamic_slice_in_dim(ranks, mine, block, 0),
+        0,
+    )
     adapter_key = jnp.dot(
         local_rank_rows[:, :rank_index], up_weight[:, :keyvalue_half], precision=highest_precision
     )
@@ -197,13 +209,7 @@
         [adapter_key, adapter_value], axis=1
     )
 
-    grad_a = exchange_sum(
-        grad_a_term.reshape(dps, grad_a_term.shape[0] // dps, grad_a_term.shape[1]),
-        dps,
-        lambda: lax.axis_index("dp"),
-        lambda j: (lax.axis_index("trial"), j, lax.axis_index("tensor")),
-        0,
-    )
+    grad_a = lax.psum_scatter(grad_a_term, "dp", scatter_dimension=0, tiled=True)
 
     key_down_gradient = jnp.dot(
         local_rank_rows[:, :rank_index].T, grad_in[:, :keyvalue_half], precision=highest_precision

time: 158 us -> 149 us (0.943)
  blocking collectives: 43.6 us -> 18.9 us
  starting transfers between devices: 0.04 us -> 8.81 us
  waiting for transfers between devices: 5.74 us -> 10.9 us
  matrix products: 16.9 us -> 19.9 us
  other arithmetic: 6.46 us -> 4.11 us
    all_to_all x1 -> x0, blocking collectives: 37.6 us -> none  [shards(): lax.all_to_all(chosen.reshape(trials * tensors, select, normed_input), ('...]
    all_gather x1, blocking collectives: 6.02 us -> 18.9 us  [shards(): every_rank = lax.all_gather(rank_gradient, 'tensor', axis=0, tiled=True)]
    all_to_all x0 -> x1, waiting for transfers between devices: none -> 10.9 us  [shards(): lax.all_to_all(chosen.reshape(trials * tensors, select, normed_input), ('...]
    all_to_all x0 -> x1, starting transfers between devices: none -> 8.77 us  [shards(): lax.all_to_all(chosen.reshape(trials * tensors, select, normed_input), ('...]
    reduce_scatter x1, waiting for transfers between devices: 5.72 us -> 0.01 us  [shards(): lax.psum_scatter(grad_a_term, 'dp', scatter_dimension=0, tiled=True)]
    dot_general x1, matrix products: 6.88 us -> 9.9 us  [shards(): keyval = jnp.dot(rows, keyvalue_weight, preferred_element_type=jnp.float32)]
    concatenate x1 -> x0, other arithmetic: 2.38 us -> none  [shards(): jnp.concatenate([keyval, ranks], axis=1)]
    unnamed x22 -> x21, local copies, waits for them, and re-layouts: 3.56 us -> 1.26 us
  transfers between devices with their start and end apart: 1 -> 2, of which waited for: 1 -> 1; matrix products, arithmetic and copies ran while one was open for 2% -> 14% of each run, Pallas kernels for 21% -> 39%
where the time goes in v5:
time: 149 us; the launch traced here: 148 us
  Pallas kernels  57.8 us (39%)
  matrix products  19.9 us (13%)
  blocking collectives  18.9 us (13%)
  between operations  14.3 us (10%)
  local copies, waits for them, and re-layouts  13.6 us (9%)
  waiting for transfers between devices  10.9 us (7%)
  starting transfers between devices  8.81 us (6%)
  other arithmetic  4.11 us (3%)
    pallas_call x1, Pallas kernels, tensor_sum(): pl.pallas_call(functools.partial(_tensor_sum_kernel, n), out_shape=(jax.S...  31.6 us
    pallas_call x1, Pallas kernels, two_stage_sum(): pl.pallas_call(functools.partial(_two_stage_sum_kernel, n1, n2), out_shap...  26.2 us
    all_gather x1, blocking collectives, shards(): every_rank = lax.all_gather(rank_gradient, 'tensor', axis=0, tiled=True)  18.9 us
    all_to_all x1, waiting for transfers between devices, shards(): lax.all_to_all(chosen.reshape(trials * tensors, select, normed_input), ('...  10.9 us
    dot_general x1, matrix products, shards(): keyval = jnp.dot(rows, keyvalue_weight, preferred_element_type=jnp.float32)  9.9 us
    all_to_all x1, starting transfers between devices, shards(): lax.all_to_all(chosen.reshape(trials * tensors, select, normed_input), ('...  8.77 us
    reshape x2, local copies, waits for them, and re-layouts, shards(): chosen.reshape(trials, select, tensors, normed_input).transpose(0, 2, 1, 3)  8.6 us
    dot_general x1, matrix products, shards(): lax.dot_general(every_rank, rows, (((0,), (0,)), ((), ())), preferred_ele...  3.03 us
  transfers between devices with their start and end apart: 2, of which 1 were waited for; matrix products, arithmetic and copies ran while one was open for 14% of the time, Pallas kernels for 39%

profile of v5, /device:TPU:1, one launch (start us, length us, event | category | flops | bytes accessed | tf_op | source)
XLA Modules:
  0.0 148.3 jit_solution(1929692417643517160)
XLA Ops:
  7.2 0.9 constant_dynamic-slice_fusion.2
  8.2 0.6 copy-done
  8.8 0.8 multiply_reduce_fusion
  9.6 1.8 %multiply_convert_fusion = bf16[128,8192]{1,0:T(8,128)(2,1)} fusion(f32[128,8192]{1,0:T(8,128)S(1)} %get-tuple-element.8, f32[8192]{0:T(1024)S(1)} %copy-done.9, f32[128]{0:T(128)S(1)} %add_rsqrt_fusion), kind=kLoop, calls=%fused_computation | loop fusion | flops 3145728 | bytes 6324736 | tf_op jit(solution)/shard_map/convert_element_type | solution.py:163
  11.4 4.5 %reshape.34 = bf16[8,16,4,2048]{3,2,1,0:T(4,128)(2,1)} reshape(bf16[128,8192]{1,0:T(8,128)(2,1)} %multiply_convert_fusion) | data formatting | bytes 4194304 | tf_op jit(solution)/shard_map/reshape | solution.py:164
  16.0 4.1 %copy.10 = bf16[8,16,4,2048]{3,1,2,0:T(8,128)(2,1)} copy(bf16[8,16,4,2048]{3,2,1,0:T(4,128)(2,1)} %reshape.34) | data formatting | bytes 4194304 | tf_op jit(solution)/shard_map/reshape | solution.py:164
  20.1 8.8 %all-to-all-start = ((bf16[32,16,2048]{2,1,0:T(8,128)(2,1)}), bf16[32,16,2048]{2,1,0:T(8,128)(2,1)}, u32[]{:S(2)}, u32[]{:S(2)}) async-start(bf16[32,16,2048]{2,1,0:T(8,128)(2,1)} %bitcast.23), calls=%async_computation | async-start | bytes 4194304 | tf_op jit(solution)/shard_map/all_to_all | solution.py:165
  29.4 18.9 %all_gather.3 = bf16[512,128]{1,0:T(8,128)(2,1)S(1)} all-gather(bf16[128,128]{1,0:T(8,128)(2,1)S(1)} %fusion.19), channel_id=1, replica_groups=mesh['trial'=8,'dp'=8,'tensor'=4] {'tensor'}, dimensions={0}, use_global_device_ids=true | all-gather | bytes 163840 | tf_op jit(solution)/shard_map/all_gather | solution.py:185
  48.3 10.9 %all-to-all-done = bf16[32,16,2048]{2,1,0:T(8,128)(2,1)} async-done(((bf16[32,16,2048]{2,1,0:T(8,128)(2,1)}), bf16[32,16,2048]{2,1,0:T(8,128)(2,1)}, u32[]{:S(2)}, u32[]{:S(2)}) %all-to-all-start) | async-done | bytes 2097184 | tf_op jit(solution)/shard_map/all_to_all | solution.py:165
  59.2 3.0 %fusion.27 = f32[128,2048]{1,0:T(8,128)} fusion(bf16[512,128]{1,0:T(8,128)(2,1)S(1)} %all_gather.3, bf16[512,2048]{1,0:T(8,128)(2,1)} %bitcast.2), kind=kOutput, calls=%fused_computation.37 | convolution fusion | flops 268435456 | bytes 3276800 | tf_op jit(solution)/shard_map/dot_general | solution.py:186
  62.3 9.9 %fusion.26 = (bf16[512,2048]{1,0:T(8,128)(2,1)}, f32[512,2048]{1,0:T(8,128)S(1)}) fusion(bf16[512,2048]{1,0:T(8,128)(2,1)} %bitcast.2, bf16[2048,2048]{1,0:T(8,128)(2,1)} %param.10), kind=kOutput, calls=%fused_computation.36 | convolution fusion | flops 4296015872 | bytes 16777216 | tf_op jit(solution)/shard_map/dot_general | solution.py:191
  72.2 2.4 %fusion.3 = f32[512,128]{1,0:T(8,128)S(1)} fusion(bf16[512,2048]{1,0:T(8,128)(2,1)} %bitcast.2, bf16[1,2048,128]{2,1,0:T(8,128)(2,1)S(1)} %copy-done.5), kind=kOutput, calls=%fused_computation.7 | convolution fusion | flops 268435456 | bytes 2883584 | tf_op jit(solution)/shard_map/dot_general | solution.py:192
  74.6 0.7 constant_dynamic-slice_fusion.own_rk_ref
  75.3 1.0 constant_dynamic-slice_fusion.1.own_kv_ref
  76.3 31.6 %shard_map.94 = (f32[128,2048]{1,0:T(8,128)}, f32[128,128]{1,0:T(8,128)}) custom-call(bf16[4,128,2048]{2,1,0:T(8,128)(2,1)} %bitcast.24, f32[4,128,128]{2,1,0:T(8,128)} %bitcast.25, f32[128,2048]{1,0:T(8,128)} %constant_dynamic-slice_fusion.1.own_kv_ref, f32[128,128]{1,0:T(8,128)} %constant_dynamic-slice_fusion.own_rk_ref), custom_call_target="tpu_custom_call" | custom-call | tf_op jit(solution)/shard_map/pallas_call | solution.py:120
  108.0 1.2 fusion.9
  109.2 0.3 concatenate.16
  109.7 1.3 fusion.5
  111.6 1.1 fusion.2.x_ref
  112.7 26.2 %shard_map.95 = f32[64,64]{1,0:T(8,128)} custom-call(f32[4,8,64,64]{3,2,1,0:T(8,128)} %fusion.2.x_ref), custom_call_target="tpu_custom_call" | custom-call | tf_op jit(solution)/shard_map/pallas_call | solution.py:69
  138.9 0.4 fusion.14
  139.3 0.4 fusion.17
  139.7 1.1 fusion.1
  140.8 0.6 copy.14
  (30 shorter events, 1.4 us)
Async XLA Ops:
  7.2 1.6 %copy-start = (bf16[128,8192]{1,0:T(8,128)(2,1)S(1)}, bf16[128,8192]{1,0:T(8,128)(2,1)}, u32[]{:S(2)}) copy-start(bf16[128,8192]{1,0:T(8,128)(2,1)} %param.7) | copy-start | bytes 6291460
  8.8 0.8 copy-start.9
  20.1 8.8 %copy-start.4 = (bf16[1,128,2048]{2,1,0:T(8,128)(2,1)S(1)}, bf16[1,128,2048]{2,1,0:T(8,128)(2,1)}, u32[]{:S(2)}) copy-start(bf16[1,128,2048]{2,1,0:T(8,128)(2,1)} %param.13) | copy-start | bytes 1572868
  20.1 8.8 %copy-start.6 = (bf16[1,64,2048]{2,1,0:T(8,128)(2,1)S(1)}, bf16[1,64,2048]{2,1,0:T(8,128)(2,1)}, u32[]{:S(2)}) copy-start(bf16[1,64,2048]{2,1,0:T(8,128)(2,1)} %param.12) | copy-start | bytes 786436
  20.1 39.1 %all-to-all-start = ((bf16[32,16,2048]{2,1,0:T(8,128)(2,1)}), bf16[32,16,2048]{2,1,0:T(8,128)(2,1)}, u32[]{:S(2)}, u32[]{:S(2)}) async-start(bf16[32,16,2048]{2,1,0:T(8,128)(2,1)} %bitcast.23), calls=%async_computation | async-start | bytes 4194304 | tf_op jit(solution)/shard_map/all_to_all | solution.py:165
  28.8 112.0 %reduce-scatter.2.cloned.1.call-start = ((), (), s32[]{:S(2)}) async-start(), calls=%async_computation.2 | async-start | bytes 1179648 | tf_op jit(solution)/shard_map/reduce_scatter | solution.py:212
  62.3 9.9 %copy-start.5 = (bf16[1,2048,128]{2,1,0:T(8,128)(2,1)S(1)}, bf16[1,2048,128]{2,1,0:T(8,128)(2,1)}, u32[]{:S(2)}) copy-start(bf16[1,2048,128]{2,1,0:T(8,128)(2,1)} %param.11) | copy-start | bytes 1572868
  74.6 1.7 %copy-start.1 = (f32[512,128]{1,0:T(8,128)}, f32[512,128]{1,0:T(8,128)S(1)}, u32[]{:S(2)}) copy-start(f32[512,128]{1,0:T(8,128)S(1)} %fusion.3) | copy-start | bytes 786436
  107.9 1.8 %copy-start.3 = (f32[128,128]{1,0:T(8,128)S(1)}, f32[128,128]{1,0:T(8,128)}, u32[]{:S(2)}) copy-start(f32[128,128]{1,0:T(8,128)} %get-tuple-element.6) | copy-start | bytes 196612
  111.4 27.5 %copy-start.7 = (bf16[1,64,2048]{2,1,0:T(8,128)(2,1)S(1)}, bf16[1,64,2048]{2,1,0:T(8,128)(2,1)}, u32[]{:S(2)}) copy-start(bf16[1,64,2048]{2,1,0:T(8,128)(2,1)} %param.12) | copy-start | bytes 786436
  112.7 27.0 %copy-start.2 = (f32[128,2048]{1,0:T(8,128)S(1)}, f32[128,2048]{1,0:T(8,128)}, u32[]{:S(2)}) copy-start(f32[128,2048]{1,0:T(8,128)} %get-tuple-element.5) | copy-start | bytes 3145732
  139.3 1.5 %copy-start.8 = (f32[64,64]{1,0:T(8,128)S(1)}, f32[64,64]{1,0:T(8,128)}, u32[]{:S(2)}) copy-start(f32[64,64]{1,0:T(8,128)} %shard_map.95) | copy-start | bytes 49156
Sparse Core Ops, SparseCore 0:
  62.4 32.9 reduce-scatter.1

commit v6 on v5

--- a/solution.py
+++ b/solution.py
@@ -158,10 +158,15 @@
     source = lax.axis_index("trial") * tensors + lax.axis_index("tensor")
     picks = lax.dynamic_slice_in_dim(trial_row_index, source * select, select, 1).reshape(-1)
     onehot = (picks[:, None] == jnp.arange(pool_dev, dtype=jnp.int32)[None, :]).astype(jnp.bfloat16)
-    wide = jnp.dot(onehot, residual_rows, preferred_element_type=jnp.float32)
-    msq = jnp.mean(wide * wide, axis=1, keepdims=True)
-    chosen = (wide * lax.rsqrt(msq + norm_eps) * input_norm_weight[None, :]).astype(jnp.bfloat16)
-    chosen = chosen.reshape(trials, select, tensors, normed_input).transpose(0, 2, 1, 3)
+    wide = jnp.einsum(
+        "tsr,rkf->tksf",
+        onehot.reshape(trials, select, pool_dev),
+        residual_rows.reshape(pool_dev, tensors, normed_input),
+        preferred_element_type=jnp.float32,
+    )
+    msq = jnp.mean(wide * wide, axis=(1, 3), keepdims=True)
+    gain = input_norm_weight.reshape(1, tensors, 1, normed_input)
+    chosen = (wide * lax.rsqrt(msq + norm_eps) * gain).astype(jnp.bfloat16)
     arrived = lax.all_to_all(
         chosen.reshape(trials * tensors, select, normed_input),
         ("trial", "tensor"),

time: 149 us -> 137 us (0.919)
  local copies, waits for them, and re-layouts: 13.6 us -> 5.02 us
  matrix products: 19.9 us -> 16.6 us
    reshape x2 -> x0, local copies, waits for them, and re-layouts: 8.6 us -> none  [shards(): chosen.reshape(trials, select, tensors, normed_input).transpose(0, 2, 1, 3)]
    dot_general x1, matrix products: 2.4 us -> 0.71 us  [shards(): ranks = jnp.dot(rows, down_weight, preferred_element_type=jnp.float32)]
    dot_general x1, matrix products: 0.84 us -> 2.42 us  [shards(): jnp.einsum('tsr,rkf->tksf', onehot.reshape(trials, select, pool_dev), res...]
    dot_general x1, matrix products: 3.03 us -> 1.46 us  [shards(): lax.dot_general(every_rank, rows, (((0,), (0,)), ((), ())), preferred_ele...]
  transfers between devices with their start and end apart: 2 -> 2, of which waited for: 1 -> 1; matrix products, arithmetic and copies ran while one was open for 14% -> 13% of each run, Pallas kernels for 39% -> 42%
where the time goes in v6:
time: 137 us; the launch traced here: 136 us
  Pallas kernels  57.8 us (42%)
  blocking collectives  18.9 us (14%)
  matrix products  16.6 us (12%)
  between operations  14.3 us (10%)
  waiting for transfers between devices  10.8 us (8%)
  starting transfers between devices  8.76 us (6%)
  local copies, waits for them, and re-layouts  5.02 us (4%)
  other arithmetic  4.28 us (3%)
    pallas_call x1, Pallas kernels, tensor_sum(): pl.pallas_call(functools.partial(_tensor_sum_kernel, n), out_shape=(jax.S...  31.6 us
    pallas_call x1, Pallas kernels, two_stage_sum(): pl.pallas_call(functools.partial(_two_stage_sum_kernel, n1, n2), out_shap...  26.2 us
    all_gather x1, blocking collectives, shards(): every_rank = lax.all_gather(rank_gradient, 'tensor', axis=0, tiled=True)  18.9 us
    all_to_all x1, waiting for transfers between devices, shards(): lax.all_to_all(chosen.reshape(trials * tensors, select, normed_input), ('...  10.8 us
    dot_general x1, matrix products, shards(): keyval = jnp.dot(rows, keyvalue_weight, preferred_element_type=jnp.float32)  9.21 us
    all_to_all x1, starting transfers between devices, shards(): lax.all_to_all(chosen.reshape(trials * tensors, select, normed_input), ('...  8.72 us
  transfers between devices with their start and end apart: 2, of which 1 were waited for; matrix products, arithmetic and copies ran while one was open for 13% of the time, Pallas kernels for 42%

profile of v6, /device:TPU:1, one launch (start us, length us, event | category | flops | bytes accessed | tf_op | source)
XLA Modules:
  0.0 136.5 jit_solution(15682817426424230887)
XLA Ops:
  7.2 0.8 mul.57
  8.0 0.8 constant_dynamic-slice_fusion.2
  8.8 2.4 %multiply_reduce_fusion = (f32[8,16]{1,0:T(8,128)S(1)}, f32[8,16,4,2048]{3,1,2,0:T(8,128)S(1)}) fusion(bf16[16,4,8,2048]{3,2,1,0:T(8,128)(2,1)} %bitcast.45, s32[8,16]{1,0:T(8,128)S(1)} %constant_dynamic-slice_fusion.2), kind=kOutput, calls=%fused_computation.1 | convolution fusion | flops 270548864 | bytes 6292480 | tf_op jit(solution)/shard_map/tsr,rkf->tksf/dot_general | solution.py:161
  11.2 2.0 %multiply_convert_fusion = bf16[8,16,4,2048]{3,1,2,0:T(8,128)(2,1)} fusion(f32[8,16,4,2048]{3,1,2,0:T(8,128)S(1)} %get-tuple-element.8, f32[4,2048]{1,0:T(4,128)S(1)} %mul.57, f32[8,16]{1,0:T(8,128)S(1)} %add_rsqrt_fusion), kind=kLoop, calls=%fused_computation | loop fusion | flops 3145728 | bytes 6324736 | tf_op jit(solution)/shard_map/convert_element_type | solution.py:169
  13.2 8.7 %all-to-all-start = ((bf16[32,16,2048]{2,1,0:T(8,128)(2,1)}), bf16[32,16,2048]{2,1,0:T(8,128)(2,1)S(1)}, u32[]{:S(2)}, u32[]{:S(2)}) async-start(bf16[32,16,2048]{2,1,0:T(8,128)(2,1)} %bitcast.44), calls=%async_computation | async-start | bytes 4194304 | tf_op jit(solution)/shard_map/all_to_all | solution.py:170
  22.0 0.2 fusion.13
  22.5 18.9 %all_gather.3 = bf16[512,128]{1,0:T(8,128)(2,1)S(1)} all-gather(bf16[128,128]{1,0:T(8,128)(2,1)S(1)} %fusion.21), channel_id=1, replica_groups=mesh['trial'=8,'dp'=8,'tensor'=4] {'tensor'}, dimensions={0}, use_global_device_ids=true | all-gather | bytes 163840 | tf_op jit(solution)/shard_map/all_gather | solution.py:190
  41.5 10.8 %all-to-all-done = bf16[32,16,2048]{2,1,0:T(8,128)(2,1)S(1)} async-done(((bf16[32,16,2048]{2,1,0:T(8,128)(2,1)}), bf16[32,16,2048]{2,1,0:T(8,128)(2,1)S(1)}, u32[]{:S(2)}, u32[]{:S(2)}) %all-to-all-start) | async-done | bytes 2097184 | tf_op jit(solution)/shard_map/all_to_all | solution.py:170
  52.3 1.5 %fusion.30 = f32[128,2048]{1,0:T(8,128)} fusion(bf16[512,128]{1,0:T(8,128)(2,1)S(1)} %all_gather.3, bf16[512,2048]{1,0:T(8,128)(2,1)S(1)} %bitcast.41), kind=kOutput, calls=%fused_computation.40 | convolution fusion | flops 268435456 | bytes 3276800 | tf_op jit(solution)/shard_map/dot_general | solution.py:191
  53.7 9.2 %fusion.29 = (bf16[512,2048]{1,0:T(8,128)(2,1)}, f32[512,2048]{1,0:T(8,128)S(1)}) fusion(bf16[512,2048]{1,0:T(8,128)(2,1)S(1)} %bitcast.42, bf16[2048,2048]{1,0:T(8,128)(2,1)} %param.10), kind=kOutput, calls=%fused_computation.39 | convolution fusion | flops 4296015872 | bytes 16777216 | tf_op jit(solution)/shard_map/dot_general | solution.py:196
  63.0 0.7 fusion.5
  63.7 0.7 constant_dynamic-slice_fusion.own_rk_ref
  64.4 1.0 constant_dynamic-slice_fusion.1.own_kv_ref
  65.4 31.6 %shard_map.94 = (f32[128,2048]{1,0:T(8,128)}, f32[128,128]{1,0:T(8,128)}) custom-call(bf16[4,128,2048]{2,1,0:T(8,128)(2,1)} %bitcast.46, f32[4,128,128]{2,1,0:T(8,128)} %bitcast.47, f32[128,2048]{1,0:T(8,128)} %constant_dynamic-slice_fusion.1.own_kv_ref, f32[128,128]{1,0:T(8,128)} %constant_dynamic-slice_fusion.own_rk_ref), custom_call_target="tpu_custom_call" | custom-call | tf_op jit(solution)/shard_map/pallas_call | solution.py:120
  97.1 1.2 fusion.11
  98.3 0.3 concatenate.16
  98.9 0.4 fusion.7
  99.3 0.3 concatenate.17
  99.8 1.1 fusion.4.x_ref
  100.9 26.2 %shard_map.95 = f32[64,64]{1,0:T(8,128)} custom-call(f32[4,8,64,64]{3,2,1,0:T(8,128)} %fusion.4.x_ref), custom_call_target="tpu_custom_call" | custom-call | tf_op jit(solution)/shard_map/pallas_call | solution.py:69
  127.1 0.4 fusion.16
  127.5 0.4 fusion.19
  127.9 1.1 fusion.3
  129.0 0.6 copy.23
  (24 shorter events, 0.7 us)
Async XLA Ops:
  7.2 55.8 %copy-start = (bf16[1,2048,128]{2,1,0:T(8,128)(2,1)S(1)}, bf16[1,2048,128]{2,1,0:T(8,128)(2,1)}, u32[]{:S(2)}) copy-start(bf16[1,2048,128]{2,1,0:T(8,128)(2,1)} %param.11) | copy-start | bytes 1572868
  13.2 8.8 %copy-start.4 = (bf16[1,128,2048]{2,1,0:T(8,128)(2,1)S(1)}, bf16[1,128,2048]{2,1,0:T(8,128)(2,1)}, u32[]{:S(2)}) copy-start(bf16[1,128,2048]{2,1,0:T(8,128)(2,1)} %param.13) | copy-start | bytes 1572868
  13.2 8.8 %copy-start.5 = (bf16[1,64,2048]{2,1,0:T(8,128)(2,1)S(1)}, bf16[1,64,2048]{2,1,0:T(8,128)(2,1)}, u32[]{:S(2)}) copy-start(bf16[1,64,2048]{2,1,0:T(8,128)(2,1)} %param.12) | copy-start | bytes 786436
  13.2 39.0 %all-to-all-start = ((bf16[32,16,2048]{2,1,0:T(8,128)(2,1)}), bf16[32,16,2048]{2,1,0:T(8,128)(2,1)S(1)}, u32[]{:S(2)}, u32[]{:S(2)}) async-start(bf16[32,16,2048]{2,1,0:T(8,128)(2,1)} %bitcast.44), calls=%async_computation | async-start | bytes 4194304 | tf_op jit(solution)/shard_map/all_to_all | solution.py:170
  21.9 107.1 %reduce-scatter.2.cloned.1.call-start = ((), (), s32[]{:S(2)}) async-start(), calls=%async_computation.2 | async-start | bytes 1179648 | tf_op jit(solution)/shard_map/reduce_scatter | solution.py:217
  63.7 1.8 %copy-start.1 = (f32[512,128]{1,0:T(8,128)}, f32[512,128]{1,0:T(8,128)S(1)}, u32[]{:S(2)}) copy-start(f32[512,128]{1,0:T(8,128)S(1)} %fusion.5) | copy-start | bytes 786436
  97.1 1.8 %copy-start.3 = (f32[128,128]{1,0:T(8,128)S(1)}, f32[128,128]{1,0:T(8,128)}, u32[]{:S(2)}) copy-start(f32[128,128]{1,0:T(8,128)} %get-tuple-element.6) | copy-start | bytes 196612
  99.6 27.5 %copy-start.6 = (bf16[1,64,2048]{2,1,0:T(8,128)(2,1)S(1)}, bf16[1,64,2048]{2,1,0:T(8,128)(2,1)}, u32[]{:S(2)}) copy-start(bf16[1,64,2048]{2,1,0:T(8,128)(2,1)} %param.12) | copy-start | bytes 786436
  99.8 28.1 %copy-start.2 = (f32[128,2048]{1,0:T(8,128)S(1)}, f32[128,2048]{1,0:T(8,128)}, u32[]{:S(2)}) copy-start(f32[128,2048]{1,0:T(8,128)} %get-tuple-element.5) | copy-start | bytes 3145732
  127.5 1.5 %copy-start.7 = (f32[64,64]{1,0:T(8,128)S(1)}, f32[64,64]{1,0:T(8,128)}, u32[]{:S(2)}) copy-start(f32[64,64]{1,0:T(8,128)} %shard_map.95) | copy-start | bytes 49156
Sparse Core Ops, SparseCore 0:
  53.9 33.3 reduce-scatter.1

commit v7 on v1

--- a/solution.py
+++ b/solution.py
@@ -1,10 +1,131 @@
+import functools
+
 import jax
 import jax.numpy as jnp
 from jax import lax
+from jax.experimental import pallas as pl
+from jax.experimental.pallas import tpu as pltpu
 from jax.sharding import PartitionSpec as P
+
+MESH = pl.DeviceIdType.MESH
 
 adapter_scale = 2.0
 norm_eps = 1e-05
+
+
+def _tensor_sum_kernel(
+    n1, n2, kv_ref, rk_ref, own_kv_ref, own_rk_ref, gk_ref, gv_ref,
+    kv_out, rk_out, b_out,
+    recv_kv, recv_rk, terms, recv_b1, partial, recv_b2, sems,
+):
+    me1 = lax.axis_index("tensor")
+    me2 = lax.axis_index("dp")
+    trial = lax.axis_index("trial")
+    first = lambda j: (trial, me2, j)
+    second = lambda j: (trial, j, me1)
+    quarter = n2 // 2
+    barrier = pltpu.get_barrier_semaphore()
+    for shift in range(1, n1):
+        pl.semaphore_signal(barrier, inc=1, device_id=first(lax.rem(me1 + shift, n1)), device_id_type=MESH)
+    for shift in range(1, n2):
+        pl.semaphore_signal(barrier, inc=1, device_id=second(lax.rem(me2 + shift, n2)), device_id_type=MESH)
+    pl.semaphore_wait(barrier, n1 + n2 - 2)
+
+    def send(src_ref, dst_ref, row, shift, device):
+        copy = pltpu.make_async_remote_copy(
+            src_ref=src_ref,
+            dst_ref=dst_ref.at[shift],
+            send_sem=sems.at[row, shift],
+            recv_sem=sems.at[row + 1, shift],
+            device_id=device,
+            device_id_type=MESH,
+        )
+        copy.start()
+        return copy
+
+    rk_copies, kv_copies = [], []
+    for shift in range(1, n1):
+        target = lax.rem(me1 + shift, n1)
+        rk_copies.append(send(rk_ref.at[target], recv_rk, 2, shift, first(target)))
+    for shift in range(1, n1):
+        target = lax.rem(me1 + shift, n1)
+        kv_copies.append(send(kv_ref.at[target], recv_kv, 0, shift, first(target)))
+
+    rk_out[...] = own_rk_ref[...]
+    for shift, copy in zip(range(1, n1), rk_copies):
+        copy.wait_recv()
+        rk_out[...] += recv_rk[shift]
+
+    xa = rk_out[...]
+    lane = lax.broadcasted_iota(jnp.int32, xa.shape, 1)
+    half = xa.shape[1] // 2
+    total = None
+    for g_ref, keep in ((gk_ref, lane < half), (gv_ref, lane >= half)):
+        part = jnp.where(keep, xa, 0.0)
+        high = part.astype(jnp.bfloat16)
+        low = (part - high.astype(jnp.float32)).astype(jnp.bfloat16)
+        g = g_ref[...]
+        for piece in (high, low):
+            term = jnp.dot(g, piece, preferred_element_type=jnp.float32)
+            total = term if total is None else total + term
+    terms[...] = total.reshape(terms.shape)
+
+    b1_copies = []
+    for shift in range(1, n1):
+        target = lax.rem(me1 + shift, n1)
+        b1_copies.append(send(terms.at[target], recv_b1, 4, shift, first(target)))
+
+    kv_out[...] = own_kv_ref[...]
+    for shift, copy in zip(range(1, n1), kv_copies):
+        copy.wait_recv()
+        kv_out[...] += recv_kv[shift].astype(jnp.float32)
+
+    summed = terms[me1]
+    for shift, copy in zip(range(1, n1), b1_copies):
+        copy.wait_recv()
+        summed = summed + recv_b1[shift]
+    partial[...] = summed.reshape(partial.shape)
+
+    b2_copies = []
+    for shift in range(1, n2):
+        target = lax.rem(me2 + shift, n2)
+        b2_copies.append(send(partial.at[lax.rem(target, quarter)], recv_b2, 6, shift, second(target)))
+    b_out[...] = partial[lax.rem(me2, quarter)]
+    for shift, copy in zip(range(1, n2), b2_copies):
+        copy.wait_recv()
+        b_out[...] += recv_b2[shift]
+
+    for copy in rk_copies + kv_copies + b1_copies + b2_copies:
+        copy.wait_send()
+
+
+def tensor_sum(kv, rk, own_kv, own_rk, gk, gv, n2, collective_id):
+    n1 = kv.shape[0]
+    quarter = n2 // 2
+    columns = gk.shape[0]
+    lanes = rk.shape[2]
+    block = columns // (n1 * quarter)
+    vmem = pl.BlockSpec(memory_space=pltpu.VMEM)
+    return pl.pallas_call(
+        functools.partial(_tensor_sum_kernel, n1, n2),
+        out_shape=(
+            jax.ShapeDtypeStruct(own_kv.shape, jnp.float32),
+            jax.ShapeDtypeStruct(own_rk.shape, jnp.float32),
+            jax.ShapeDtypeStruct((block, lanes), jnp.float32),
+        ),
+        in_specs=[vmem] * 6,
+        out_specs=(vmem, vmem, vmem),
+        scratch_shapes=[
+            pltpu.VMEM(kv.shape, kv.dtype),
+            pltpu.VMEM(rk.shape, rk.dtype),
+            pltpu.VMEM((n1, quarter * block, lanes), jnp.float32),
+            pltpu.VMEM((n1, quarter * block, lanes), jnp.float32),
+            pltpu.VMEM((quarter, block, lanes), jnp.float32),
+            pltpu.VMEM((n2, block, lanes), jnp.float32),
+            pltpu.SemaphoreType.DMA((8, max(n1, n2))),
+        ],
+        compiler_params=pltpu.CompilerParams(collective_id=collective_id, has_side_effects=True),
+    )(kv, rk, own_kv, own_rk, gk, gv)
 
 
 def shards(
@@ -31,10 +152,15 @@
     source = lax.axis_index("trial") * tensors + lax.axis_index("tensor")
     picks = lax.dynamic_slice_in_dim(trial_row_index, source * select, select, 1).reshape(-1)
     onehot = (picks[:, None] == jnp.arange(pool_dev, dtype=jnp.int32)[None, :]).astype(jnp.bfloat16)
-    wide = jnp.dot(onehot, residual_rows, preferred_element_type=jnp.float32)
-    msq = jnp.mean(wide * wide, axis=1, keepdims=True)
-    chosen = (wide * lax.rsqrt(msq + norm_eps) * input_norm_weight[None, :]).astype(jnp.bfloat16)
-    chosen = chosen.reshape(trials, select, tensors, normed_input).transpose(0, 2, 1, 3)
+    wide = jnp.einsum(
+        "tsr,rkf->tksf",
+        onehot.reshape(trials, select, pool_dev),
+        residual_rows.reshape(pool_dev, tensors, normed_input),
+        preferred_element_type=jnp.float32,
+    )
+    msq = jnp.mean(wide * wide, axis=(1, 3), keepdims=True)
+    gain = input_norm_weight.reshape(1, tensors, 1, normed_input)
+    chosen = (wide * lax.rsqrt(msq + norm_eps) * gain).astype(jnp.bfloat16)
     arrived = lax.all_to_all(
         chosen.reshape(trials * tensors, select, normed_input),
         ("trial", "tensor"),
@@ -63,11 +189,22 @@
     down_weight = adapter_down_weight[0]
     keyval = jnp.dot(rows, keyvalue_weight, preferred_element_type=jnp.float32)
     ranks = jnp.dot(rows, down_weight, preferred_element_type=jnp.float32)
-    summed = lax.psum_scatter(
-        jnp.concatenate([keyval, ranks], axis=1), "tensor", scatter_dimension=0, tiled=True
-    )
-    frozen_output_local = summed[:, :kv_width]
-    local_rank_rows = summed[:, kv_width:]
+    block = tok_dev // tensors
+    mine = lax.axis_index("tensor") * block
+    quarter = dps // 2
+    width = kv_width // (dps * tensors)
+    grad_t = keyvalue_gradient[0].T.reshape(2, quarter, tensors, width, tok_dev // tensors)
+    grad_t = grad_t.transpose(0, 2, 1, 3, 4).reshape(2, keyvalue_half, tok_dev // tensors)
+    frozen_output_local, local_rank_rows, up_block = tensor_sum(
+        keyval.astype(jnp.bfloat16).reshape(tensors, block, kv_width),
+        ranks.reshape(tensors, block, ranks.shape[1]),
+        lax.dynamic_slice_in_dim(keyval, mine, block, 0),
+        lax.dynamic_slice_in_dim(ranks, mine, block, 0),
+        grad_t[0],
+        grad_t[1],
+        dps,
+        0,
+    )
     adapter_key = jnp.dot(
         local_rank_rows[:, :rank_index], up_weight[:, :keyvalue_half], precision=highest_precision
     )
@@ -80,23 +217,9 @@
 
     grad_a = lax.psum_scatter(grad_a_term, "dp", scatter_dimension=0, tiled=True)
 
-    key_down_gradient = jnp.dot(
-        local_rank_rows[:, :rank_index].T, grad_in[:, :keyvalue_half], precision=highest_precision
-    )
-    value_down_gradient = jnp.dot(
-        local_rank_rows[:, rank_index:].T, grad_in[:, keyvalue_half:], precision=highest_precision
-    )
-    up_gradient_term = adapter_scale * jnp.concatenate(
-        [key_down_gradient, value_down_gradient], axis=1
-    )
-    width = up_gradient_term.shape[1] // (dps * tensors)
-    up_gradient_term = (
-        up_gradient_term.reshape(rank_index, dps, tensors, width)
-        .transpose(0, 2, 1, 3)
-        .reshape(rank_index, dps * tensors * width)
-    )
-    grad_b = lax.psum_scatter(up_gradient_term, "tensor", scatter_dimension=1, tiled=True)
-    grad_b = lax.psum_scatter(grad_b, "dp", scatter_dimension=1, tiled=True)
+    grad_b = adapter_scale * jnp.where(
+        lax.axis_index("dp") < quarter, up_block[:, :rank_index], up_block[:, rank_index:]
+    ).T
     return (keyvalue_output[None], grad_a[None], grad_b[None])
 
 

time: 230 us -> 127 us (0.55); the launches traced: 225 us -> 126 us
  waiting for transfers between devices: 129 us -> 10.8 us
  Pallas kernels: 0 us -> 49 us
  blocking collectives: 43.3 us -> 16 us
  starting transfers between devices: 0.16 us -> 8.63 us
  local copies, waits for them, and re-layouts: 14.6 us -> 6.82 us
    reduce_scatter x2 -> x0, waiting for transfers between devices: 63.3 us -> none  [the longest x1 49.4 us: shards(): lax.psum_scatter(jnp.concatenate([keyval, ranks], axis=1), 'tensor', scat...]
    pallas_call x0 -> x1, Pallas kernels: none -> 49 us  [tensor_sum(): pl.pallas_call(functools.partial(_tensor_sum_kernel, n1, n2), out_shape=(...]
    reduce_scatter x1, waiting for transfers between devices: 39.4 us -> 0.01 us  [shards(): lax.psum_scatter(grad_a_term, 'dp', scatter_dimension=0, tiled=True)]
    all_to_all x1 -> x0, blocking collectives: 37.6 us -> none  [shards(): lax.all_to_all(chosen.reshape(trials * tensors, select, normed_input), ('...]
    unnamed x5 -> x1, waiting for transfers between devices: 26 us -> 0.02 us
    all_to_all x0 -> x1, waiting for transfers between devices: none -> 10.8 us  [shards(): lax.all_to_all(chosen.reshape(trials * tensors, select, normed_input), ('...]
    all_gather x1, blocking collectives: 5.69 us -> 16 us  [shards(): every_rank = lax.all_gather(rank_gradient, 'tensor', axis=0, tiled=True)]
    all_to_all x0 -> x1, starting transfers between devices: none -> 8.59 us  [shards(): lax.all_to_all(chosen.reshape(trials * tensors, select, normed_input), ('...]
  transfers between devices with their start and end apart: 4 -> 2, of which waited for: 4 -> 1; matrix products, arithmetic and copies ran while one was open for 5% -> 15% of each run, Pallas kernels for 0% -> 39%
where the time goes in v7:
time: 127 us; the launch traced here: 126 us
  Pallas kernels  49 us (39%)
  matrix products  16.8 us (13%)
  blocking collectives  16 us (13%)
  between operations  14.2 us (11%)
  waiting for transfers between devices  10.8 us (9%)
  starting transfers between devices  8.63 us (7%)
  local copies, waits for them, and re-layouts  6.82 us (5%)
  other arithmetic  4.15 us (3%)
    pallas_call x1, Pallas kernels, tensor_sum(): pl.pallas_call(functools.partial(_tensor_sum_kernel, n1, n2), out_shape=(...  49 us
    all_gather x1, blocking collectives, shards(): every_rank = lax.all_gather(rank_gradient, 'tensor', axis=0, tiled=True)  16 us
    all_to_all x1, waiting for transfers between devices, shards(): lax.all_to_all(chosen.reshape(trials * tensors, select, normed_input), ('...  10.8 us
    dot_general x1, matrix products, shards(): keyval = jnp.dot(rows, keyvalue_weight, preferred_element_type=jnp.float32)  9.22 us
    all_to_all x1, starting transfers between devices, shards(): lax.all_to_all(chosen.reshape(trials * tensors, select, normed_input), ('...  8.59 us
  transfers between devices with their start and end apart: 2, of which 1 were waited for; matrix products, arithmetic and copies ran while one was open for 15% of the time, Pallas kernels for 39%

profile of v7, /device:TPU:1, one launch (start us, length us, event | category | flops | bytes accessed | tf_op | source)
XLA Modules:
  0.0 126.4 jit_solution(12114474177252062506)
XLA Ops:
  7.2 0.8 mul.59
  8.0 0.8 constant_dynamic-slice_fusion.2
  8.8 2.4 %multiply_reduce_fusion = (f32[8,16]{1,0:T(8,128)S(1)}, f32[8,16,4,2048]{3,1,2,0:T(8,128)S(1)}) fusion(bf16[16,4,8,2048]{3,2,1,0:T(8,128)(2,1)} %bitcast.54, s32[8,16]{1,0:T(8,128)S(1)} %constant_dynamic-slice_fusion.2), kind=kOutput, calls=%fused_computation.1 | convolution fusion | flops 270548864 | bytes 6292480 | tf_op jit(solution)/shard_map/tsr,rkf->tksf/dot_general | solution.py:155
  11.2 2.0 %multiply_convert_fusion = bf16[8,16,4,2048]{3,1,2,0:T(8,128)(2,1)} fusion(f32[8,16,4,2048]{3,1,2,0:T(8,128)S(1)} %get-tuple-element.18, f32[4,2048]{1,0:T(4,128)S(1)} %mul.59, f32[8,16]{1,0:T(8,128)S(1)} %add_rsqrt_fusion), kind=kLoop, calls=%fused_computation | loop fusion | flops 3145728 | bytes 6324736 | tf_op jit(solution)/shard_map/convert_element_type | solution.py:163
  13.2 8.6 %all-to-all-start = ((bf16[32,16,2048]{2,1,0:T(8,128)(2,1)}), bf16[32,16,2048]{2,1,0:T(8,128)(2,1)S(1)}, u32[]{:S(2)}, u32[]{:S(2)}) async-start(bf16[32,16,2048]{2,1,0:T(8,128)(2,1)} %bitcast.53), calls=%async_computation | async-start | bytes 4194304 | tf_op jit(solution)/shard_map/all_to_all | solution.py:164
  21.9 1.3 %copy.14 = bf16[1,128,2048]{1,2,0:T(8,128)(2,1)S(1)} copy(bf16[1,128,2048]{2,1,0:T(8,128)(2,1)} %param.13) | data formatting | bytes 1048576 | tf_op args[6]
  23.3 0.7 copy.16
  24.0 0.7 copy.15
  24.7 0.3 fusion.8
  25.0 0.3 fusion.6
  25.3 0.1 fusion.16
  25.4 16.0 %all_gather.3 = bf16[512,128]{1,0:T(8,128)(2,1)S(1)} all-gather(bf16[128,128]{1,0:T(8,128)(2,1)S(1)} %fusion.16), channel_id=1, replica_groups=mesh['trial'=8,'dp'=8,'tensor'=4] {'tensor'}, dimensions={0}, use_global_device_ids=true | all-gather | bytes 163840 | tf_op jit(solution)/shard_map/all_gather | solution.py:184
  41.4 10.8 %all-to-all-done = bf16[32,16,2048]{2,1,0:T(8,128)(2,1)S(1)} async-done(((bf16[32,16,2048]{2,1,0:T(8,128)(2,1)}), bf16[32,16,2048]{2,1,0:T(8,128)(2,1)S(1)}, u32[]{:S(2)}, u32[]{:S(2)}) %all-to-all-start) | async-done | bytes 2097184 | tf_op jit(solution)/shard_map/all_to_all | solution.py:164
  52.1 0.7 fusion.4
  52.9 1.5 %fusion.24 = f32[128,2048]{1,0:T(8,128)} fusion(bf16[512,128]{1,0:T(8,128)(2,1)S(1)} %all_gather.3, bf16[512,2048]{1,0:T(8,128)(2,1)S(1)} %bitcast.51), kind=kOutput, calls=%fused_computation.34 | convolution fusion | flops 268435456 | bytes 3276800 | tf_op jit(solution)/shard_map/dot_general | solution.py:185
  54.3 0.6 constant_dynamic-slice_fusion.own_rk_ref
  55.0 9.2 %fusion.23 = (bf16[512,2048]{1,0:T(8,128)(2,1)}, f32[512,2048]{1,0:T(8,128)S(1)}) fusion(bf16[512,2048]{1,0:T(8,128)(2,1)S(1)} %bitcast.52, bf16[2048,2048]{1,0:T(8,128)(2,1)} %param.10), kind=kOutput, calls=%fused_computation.33 | convolution fusion | flops 4296015872 | bytes 16777216 | tf_op jit(solution)/shard_map/dot_general | solution.py:190
  64.2 1.0 constant_dynamic-slice_fusion.1.own_kv_ref
  65.2 49.0 %shard_map.94 = (f32[128,2048]{1,0:T(8,128)}, f32[128,128]{1,0:T(8,128)}, f32[64,128]{1,0:T(8,128)}) custom-call(bf16[4,128,2048]{2,1,0:T(8,128)(2,1)} %bitcast.55, f32[4,128,128]{2,1,0:T(8,128)} %bitcast.59, f32[128,2048]{1,0:T(8,128)} %constant_dynamic-slice_fusion.1.own_kv_ref, f32[128,128]{1,0:T(8,128)} %constant_dynamic-slice_fusion.own_rk_ref, ...), custom_call_target="tpu_custom_call" | custom-call | tf_op jit(solution)/shard_map/pallas_call | solution.py:109
  114.3 0.9 multiply_bitcast_fusion
  115.2 0.7 copy.17
  115.9 1.3 fusion.11
  117.2 1.2 fusion.14
  118.4 1.1 fusion.3
  (13 shorter events, 0.1 us)
Async XLA Ops:
  7.2 45.0 %copy-start = (bf16[1,2048,128]{2,1,0:T(8,128)(2,1)S(1)}, bf16[1,2048,128]{2,1,0:T(8,128)(2,1)}, u32[]{:S(2)}) copy-start(bf16[1,2048,128]{2,1,0:T(8,128)(2,1)} %param.11) | copy-start | bytes 1572868
  13.2 38.9 %all-to-all-start = ((bf16[32,16,2048]{2,1,0:T(8,128)(2,1)}), bf16[32,16,2048]{2,1,0:T(8,128)(2,1)S(1)}, u32[]{:S(2)}, u32[]{:S(2)}) async-start(bf16[32,16,2048]{2,1,0:T(8,128)(2,1)} %bitcast.53), calls=%async_computation | async-start | bytes 4194304 | tf_op jit(solution)/shard_map/all_to_all | solution.py:164
  21.8 2.9 %copy-start.3 = (bf16[1,64,2048]{2,1,0:T(8,128)(2,1)S(1)}, bf16[1,64,2048]{2,1,0:T(8,128)(2,1)}, u32[]{:S(2)}) copy-start(bf16[1,64,2048]{2,1,0:T(8,128)(2,1)} %param.12) | copy-start | bytes 786436
  21.8 97.7 %reduce-scatter.2.cloned.1.call-start = ((), (), s32[]{:S(2)}) async-start(), calls=%async_computation.2 | async-start | bytes 1179648 | tf_op jit(solution)/shard_map/reduce_scatter | solution.py:218
  52.8 1.5 %copy-start.1 = (f32[512,128]{1,0:T(8,128)}, f32[512,128]{1,0:T(8,128)S(1)}, u32[]{:S(2)}) copy-start(f32[512,128]{1,0:T(8,128)S(1)} %fusion.4) | copy-start | bytes 786436
  114.3 4.1 %copy-start.2 = (f32[128,2048]{1,0:T(8,128)S(1)}, f32[128,2048]{1,0:T(8,128)}, u32[]{:S(2)}) copy-start(f32[128,2048]{1,0:T(8,128)} %get-tuple-element.6) | copy-start | bytes 3145732
Sparse Core Ops, SparseCore 0:
  54.5 32.9 reduce-scatter.1

commit v8 on v7

--- a/solution.py
+++ b/solution.py
@@ -14,7 +14,7 @@
 
 
 def _tensor_sum_kernel(
-    n1, n2, kv_ref, rk_ref, own_kv_ref, own_rk_ref, gk_ref, gv_ref,
+    n1, n2, kv_ref, rk_ref, own_kv_ref, own_rk_ref, gk_ref, gv_ref, up_ref,
     kv_out, rk_out, b_out,
     recv_kv, recv_rk, terms, recv_b1, partial, recv_b2, sems,
 ):
@@ -75,7 +75,13 @@
         target = lax.rem(me1 + shift, n1)
         b1_copies.append(send(terms.at[target], recv_b1, 4, shift, first(target)))
 
-    kv_out[...] = own_kv_ref[...]
+    high = xa.astype(jnp.bfloat16)
+    low = (xa - high.astype(jnp.float32)).astype(jnp.bfloat16)
+    up = up_ref[...]
+    adapter = jnp.dot(high, up, preferred_element_type=jnp.float32) + jnp.dot(
+        low, up, preferred_element_type=jnp.float32
+    )
+    kv_out[...] = own_kv_ref[...] + adapter_scale * adapter
     for shift, copy in zip(range(1, n1), kv_copies):
         copy.wait_recv()
         kv_out[...] += recv_kv[shift].astype(jnp.float32)
@@ -99,7 +105,7 @@
         copy.wait_send()
 
 
-def tensor_sum(kv, rk, own_kv, own_rk, gk, gv, n2, collective_id):
+def tensor_sum(kv, rk, own_kv, own_rk, gk, gv, up, n2, collective_id):
     n1 = kv.shape[0]
     quarter = n2 // 2
     columns = gk.shape[0]
@@ -113,7 +119,7 @@
             jax.ShapeDtypeStruct(own_rk.shape, jnp.float32),
             jax.ShapeDtypeStruct((block, lanes), jnp.float32),
         ),
-        in_specs=[vmem] * 6,
+        in_specs=[vmem] * 7,
         out_specs=(vmem, vmem, vmem),
         scratch_shapes=[
             pltpu.VMEM(kv.shape, kv.dtype),
@@ -125,7 +131,7 @@
             pltpu.SemaphoreType.DMA((8, max(n1, n2))),
         ],
         compiler_params=pltpu.CompilerParams(collective_id=collective_id, has_side_effects=True),
-    )(kv, rk, own_kv, own_rk, gk, gv)
+    )(kv, rk, own_kv, own_rk, gk, gv, up)
 
 
 def shards(
@@ -161,14 +167,18 @@
     msq = jnp.mean(wide * wide, axis=(1, 3), keepdims=True)
     gain = input_norm_weight.reshape(1, tensors, 1, normed_input)
     chosen = (wide * lax.rsqrt(msq + norm_eps) * gain).astype(jnp.bfloat16)
-    arrived = lax.all_to_all(
-        chosen.reshape(trials * tensors, select, normed_input),
-        ("trial", "tensor"),
-        split_axis=0,
-        concat_axis=0,
-        tiled=True,
-    )
-    rows = arrived.reshape(tok_dev, normed_input)
+    half_in = normed_input // 2
+    chosen = chosen.reshape(trials * tensors, select, normed_input)
+    halves = [
+        lax.all_to_all(
+            chosen[:, :, h * half_in:(h + 1) * half_in],
+            ("trial", "tensor"),
+            split_axis=0,
+            concat_axis=0,
+            tiled=True,
+        ).reshape(tok_dev, half_in)
+        for h in range(2)
+    ]
 
     up_weight = adapter_up_weight[0].astype(jnp.float32)
     grad_in = keyvalue_gradient[0].astype(jnp.float32)
@@ -182,13 +192,29 @@
         adapter_scale * jnp.concatenate([key_gradient_full, value_gradient_full], axis=1)
     ).astype(jnp.bfloat16)
     every_rank = lax.all_gather(rank_gradient, "tensor", axis=0, tiled=True)
-    grad_a_term = lax.dot_general(
-        every_rank, rows, (((0,), (0,)), ((), ())), preferred_element_type=jnp.float32
+    grad_a_term = jnp.concatenate(
+        [
+            lax.dot_general(
+                every_rank, rows_h, (((0,), (0,)), ((), ())), preferred_element_type=jnp.float32
+            )
+            for rows_h in halves
+        ],
+        axis=1,
     )
 
     down_weight = adapter_down_weight[0]
-    keyval = jnp.dot(rows, keyvalue_weight, preferred_element_type=jnp.float32)
-    ranks = jnp.dot(rows, down_weight, preferred_element_type=jnp.float32)
+    keyval = None
+    ranks = None
+    for h, rows_h in enumerate(halves):
+        features = slice(h * half_in, (h + 1) * half_in)
+        kv_h = jnp.dot(rows_h, keyvalue_weight[features], preferred_element_type=jnp.float32)
+        rk_h = jnp.dot(rows_h, down_weight[features], preferred_element_type=jnp.float32)
+        keyval = kv_h if keyval is None else keyval + kv_h
+        ranks = rk_h if ranks is None else ranks + rk_h
+    up_bf = adapter_up_weight[0]
+    block_up = jnp.zeros((2 * rank_index, kv_width), up_bf.dtype)
+    block_up = block_up.at[:rank_index, :keyvalue_half].set(up_bf[:, :keyvalue_half])
+    block_up = block_up.at[rank_index:, keyvalue_half:].set(up_bf[:, keyvalue_half:])
     block = tok_dev // tensors
     mine = lax.axis_index("tensor") * block
     quarter = dps // 2
@@ -202,18 +228,11 @@
         lax.dynamic_slice_in_dim(ranks, mine, block, 0),
         grad_t[0],
         grad_t[1],
+        block_up,
         dps,
         0,
     )
-    adapter_key = jnp.dot(
-        local_rank_rows[:, :rank_index], up_weight[:, :keyvalue_half], precision=highest_precision
-    )
-    adapter_value = jnp.dot(
-        local_rank_rows[:, rank_index:], up_weight[:, keyvalue_half:], precision=highest_precision
-    )
-    keyvalue_output = frozen_output_local + adapter_scale * jnp.concatenate(
-        [adapter_key, adapter_value], axis=1
-    )
+    keyvalue_output = frozen_output_local
 
     grad_a = lax.psum_scatter(grad_a_term, "dp", scatter_dimension=0, tiled=True)
 

time: 127 us -> 134 us (1.055)
  waiting for transfers between devices: 10.8 us -> 24.7 us
  blocking collectives: 16 us -> 6.02 us
  starting transfers between devices: 8.63 us -> 13.1 us
  local copies, waits for them, and re-layouts: 6.82 us -> 9.05 us
  matrix products: 16.8 us -> 14.9 us
  other arithmetic: 4.15 us -> 2.61 us
    all_to_all x1 -> x2, waiting for transfers between devices: 10.8 us -> 24.7 us  [shards(): lax.all_to_all(chosen[:, :, h * half_in:(h + 1) * half_in], ('trial', 'te...]
    all_gather x1, blocking collectives: 16 us -> 6.02 us  [shards(): every_rank = lax.all_gather(rank_gradient, 'tensor', axis=0, tiled=True)]
    all_to_all x1 -> x2, starting transfers between devices: 8.59 us -> 13.1 us  [shards(): lax.all_to_all(chosen[:, :, h * half_in:(h + 1) * half_in], ('trial', 'te...]
    dot_general x5 -> x6, matrix products: 13.8 us -> 12.1 us  [the longest x2 8.39 us: shards(): jnp.dot(rows_h, keyvalue_weight[features], preferred_element_type=jnp.flo...]
    slice x0 -> x2, local copies, waits for them, and re-layouts: none -> 1.58 us  [the longest x1 1.57 us: shards(): chosen[:, :, h * half_in:(h + 1) * half_in]]
    convert_element_type x1, other arithmetic: 2 us -> 0.64 us  [shards(): chosen = (wide * lax.rsqrt(msq + norm_eps) * gain).astype(jnp.bfloat16)]
    unnamed x10 -> x17, local copies, waits for them, and re-layouts: 2.07 us -> 3.31 us
  transfers between devices with their start and end apart: 2 -> 3, of which waited for: 1 -> 2; matrix products, arithmetic and copies ran while one was open for 15% -> 13% of each run, Pallas kernels for 39% -> 37%
where the time goes in v8:
time: 134 us; the launch traced here: 133 us
  Pallas kernels  48.7 us (36%)
  waiting for transfers between devices  24.7 us (18%)
  matrix products  14.9 us (11%)
  between operations  14.3 us (11%)
  starting transfers between devices  13.1 us (10%)
  local copies, waits for them, and re-layouts  9.05 us (7%)
  blocking collectives  6.02 us (4%)
  other arithmetic  2.61 us (2%)
    pallas_call x1, Pallas kernels, tensor_sum(): pl.pallas_call(functools.partial(_tensor_sum_kernel, n1, n2), out_shape=(...  48.7 us
    all_to_all x2, waiting for transfers between devices, shards(): lax.all_to_all(chosen[:, :, h * half_in:(h + 1) * half_in], ('trial', 'te...  24.7 us
    all_to_all x2, starting transfers between devices, shards(): lax.all_to_all(chosen[:, :, h * half_in:(h + 1) * half_in], ('trial', 'te...  13.1 us
    dot_general x2, matrix products, shards(): jnp.dot(rows_h, keyvalue_weight[features], preferred_element_type=jnp.flo...  8.39 us
    all_gather x1, blocking collectives, shards(): every_rank = lax.all_gather(rank_gradient, 'tensor', axis=0, tiled=True)  6.02 us
    unnamed x17, local copies, waits for them, and re-layouts  3.31 us
    dot_general x2, matrix products, shards(): jnp.dot(rows_h, down_weight[features], preferred_element_type=jnp.float32)  3.12 us
  transfers between devices with their start and end apart: 3, of which 2 were waited for; matrix products, arithmetic and copies ran while one was open for 13% of the time, Pallas kernels for 37%

profile of v8, /device:TPU:1, one launch (start us, length us, event | category | flops | bytes accessed | tf_op | source)
XLA Modules:
  0.0 133.4 jit_solution(12743602807012963290)
XLA Ops:
  7.2 0.8 mul.53
  8.0 2.4 %multiply_reduce_fusion = (f32[8,16]{1,0:T(8,128)S(1)}, f32[8,16,4,2048]{3,1,2,0:T(8,128)S(1)}) fusion(bf16[16,4,8,2048]{3,2,1,0:T(8,128)(2,1)} %bitcast.63, s32[8,16]{1,0:T(8,128)S(1)} %constant_dynamic-slice_fusion.2), kind=kOutput, calls=%fused_computation.5 | convolution fusion | flops 270548864 | bytes 6292480 | tf_op jit(solution)/shard_map/tsr,rkf->tksf/dot_general | solution.py:161
  10.5 0.6 multiply_convert_fusion
  11.2 1.6 %fusion.24 = (bf16[32,16,1024]{2,1,0:T(8,128)(2,1)}, bf16[32,16,1024]{2,1,0:T(8,128)(2,1)}) fusion(bf16[32,16,2048]{2,1,0:T(8,128)(2,1)S(1)} %bitcast.62), kind=kLoop, calls=%fused_computation.34 | loop fusion | bytes 4194304 | tf_op jit(solution)/shard_map/slice | solution.py:174
  12.7 8.6 %all-to-all-start = ((bf16[32,16,1024]{2,1,0:T(8,128)(2,1)}), bf16[32,16,1024]{2,1,0:T(8,128)(2,1)S(1)}, u32[]{:S(2)}, u32[]{:S(2)}) async-start(bf16[32,16,1024]{2,1,0:T(8,128)(2,1)} %get-tuple-element.37), calls=%async_computation | async-start | bytes 2097152 | tf_op jit(solution)/shard_map/all_to_all | solution.py:173
  21.9 16.9 %all-to-all-done = bf16[32,16,1024]{2,1,0:T(8,128)(2,1)S(1)} async-done(((bf16[32,16,1024]{2,1,0:T(8,128)(2,1)}), bf16[32,16,1024]{2,1,0:T(8,128)(2,1)S(1)}, u32[]{:S(2)}, u32[]{:S(2)}) %all-to-all-start) | async-done | bytes 1048608 | tf_op jit(solution)/shard_map/all_to_all | solution.py:173
  38.7 4.5 %all-to-all-start.1 = ((bf16[32,16,1024]{2,1,0:T(8,128)(2,1)}), bf16[32,16,1024]{2,1,0:T(8,128)(2,1)S(1)}, u32[]{:S(2)}, u32[]{:S(2)}) async-start(bf16[32,16,1024]{2,1,0:T(8,128)(2,1)} %get-tuple-element.38), calls=%async_computation.1 | async-start | bytes 2097152 | tf_op jit(solution)/shard_map/all_to_all | solution.py:173
  43.5 0.7 copy.16
  44.2 0.7 copy.15
  45.0 6.0 %all_gather.3 = bf16[512,128]{0,1:T(8,128)(2,1)S(1)} all-gather(bf16[128,128]{0,1:T(8,128)(2,1)S(1)} %fusion.19), channel_id=1, replica_groups=mesh['trial'=8,'dp'=8,'tensor'=4] {'tensor'}, dimensions={0}, use_global_device_ids=true | all-gather | bytes 163840 | tf_op jit(solution)/shard_map/all_gather | solution.py:194
  51.1 1.6 %fusion.14 = f32[512,128]{1,0:T(8,128)S(1)} fusion(bf16[512,1024]{1,0:T(8,128)(2,1)S(1)} %bitcast.59, bf16[1,2048,128]{2,1,0:T(8,128)(2,1)} %param.15), kind=kOutput, calls=%fused_computation.17 | convolution fusion | flops 134217728 | bytes 1572864 | tf_op jit(solution)/shard_map/dot_general | solution.py:211
  52.7 0.3 fusion.27
  53.0 7.8 %all-to-all-done.1 = bf16[32,16,1024]{2,1,0:T(8,128)(2,1)S(1)} async-done(((bf16[32,16,1024]{2,1,0:T(8,128)(2,1)}), bf16[32,16,1024]{2,1,0:T(8,128)(2,1)S(1)}, u32[]{:S(2)}, u32[]{:S(2)}) %all-to-all-start.1) | async-done | bytes 1048608 | tf_op jit(solution)/shard_map/all_to_all | solution.py:173
  60.8 0.3 fusion.28
  61.1 1.0 pad_maximum_fusion
  62.2 1.5 %convolution_add_fusion = f32[512,128]{1,0:T(8,128)S(1)} fusion(f32[512,128]{1,0:T(8,128)S(1)} %fusion.14, bf16[512,1024]{1,0:T(8,128)(2,1)S(1)} %bitcast.57, bf16[1,2048,128]{2,1,0:T(8,128)(2,1)} %param.15), kind=kOutput, calls=%fused_computation.10 | convolution fusion | flops 134283264 | bytes 1835008 | tf_op jit(solution)/shard_map/dot_general | solution.py:211
  63.7 0.7 constant_dynamic-slice_fusion.own_rk_ref
  64.4 4.7 %fusion = f32[512,2048]{1,0:T(8,128)S(1)} fusion(bf16[512,1024]{1,0:T(8,128)(2,1)S(1)} %bitcast.58, bf16[2048,2048]{1,0:T(8,128)(2,1)} %param.14), kind=kOutput, calls=%fused_computation | convolution fusion | flops 2147483648 | bytes 9437184 | tf_op jit(solution)/shard_map/dot_general | solution.py:210
  69.2 3.7 %fusion.26 = (bf16[512,2048]{1,0:T(8,128)(2,1)}, f32[512,2048]{1,0:T(8,128)S(1)}) fusion(f32[512,2048]{1,0:T(8,128)S(1)} %fusion, bf16[512,1024]{1,0:T(8,128)(2,1)S(1)} %bitcast.61, bf16[2048,2048]{1,0:T(8,128)(2,1)S(1)} %bitcast.77), kind=kOutput, calls=%fused_computation.36 | convolution fusion | flops 2149580800 | bytes 15728640 | tf_op jit(solution)/shard_map/dot_general | solution.py:210
  72.9 1.0 constant_dynamic-slice_fusion.1.own_kv_ref
  73.9 48.7 %shard_map.94 = (f32[128,2048]{1,0:T(8,128)}, f32[128,128]{1,0:T(8,128)}, f32[64,128]{1,0:T(8,128)}) custom-call(bf16[4,128,2048]{2,1,0:T(8,128)(2,1)} %bitcast.64, f32[4,128,128]{2,1,0:T(8,128)} %bitcast.68, f32[128,2048]{1,0:T(8,128)} %constant_dynamic-slice_fusion.1.own_kv_ref, f32[128,128]{1,0:T(8,128)} %constant_dynamic-slice_fusion.own_rk_ref, ...), custom_call_target="tpu_custom_call" | custom-call | tf_op jit(solution)/shard_map/pallas_call | solution.py:115
  122.6 0.9 multiply_bitcast_fusion
  123.5 0.7 copy.17
  124.2 2.3 %copy.28 = f32[1,128,2048]{2,1,0:T(8,128)} copy(f32[1,128,2048]{2,1,0:T(8,128)} %bitcast.71) | data formatting | bytes 2097152
  (28 shorter events, 0.9 us)
Async XLA Ops:
  7.2 0.8 copy-start
  11.1 10.2 %copy-start.3 = (bf16[1,128,2048]{2,1,0:T(8,128)(2,1)S(1)}, bf16[1,128,2048]{2,1,0:T(8,128)(2,1)}, u32[]{:S(2)}) copy-start(bf16[1,128,2048]{2,1,0:T(8,128)(2,1)} %param.17) | copy-start | bytes 1572868
  11.2 10.5 %copy-start.4 = (bf16[1,64,2048]{2,1,0:T(8,128)(2,1)S(1)}, bf16[1,64,2048]{2,1,0:T(8,128)(2,1)}, u32[]{:S(2)}) copy-start(bf16[1,64,2048]{2,1,0:T(8,128)(2,1)} %param.16) | copy-start | bytes 786436
  12.7 26.0 %all-to-all-start = ((bf16[32,16,1024]{2,1,0:T(8,128)(2,1)}), bf16[32,16,1024]{2,1,0:T(8,128)(2,1)S(1)}, u32[]{:S(2)}, u32[]{:S(2)}) async-start(bf16[32,16,1024]{2,1,0:T(8,128)(2,1)} %get-tuple-element.37), calls=%async_computation | async-start | bytes 2097152 | tf_op jit(solution)/shard_map/all_to_all | solution.py:173
  38.7 22.0 %all-to-all-start.1 = ((bf16[32,16,1024]{2,1,0:T(8,128)(2,1)}), bf16[32,16,1024]{2,1,0:T(8,128)(2,1)S(1)}, u32[]{:S(2)}, u32[]{:S(2)}) async-start(bf16[32,16,1024]{2,1,0:T(8,128)(2,1)} %get-tuple-element.38), calls=%async_computation.1 | async-start | bytes 2097152 | tf_op jit(solution)/shard_map/all_to_all | solution.py:173
  43.3 81.0 %reduce-scatter.2.cloned.1.call-start = ((), (), s32[]{:S(2)}) async-start(), calls=%async_computation.3 | async-start | bytes 1179648 | tf_op jit(solution)/shard_map/reduce_scatter | solution.py:237
  51.1 12.6 %copy-start.1 = (bf16[128,2048]{1,0:T(8,128)(2,1)}, bf16[128,2048]{1,0:T(8,128)(2,1)S(1)}, u32[]{:S(2)}) copy-start(bf16[128,2048]{1,0:T(8,128)(2,1)S(1)} %slice_dynamic-update-slice_fusion.up_ref) | copy-start | bytes 1572868
  62.1 7.0 %slice-start = ((s8[8388608]{0:T(1024)(128)(4,1)}), s8[4194304]{0:T(1024)(128)(4,1)S(1)}, s32[]{:S(2)}) async-start(s8[8388608]{0:T(1024)(128)(4,1)} %bitcast.76), calls=%async_computation.4 | async-start | bytes 8388608
  63.7 5.4 %copy-start.2 = (f32[512,128]{1,0:T(8,128)}, f32[512,128]{1,0:T(8,128)S(1)}, u32[]{:S(2)}) copy-start(f32[512,128]{1,0:T(8,128)S(1)} %convolution_add_fusion) | copy-start | bytes 786436
  64.4 4.7 %slice-start.1 = ((s8[8388608]{0:T(1024)(128)(4,1)}), s8[4194304]{0:T(1024)(128)(4,1)S(1)}, s32[]{:S(2)}) async-start(s8[8388608]{0:T(1024)(128)(4,1)} %bitcast.76), calls=%async_computation.5 | async-start | bytes 8388608
Sparse Core Ops, SparseCore 0:
  62.3 35.9 reduce-scatter.1

commit v9 on v7

--- a/solution.py
+++ b/solution.py
@@ -16,7 +16,7 @@
 def _tensor_sum_kernel(
     n1, n2, kv_ref, rk_ref, own_kv_ref, own_rk_ref, gk_ref, gv_ref,
     kv_out, rk_out, b_out,
-    recv_kv, recv_rk, terms, recv_b1, partial, recv_b2, sems,
+    recv_kv, recv_rk, terms, recv_b1, partial, recv_b2, forward, sems,
 ):
     me1 = lax.axis_index("tensor")
     me2 = lax.axis_index("dp")
@@ -43,13 +43,15 @@
         copy.start()
         return copy
 
+    partner = me1 + 1 - 2 * lax.rem(me1, 2)
+    across = lax.rem(me1 + 2, n1)
+    diagonal = across + 1 - 2 * lax.rem(across, 2)
     rk_copies, kv_copies = [], []
     for shift in range(1, n1):
         target = lax.rem(me1 + shift, n1)
         rk_copies.append(send(rk_ref.at[target], recv_rk, 2, shift, first(target)))
-    for shift in range(1, n1):
-        target = lax.rem(me1 + shift, n1)
-        kv_copies.append(send(kv_ref.at[target], recv_kv, 0, shift, first(target)))
+    for slot, block in enumerate((partner, diagonal)):
+        kv_copies.append(send(kv_ref.at[block], recv_kv, 0, slot, first(partner)))
 
     rk_out[...] = own_rk_ref[...]
     for shift, copy in zip(range(1, n1), rk_copies):
@@ -75,10 +77,13 @@
         target = lax.rem(me1 + shift, n1)
         b1_copies.append(send(terms.at[target], recv_b1, 4, shift, first(target)))
 
-    kv_out[...] = own_kv_ref[...]
-    for shift, copy in zip(range(1, n1), kv_copies):
-        copy.wait_recv()
-        kv_out[...] += recv_kv[shift].astype(jnp.float32)
+    kv_copies[1].wait_recv()
+    forward[...] = (
+        kv_ref[across].astype(jnp.float32) + recv_kv[1].astype(jnp.float32)
+    ).astype(forward.dtype)
+    kv_copies.append(send(forward, recv_kv, 0, 2, first(across)))
+    kv_copies[0].wait_recv()
+    kv_out[...] = own_kv_ref[...] + recv_kv[0].astype(jnp.float32)
 
     summed = terms[me1]
     for shift, copy in zip(range(1, n1), b1_copies):
@@ -90,6 +95,8 @@
     for shift in range(1, n2):
         target = lax.rem(me2 + shift, n2)
         b2_copies.append(send(partial.at[lax.rem(target, quarter)], recv_b2, 6, shift, second(target)))
+    kv_copies[2].wait_recv()
+    kv_out[...] += recv_kv[2].astype(jnp.float32)
     b_out[...] = partial[lax.rem(me2, quarter)]
     for shift, copy in zip(range(1, n2), b2_copies):
         copy.wait_recv()
@@ -122,6 +129,7 @@
             pltpu.VMEM((n1, quarter * block, lanes), jnp.float32),
             pltpu.VMEM((quarter, block, lanes), jnp.float32),
             pltpu.VMEM((n2, block, lanes), jnp.float32),
+            pltpu.VMEM(kv.shape[1:], kv.dtype),
             pltpu.SemaphoreType.DMA((8, max(n1, n2))),
         ],
         compiler_params=pltpu.CompilerParams(collective_id=collective_id, has_side_effects=True),

time: 127 us -> 112 us (0.88)
  Pallas kernels: 49 us -> 34.3 us
    pallas_call x1, Pallas kernels: 49 us -> 34.3 us  [tensor_sum(): pl.pallas_call(functools.partial(_tensor_sum_kernel, n1, n2), out_shape=(...]
  transfers between devices with their start and end apart: 2 -> 2, of which waited for: 1 -> 1; matrix products, arithmetic and copies ran while one was open for 15% -> 17% of each run, Pallas kernels for 39% -> 31%
where the time goes in v9:
time: 112 us
  Pallas kernels  34.3 us (31%)
  matrix products  16.8 us (15%)
  blocking collectives  16 us (14%)
  between operations  14.2 us (13%)
  waiting for transfers between devices  10.8 us (10%)
  starting transfers between devices  8.63 us (8%)
  local copies, waits for them, and re-layouts  6.82 us (6%)
  other arithmetic  4.15 us (4%)
    pallas_call x1, Pallas kernels, tensor_sum(): pl.pallas_call(functools.partial(_tensor_sum_kernel, n1, n2), out_shape=(...  34.3 us
    all_gather x1, blocking collectives, shards(): every_rank = lax.all_gather(rank_gradient, 'tensor', axis=0, tiled=True)  16 us
    all_to_all x1, waiting for transfers between devices, shards(): lax.all_to_all(chosen.reshape(trials * tensors, select, normed_input), ('...  10.8 us
    dot_general x1, matrix products, shards(): keyval = jnp.dot(rows, keyvalue_weight, preferred_element_type=jnp.float32)  9.22 us
    all_to_all x1, starting transfers between devices, shards(): lax.all_to_all(chosen.reshape(trials * tensors, select, normed_input), ('...  8.59 us
    dot_general x1, matrix products, shards(): jnp.einsum('tsr,rkf->tksf', onehot.reshape(trials, select, pool_dev), res...  2.42 us
  transfers between devices with their start and end apart: 2, of which 1 were waited for; matrix products, arithmetic and copies ran while one was open for 17% of the time, Pallas kernels for 31%

profile of v9, /device:TPU:1, one launch (start us, length us, event | category | flops | bytes accessed | tf_op | source)
XLA Modules:
  0.0 111.7 jit_solution(5461655253966571912)
XLA Ops:
  7.2 0.8 mul.59
  8.0 0.8 constant_dynamic-slice_fusion.2
  8.8 2.4 %multiply_reduce_fusion = (f32[8,16]{1,0:T(8,128)S(1)}, f32[8,16,4,2048]{3,1,2,0:T(8,128)S(1)}) fusion(bf16[16,4,8,2048]{3,2,1,0:T(8,128)(2,1)} %bitcast.54, s32[8,16]{1,0:T(8,128)S(1)} %constant_dynamic-slice_fusion.2), kind=kOutput, calls=%fused_computation.1 | convolution fusion | flops 270548864 | bytes 6292480 | tf_op jit(solution)/shard_map/tsr,rkf->tksf/dot_general | solution.py:163
  11.2 2.0 %multiply_convert_fusion = bf16[8,16,4,2048]{3,1,2,0:T(8,128)(2,1)} fusion(f32[8,16,4,2048]{3,1,2,0:T(8,128)S(1)} %get-tuple-element.18, f32[4,2048]{1,0:T(4,128)S(1)} %mul.59, f32[8,16]{1,0:T(8,128)S(1)} %add_rsqrt_fusion), kind=kLoop, calls=%fused_computation | loop fusion | flops 3145728 | bytes 6324736 | tf_op jit(solution)/shard_map/convert_element_type | solution.py:171
  13.2 8.6 %all-to-all-start = ((bf16[32,16,2048]{2,1,0:T(8,128)(2,1)}), bf16[32,16,2048]{2,1,0:T(8,128)(2,1)S(1)}, u32[]{:S(2)}, u32[]{:S(2)}) async-start(bf16[32,16,2048]{2,1,0:T(8,128)(2,1)} %bitcast.53), calls=%async_computation | async-start | bytes 4194304 | tf_op jit(solution)/shard_map/all_to_all | solution.py:172
  21.9 1.3 %copy.14 = bf16[1,128,2048]{1,2,0:T(8,128)(2,1)S(1)} copy(bf16[1,128,2048]{2,1,0:T(8,128)(2,1)} %param.13) | data formatting | bytes 1048576 | tf_op args[6]
  23.3 0.7 copy.16
  24.0 0.7 copy.15
  24.7 0.3 fusion.8
  25.0 0.3 fusion.6
  25.3 0.1 fusion.16
  25.4 16.0 %all_gather.3 = bf16[512,128]{1,0:T(8,128)(2,1)S(1)} all-gather(bf16[128,128]{1,0:T(8,128)(2,1)S(1)} %fusion.16), channel_id=1, replica_groups=mesh['trial'=8,'dp'=8,'tensor'=4] {'tensor'}, dimensions={0}, use_global_device_ids=true | all-gather | bytes 163840 | tf_op jit(solution)/shard_map/all_gather | solution.py:192
  41.4 10.8 %all-to-all-done = bf16[32,16,2048]{2,1,0:T(8,128)(2,1)S(1)} async-done(((bf16[32,16,2048]{2,1,0:T(8,128)(2,1)}), bf16[32,16,2048]{2,1,0:T(8,128)(2,1)S(1)}, u32[]{:S(2)}, u32[]{:S(2)}) %all-to-all-start) | async-done | bytes 2097184 | tf_op jit(solution)/shard_map/all_to_all | solution.py:172
  52.1 0.7 fusion.4
  52.9 1.5 %fusion.24 = f32[128,2048]{1,0:T(8,128)} fusion(bf16[512,128]{1,0:T(8,128)(2,1)S(1)} %all_gather.3, bf16[512,2048]{1,0:T(8,128)(2,1)S(1)} %bitcast.51), kind=kOutput, calls=%fused_computation.34 | convolution fusion | flops 268435456 | bytes 3276800 | tf_op jit(solution)/shard_map/dot_general | solution.py:193
  54.3 0.6 constant_dynamic-slice_fusion.own_rk_ref
  55.0 9.2 %fusion.23 = (bf16[512,2048]{1,0:T(8,128)(2,1)}, f32[512,2048]{1,0:T(8,128)S(1)}) fusion(bf16[512,2048]{1,0:T(8,128)(2,1)S(1)} %bitcast.52, bf16[2048,2048]{1,0:T(8,128)(2,1)} %param.10), kind=kOutput, calls=%fused_computation.33 | convolution fusion | flops 4296015872 | bytes 16777216 | tf_op jit(solution)/shard_map/dot_general | solution.py:198
  64.2 1.0 constant_dynamic-slice_fusion.1.own_kv_ref
  65.2 34.3 %shard_map.94 = (f32[128,2048]{1,0:T(8,128)}, f32[128,128]{1,0:T(8,128)}, f32[64,128]{1,0:T(8,128)}) custom-call(bf16[4,128,2048]{2,1,0:T(8,128)(2,1)} %bitcast.55, f32[4,128,128]{2,1,0:T(8,128)} %bitcast.59, f32[128,2048]{1,0:T(8,128)} %constant_dynamic-slice_fusion.1.own_kv_ref, f32[128,128]{1,0:T(8,128)} %constant_dynamic-slice_fusion.own_rk_ref, ...), custom_call_target="tpu_custom_call" | custom-call | tf_op jit(solution)/shard_map/pallas_call | solution.py:116
  99.6 0.9 multiply_bitcast_fusion
  100.5 0.7 copy.17
  101.2 1.3 %fusion.11 = f32[128,1024]{1,0:T(8,128)S(1)} fusion(bf16[64,2048]{1,0:T(8,128)(2,1)S(1)} %bitcast.64, f32[128,128]{1,0:T(8,128)} %get-tuple-element.7), kind=kOutput, calls=%fused_computation.15 | convolution fusion | flops 100663296 | bytes 720896 | tf_op jit(solution)/shard_map/dot_general | solution.py:219
  102.5 1.2 %fusion.14 = f32[128,1024]{1,0:T(8,128)S(1)} fusion(bf16[64,2048]{1,0:T(8,128)(2,1)S(1)} %bitcast.65, f32[128,128]{1,0:T(8,128)} %get-tuple-element.7), kind=kOutput, calls=%fused_computation.18 | convolution fusion | flops 100663296 | bytes 720896 | tf_op jit(solution)/shard_map/dot_general | solution.py:216
  103.7 1.1 %fusion.3 = f32[1,128,2048]{2,1,0:T(8,128)} fusion(f32[128,2048]{1,0:T(8,128)S(1)} %copy-done.2, f32[128,1024]{1,0:T(8,128)S(1)} %fusion.11, f32[128,1024]{1,0:T(8,128)S(1)} %fusion.14), kind=kLoop, calls=%fused_computation.7 | loop fusion | flops 786432 | bytes 3145728 | tf_op jit(solution)/shard_map/broadcast_in_dim | solution.py:231
  (13 shorter events, 0.1 us)
Async XLA Ops:
  7.2 45.0 %copy-start = (bf16[1,2048,128]{2,1,0:T(8,128)(2,1)S(1)}, bf16[1,2048,128]{2,1,0:T(8,128)(2,1)}, u32[]{:S(2)}) copy-start(bf16[1,2048,128]{2,1,0:T(8,128)(2,1)} %param.11) | copy-start | bytes 1572868
  13.2 38.9 %all-to-all-start = ((bf16[32,16,2048]{2,1,0:T(8,128)(2,1)}), bf16[32,16,2048]{2,1,0:T(8,128)(2,1)S(1)}, u32[]{:S(2)}, u32[]{:S(2)}) async-start(bf16[32,16,2048]{2,1,0:T(8,128)(2,1)} %bitcast.53), calls=%async_computation | async-start | bytes 4194304 | tf_op jit(solution)/shard_map/all_to_all | solution.py:172
  21.8 2.9 %copy-start.3 = (bf16[1,64,2048]{2,1,0:T(8,128)(2,1)S(1)}, bf16[1,64,2048]{2,1,0:T(8,128)(2,1)}, u32[]{:S(2)}) copy-start(bf16[1,64,2048]{2,1,0:T(8,128)(2,1)} %param.12) | copy-start | bytes 786436
  21.8 83.0 %reduce-scatter.2.cloned.1.call-start = ((), (), s32[]{:S(2)}) async-start(), calls=%async_computation.2 | async-start | bytes 1179648 | tf_op jit(solution)/shard_map/reduce_scatter | solution.py:226
  52.8 1.5 %copy-start.1 = (f32[512,128]{1,0:T(8,128)}, f32[512,128]{1,0:T(8,128)S(1)}, u32[]{:S(2)}) copy-start(f32[512,128]{1,0:T(8,128)S(1)} %fusion.4) | copy-start | bytes 786436
  99.6 4.1 %copy-start.2 = (f32[128,2048]{1,0:T(8,128)S(1)}, f32[128,2048]{1,0:T(8,128)}, u32[]{:S(2)}) copy-start(f32[128,2048]{1,0:T(8,128)} %get-tuple-element.6) | copy-start | bytes 3145732
Sparse Core Ops, SparseCore 0:
  54.5 33.7 reduce-scatter.1

commit v10 on v7

--- a/solution.py
+++ b/solution.py
@@ -16,7 +16,7 @@
 def _tensor_sum_kernel(
     n1, n2, kv_ref, rk_ref, own_kv_ref, own_rk_ref, gk_ref, gv_ref,
     kv_out, rk_out, b_out,
-    recv_kv, recv_rk, terms, recv_b1, partial, recv_b2, sems,
+    recv_kv, recv_rk, terms, recv_b1, partial, recv_b2, forward, sems, kv_sems,
 ):
     me1 = lax.axis_index("tensor")
     me2 = lax.axis_index("dp")
@@ -43,13 +43,31 @@
         copy.start()
         return copy
 
-    rk_copies, kv_copies = [], []
+    partner = me1 + 1 - 2 * lax.rem(me1, 2)
+    across = lax.rem(me1 + 2, n1)
+    diagonal = across + 1 - 2 * lax.rem(across, 2)
+    rk_copies = []
     for shift in range(1, n1):
         target = lax.rem(me1 + shift, n1)
         rk_copies.append(send(rk_ref.at[target], recv_rk, 2, shift, first(target)))
-    for shift in range(1, n1):
-        target = lax.rem(me1 + shift, n1)
-        kv_copies.append(send(kv_ref.at[target], recv_kv, 0, shift, first(target)))
+    pieces = kv_sems.shape[2]
+    step = kv_ref.shape[1] // pieces
+
+    def send_piece(src_ref, slot, piece, device):
+        rows = pl.ds(piece * step, step)
+        copy = pltpu.make_async_remote_copy(
+            src_ref=src_ref.at[rows],
+            dst_ref=recv_kv.at[slot, rows],
+            send_sem=kv_sems.at[0, slot, piece],
+            recv_sem=kv_sems.at[1, slot, piece],
+            device_id=device,
+            device_id_type=MESH,
+        )
+        copy.start()
+        return copy
+
+    diagonal_copies = [send_piece(kv_ref.at[diagonal], 1, p, first(partner)) for p in range(pieces)]
+    own_copies = [send_piece(kv_ref.at[partner], 0, p, first(partner)) for p in range(pieces)]
 
     rk_out[...] = own_rk_ref[...]
     for shift, copy in zip(range(1, n1), rk_copies):
@@ -75,10 +93,18 @@
         target = lax.rem(me1 + shift, n1)
         b1_copies.append(send(terms.at[target], recv_b1, 4, shift, first(target)))
 
-    kv_out[...] = own_kv_ref[...]
-    for shift, copy in zip(range(1, n1), kv_copies):
-        copy.wait_recv()
-        kv_out[...] += recv_kv[shift].astype(jnp.float32)
+    forward_copies = []
+    for p, copy in enumerate(diagonal_copies):
+        rows = pl.ds(p * step, step)
+        copy.wait_recv()
+        forward[rows, :] = (
+            kv_ref[across, rows, :].astype(jnp.float32) + recv_kv[1, rows, :].astype(jnp.float32)
+        ).astype(forward.dtype)
+        forward_copies.append(send_piece(forward, 2, p, first(across)))
+    for p, copy in enumerate(own_copies):
+        rows = pl.ds(p * step, step)
+        copy.wait_recv()
+        kv_out[rows, :] = own_kv_ref[rows, :] + recv_kv[0, rows, :].astype(jnp.float32)
 
     summed = terms[me1]
     for shift, copy in zip(range(1, n1), b1_copies):
@@ -90,12 +116,16 @@
     for shift in range(1, n2):
         target = lax.rem(me2 + shift, n2)
         b2_copies.append(send(partial.at[lax.rem(target, quarter)], recv_b2, 6, shift, second(target)))
+    for p, copy in enumerate(forward_copies):
+        rows = pl.ds(p * step, step)
+        copy.wait_recv()
+        kv_out[rows, :] += recv_kv[2, rows, :].astype(jnp.float32)
     b_out[...] = partial[lax.rem(me2, quarter)]
     for shift, copy in zip(range(1, n2), b2_copies):
         copy.wait_recv()
         b_out[...] += recv_b2[shift]
 
-    for copy in rk_copies + kv_copies + b1_copies + b2_copies:
+    for copy in rk_copies + diagonal_copies + own_copies + forward_copies + b1_copies + b2_copies:
         copy.wait_send()
 
 
@@ -122,7 +152,9 @@
             pltpu.VMEM((n1, quarter * block, lanes), jnp.float32),
             pltpu.VMEM((quarter, block, lanes), jnp.float32),
             pltpu.VMEM((n2, block, lanes), jnp.float32),
+            pltpu.VMEM(kv.shape[1:], kv.dtype),
             pltpu.SemaphoreType.DMA((8, max(n1, n2))),
+            pltpu.SemaphoreType.DMA((2, 3, 4)),
         ],
         compiler_params=pltpu.CompilerParams(collective_id=collective_id, has_side_effects=True),
     )(kv, rk, own_kv, own_rk, gk, gv)

time: 127 us -> 112 us (0.88)
  Pallas kernels: 49 us -> 34.5 us
    pallas_call x1, Pallas kernels: 49 us -> 34.5 us  [tensor_sum(): pl.pallas_call(functools.partial(_tensor_sum_kernel, n1, n2), out_shape=(...]
  transfers between devices with their start and end apart: 2 -> 2, of which waited for: 1 -> 1; matrix products, arithmetic and copies ran while one was open for 15% -> 17% of each run, Pallas kernels for 39% -> 31%
where the time goes in v10:
time: 112 us
  Pallas kernels  34.5 us (31%)
  matrix products  16.8 us (15%)
  blocking collectives  16 us (14%)
  between operations  14.2 us (13%)
  waiting for transfers between devices  10.8 us (10%)
  starting transfers between devices  8.63 us (8%)
  local copies, waits for them, and re-layouts  6.82 us (6%)
  other arithmetic  4.15 us (4%)
    pallas_call x1, Pallas kernels, tensor_sum(): pl.pallas_call(functools.partial(_tensor_sum_kernel, n1, n2), out_shape=(...  34.5 us
    all_gather x1, blocking collectives, shards(): every_rank = lax.all_gather(rank_gradient, 'tensor', axis=0, tiled=True)  16 us
    all_to_all x1, waiting for transfers between devices, shards(): lax.all_to_all(chosen.reshape(trials * tensors, select, normed_input), ('...  10.8 us
    dot_general x1, matrix products, shards(): keyval = jnp.dot(rows, keyvalue_weight, preferred_element_type=jnp.float32)  9.22 us
    all_to_all x1, starting transfers between devices, shards(): lax.all_to_all(chosen.reshape(trials * tensors, select, normed_input), ('...  8.59 us
    dot_general x1, matrix products, shards(): jnp.einsum('tsr,rkf->tksf', onehot.reshape(trials, select, pool_dev), res...  2.42 us
  transfers between devices with their start and end apart: 2, of which 1 were waited for; matrix products, arithmetic and copies ran while one was open for 17% of the time, Pallas kernels for 31%

profile of v10, /device:TPU:1, one launch (start us, length us, event | category | flops | bytes accessed | tf_op | source)
XLA Modules:
  0.0 111.8 jit_solution(6788851381258261815)
XLA Ops:
  7.2 0.8 mul.59
  8.0 0.8 constant_dynamic-slice_fusion.2
  8.8 2.4 %multiply_reduce_fusion = (f32[8,16]{1,0:T(8,128)S(1)}, f32[8,16,4,2048]{3,1,2,0:T(8,128)S(1)}) fusion(bf16[16,4,8,2048]{3,2,1,0:T(8,128)(2,1)} %bitcast.54, s32[8,16]{1,0:T(8,128)S(1)} %constant_dynamic-slice_fusion.2), kind=kOutput, calls=%fused_computation.1 | convolution fusion | flops 270548864 | bytes 6292480 | tf_op jit(solution)/shard_map/tsr,rkf->tksf/dot_general | solution.py:187
  11.2 2.0 %multiply_convert_fusion = bf16[8,16,4,2048]{3,1,2,0:T(8,128)(2,1)} fusion(f32[8,16,4,2048]{3,1,2,0:T(8,128)S(1)} %get-tuple-element.18, f32[4,2048]{1,0:T(4,128)S(1)} %mul.59, f32[8,16]{1,0:T(8,128)S(1)} %add_rsqrt_fusion), kind=kLoop, calls=%fused_computation | loop fusion | flops 3145728 | bytes 6324736 | tf_op jit(solution)/shard_map/convert_element_type | solution.py:195
  13.2 8.6 %all-to-all-start = ((bf16[32,16,2048]{2,1,0:T(8,128)(2,1)}), bf16[32,16,2048]{2,1,0:T(8,128)(2,1)S(1)}, u32[]{:S(2)}, u32[]{:S(2)}) async-start(bf16[32,16,2048]{2,1,0:T(8,128)(2,1)} %bitcast.53), calls=%async_computation | async-start | bytes 4194304 | tf_op jit(solution)/shard_map/all_to_all | solution.py:196
  21.9 1.3 %copy.14 = bf16[1,128,2048]{1,2,0:T(8,128)(2,1)S(1)} copy(bf16[1,128,2048]{2,1,0:T(8,128)(2,1)} %param.13) | data formatting | bytes 1048576 | tf_op args[6]
  23.3 0.7 copy.16
  24.0 0.7 copy.15
  24.7 0.3 fusion.8
  25.0 0.3 fusion.6
  25.3 0.1 fusion.16
  25.4 16.0 %all_gather.3 = bf16[512,128]{1,0:T(8,128)(2,1)S(1)} all-gather(bf16[128,128]{1,0:T(8,128)(2,1)S(1)} %fusion.16), channel_id=1, replica_groups=mesh['trial'=8,'dp'=8,'tensor'=4] {'tensor'}, dimensions={0}, use_global_device_ids=true | all-gather | bytes 163840 | tf_op jit(solution)/shard_map/all_gather | solution.py:216
  41.4 10.8 %all-to-all-done = bf16[32,16,2048]{2,1,0:T(8,128)(2,1)S(1)} async-done(((bf16[32,16,2048]{2,1,0:T(8,128)(2,1)}), bf16[32,16,2048]{2,1,0:T(8,128)(2,1)S(1)}, u32[]{:S(2)}, u32[]{:S(2)}) %all-to-all-start) | async-done | bytes 2097184 | tf_op jit(solution)/shard_map/all_to_all | solution.py:196
  52.1 0.7 fusion.4
  52.9 1.5 %fusion.24 = f32[128,2048]{1,0:T(8,128)} fusion(bf16[512,128]{1,0:T(8,128)(2,1)S(1)} %all_gather.3, bf16[512,2048]{1,0:T(8,128)(2,1)S(1)} %bitcast.51), kind=kOutput, calls=%fused_computation.34 | convolution fusion | flops 268435456 | bytes 3276800 | tf_op jit(solution)/shard_map/dot_general | solution.py:217
  54.3 0.6 constant_dynamic-slice_fusion.own_rk_ref
  55.0 9.2 %fusion.23 = (bf16[512,2048]{1,0:T(8,128)(2,1)}, f32[512,2048]{1,0:T(8,128)S(1)}) fusion(bf16[512,2048]{1,0:T(8,128)(2,1)S(1)} %bitcast.52, bf16[2048,2048]{1,0:T(8,128)(2,1)} %param.10), kind=kOutput, calls=%fused_computation.33 | convolution fusion | flops 4296015872 | bytes 16777216 | tf_op jit(solution)/shard_map/dot_general | solution.py:222
  64.2 1.0 constant_dynamic-slice_fusion.1.own_kv_ref
  65.2 34.5 %shard_map.94 = (f32[128,2048]{1,0:T(8,128)}, f32[128,128]{1,0:T(8,128)}, f32[64,128]{1,0:T(8,128)}) custom-call(bf16[4,128,2048]{2,1,0:T(8,128)(2,1)} %bitcast.55, f32[4,128,128]{2,1,0:T(8,128)} %bitcast.59, f32[128,2048]{1,0:T(8,128)} %constant_dynamic-slice_fusion.1.own_kv_ref, f32[128,128]{1,0:T(8,128)} %constant_dynamic-slice_fusion.own_rk_ref, ...), custom_call_target="tpu_custom_call" | custom-call | tf_op jit(solution)/shard_map/pallas_call | solution.py:139
  99.8 0.9 multiply_bitcast_fusion
  100.7 0.7 copy.17
  101.4 1.3 %fusion.11 = f32[128,1024]{1,0:T(8,128)S(1)} fusion(bf16[64,2048]{1,0:T(8,128)(2,1)S(1)} %bitcast.64, f32[128,128]{1,0:T(8,128)} %get-tuple-element.7), kind=kOutput, calls=%fused_computation.15 | convolution fusion | flops 100663296 | bytes 720896 | tf_op jit(solution)/shard_map/dot_general | solution.py:243
  102.7 1.2 %fusion.14 = f32[128,1024]{1,0:T(8,128)S(1)} fusion(bf16[64,2048]{1,0:T(8,128)(2,1)S(1)} %bitcast.65, f32[128,128]{1,0:T(8,128)} %get-tuple-element.7), kind=kOutput, calls=%fused_computation.18 | convolution fusion | flops 100663296 | bytes 720896 | tf_op jit(solution)/shard_map/dot_general | solution.py:240
  103.9 1.1 fusion.3
  (13 shorter events, 0.1 us)
Async XLA Ops:
  7.2 45.0 %copy-start = (bf16[1,2048,128]{2,1,0:T(8,128)(2,1)S(1)}, bf16[1,2048,128]{2,1,0:T(8,128)(2,1)}, u32[]{:S(2)}) copy-start(bf16[1,2048,128]{2,1,0:T(8,128)(2,1)} %param.11) | copy-start | bytes 1572868
  13.2 38.9 %all-to-all-start = ((bf16[32,16,2048]{2,1,0:T(8,128)(2,1)}), bf16[32,16,2048]{2,1,0:T(8,128)(2,1)S(1)}, u32[]{:S(2)}, u32[]{:S(2)}) async-start(bf16[32,16,2048]{2,1,0:T(8,128)(2,1)} %bitcast.53), calls=%async_computation | async-start | bytes 4194304 | tf_op jit(solution)/shard_map/all_to_all | solution.py:196
  21.8 2.9 %copy-start.3 = (bf16[1,64,2048]{2,1,0:T(8,128)(2,1)S(1)}, bf16[1,64,2048]{2,1,0:T(8,128)(2,1)}, u32[]{:S(2)}) copy-start(bf16[1,64,2048]{2,1,0:T(8,128)(2,1)} %param.12) | copy-start | bytes 786436
  21.8 83.2 %reduce-scatter.2.cloned.1.call-start = ((), (), s32[]{:S(2)}) async-start(), calls=%async_computation.2 | async-start | bytes 1179648 | tf_op jit(solution)/shard_map/reduce_scatter | solution.py:250
  52.8 1.5 %copy-start.1 = (f32[512,128]{1,0:T(8,128)}, f32[512,128]{1,0:T(8,128)S(1)}, u32[]{:S(2)}) copy-start(f32[512,128]{1,0:T(8,128)S(1)} %fusion.4) | copy-start | bytes 786436
  99.8 4.1 %copy-start.2 = (f32[128,2048]{1,0:T(8,128)S(1)}, f32[128,2048]{1,0:T(8,128)}, u32[]{:S(2)}) copy-start(f32[128,2048]{1,0:T(8,128)} %get-tuple-element.6) | copy-start | bytes 3145732
Sparse Core Ops, SparseCore 0:
  54.5 33.7 reduce-scatter.1

commit v11 on v10

--- a/solution.py
+++ b/solution.py
@@ -190,9 +190,11 @@
         residual_rows.reshape(pool_dev, tensors, normed_input),
         preferred_element_type=jnp.float32,
     )
-    msq = jnp.mean(wide * wide, axis=(1, 3), keepdims=True)
+    raw = residual_rows.astype(jnp.float32)
+    row_scale = lax.rsqrt(jnp.mean(raw * raw, axis=1) + norm_eps)
+    picked_scale = jnp.dot(onehot.astype(jnp.float32), row_scale, precision=highest_precision)
     gain = input_norm_weight.reshape(1, tensors, 1, normed_input)
-    chosen = (wide * lax.rsqrt(msq + norm_eps) * gain).astype(jnp.bfloat16)
+    chosen = (wide * picked_scale.reshape(trials, 1, select, 1) * gain).astype(jnp.bfloat16)
     arrived = lax.all_to_all(
         chosen.reshape(trials * tensors, select, normed_input),
         ("trial", "tensor"),
@@ -221,6 +223,10 @@
     down_weight = adapter_down_weight[0]
     keyval = jnp.dot(rows, keyvalue_weight, preferred_element_type=jnp.float32)
     ranks = jnp.dot(rows, down_weight, preferred_element_type=jnp.float32)
+    up_bf = adapter_up_weight[0]
+    block_up = jnp.zeros((2 * rank_index, kv_width), up_bf.dtype)
+    block_up = block_up.at[:rank_index, :keyvalue_half].set(up_bf[:, :keyvalue_half])
+    block_up = block_up.at[rank_index:, keyvalue_half:].set(up_bf[:, keyvalue_half:])
     block = tok_dev // tensors
     mine = lax.axis_index("tensor") * block
     quarter = dps // 2
@@ -237,15 +243,14 @@
         dps,
         0,
     )
-    adapter_key = jnp.dot(
-        local_rank_rows[:, :rank_index], up_weight[:, :keyvalue_half], precision=highest_precision
-    )
-    adapter_value = jnp.dot(
-        local_rank_rows[:, rank_index:], up_weight[:, keyvalue_half:], precision=highest_precision
-    )
-    keyvalue_output = frozen_output_local + adapter_scale * jnp.concatenate(
-        [adapter_key, adapter_value], axis=1
-    )
+    high = local_rank_rows.astype(jnp.bfloat16)
+    low = (local_rank_rows - high.astype(jnp.float32)).astype(jnp.bfloat16)
+    adapter = jnp.dot(
+        jnp.concatenate([high, low], axis=1),
+        jnp.concatenate([block_up, block_up], axis=0),
+        preferred_element_type=jnp.float32,
+    )
+    keyvalue_output = frozen_output_local + adapter_scale * adapter
 
     grad_a = lax.psum_scatter(grad_a_term, "dp", scatter_dimension=0, tiled=True)
 

time: 112 us -> 112 us (level)
  local copies, waits for them, and re-layouts: 6.82 us -> 7.94 us
    reduce_sum x0 -> x1, other arithmetic: none -> 2.08 us  [shards(): row_scale = lax.rsqrt(jnp.mean(raw * raw, axis=1) + norm_eps)]
    scatter x0 -> x2, local copies, waits for them, and re-layouts: none -> 1.53 us  [the longest x1 0.86 us: shards(): block_up.at[:rank_index, :keyvalue_half].set(up_bf[:, :keyvalue_half])]
    broadcast_in_dim x2 -> x1, other arithmetic: 2.06 us -> 0.91 us  [shards(): return (keyvalue_output[None], grad_a[None], grad_b[None])]
  transfers between devices with their start and end apart: 2 -> 2, of which waited for: 1 -> 1; matrix products, arithmetic and copies ran while one was open for 17% -> 19% of each run, Pallas kernels for 31% -> 31%
where the time goes in v11:
time: 112 us
  Pallas kernels  34.7 us (31%)
  matrix products  17 us (15%)
  blocking collectives  15.1 us (13%)
  between operations  14.2 us (13%)
  waiting for transfers between devices  10.1 us (9%)
  starting transfers between devices  8.63 us (8%)
  local copies, waits for them, and re-layouts  7.94 us (7%)
  other arithmetic  4 us (4%)
    pallas_call x1, Pallas kernels, tensor_sum(): pl.pallas_call(functools.partial(_tensor_sum_kernel, n1, n2), out_shape=(...  34.7 us
    all_gather x1, blocking collectives, shards(): every_rank = lax.all_gather(rank_gradient, 'tensor', axis=0, tiled=True)  15.1 us
    all_to_all x1, waiting for transfers between devices, shards(): lax.all_to_all(chosen.reshape(trials * tensors, select, normed_input), ('...  10.1 us
    dot_general x1, matrix products, shards(): keyval = jnp.dot(rows, keyvalue_weight, preferred_element_type=jnp.float32)  9.22 us
    all_to_all x1, starting transfers between devices, shards(): lax.all_to_all(chosen.reshape(trials * tensors, select, normed_input), ('...  8.59 us
    dot_general x1, matrix products, shards(): jnp.dot(jnp.concatenate([high, low], axis=1), jnp.concatenate([block_up,...  2.83 us
  transfers between devices with their start and end apart: 2, of which 1 were waited for; matrix products, arithmetic and copies ran while one was open for 19% of the time, Pallas kernels for 31%

profile of v11, /device:TPU:1, one launch (start us, length us, event | category | flops | bytes accessed | tf_op | source)
XLA Modules:
  0.0 111.7 jit_solution(17945118636839038237)
XLA Ops:
  7.2 0.9 constant_dynamic-slice_fusion.2
  8.2 2.1 %multiply_reduce_fusion = f32[128]{0:T(128)S(1)} fusion(bf16[128,8192]{1,0:T(8,128)(2,1)} %param.11), kind=kLoop, calls=%fused_computation.1 | loop fusion | flops 3145600 | bytes 2097664 | tf_op jit(solution)/shard_map/reduce_sum | solution.py:194
  10.3 0.2 convolution_bitcast_fusion
  10.7 2.1 %multiply_convert_fusion = bf16[8,16,4,2048]{3,1,2,0:T(8,128)(2,1)} fusion(bf16[16,4,8,2048]{3,2,1,0:T(8,128)(2,1)S(1)} %bitcast.52, f32[4,2048]{1,0:T(4,128)S(1)} %mul.61, f32[8,16]{1,0:T(8,128)S(1)} %mul.58, s32[8,16]{1,0:T(8,128)S(1)} %constant_dynamic-slice_fusion.2), kind=kOutput, calls=%fused_computation | convolution fusion | flops 271597568 | bytes 4228096 | tf_op jit(solution)/shard_map/tsr,rkf->tksf/dot_general | solution.py:187
  12.8 8.6 %all-to-all-start = ((bf16[32,16,2048]{2,1,0:T(8,128)(2,1)}), bf16[32,16,2048]{2,1,0:T(8,128)(2,1)S(1)}, u32[]{:S(2)}, u32[]{:S(2)}) async-start(bf16[32,16,2048]{2,1,0:T(8,128)(2,1)} %bitcast.53), calls=%async_computation | async-start | bytes 4194304 | tf_op jit(solution)/shard_map/all_to_all | solution.py:198
  21.4 1.3 %copy.14 = bf16[1,128,2048]{1,2,0:T(8,128)(2,1)S(1)} copy(bf16[1,128,2048]{2,1,0:T(8,128)(2,1)} %param.17) | data formatting | bytes 1048576 | tf_op args[6]
  22.8 0.7 copy.15
  23.6 0.7 copy.16
  24.3 0.9 scatter.6
  25.2 0.3 fusion.10
  25.4 0.3 fusion.8
  25.8 15.1 %all_gather.3 = bf16[512,128]{1,0:T(8,128)(2,1)S(1)} all-gather(bf16[128,128]{1,0:T(8,128)(2,1)S(1)} %fusion.16), channel_id=1, replica_groups=mesh['trial'=8,'dp'=8,'tensor'=4] {'tensor'}, dimensions={0}, use_global_device_ids=true | all-gather | bytes 163840 | tf_op jit(solution)/shard_map/all_gather | solution.py:218
  40.9 0.7 slice_dynamic-update-slice_fusion
  41.6 10.1 %all-to-all-done = bf16[32,16,2048]{2,1,0:T(8,128)(2,1)S(1)} async-done(((bf16[32,16,2048]{2,1,0:T(8,128)(2,1)}), bf16[32,16,2048]{2,1,0:T(8,128)(2,1)S(1)}, u32[]{:S(2)}, u32[]{:S(2)}) %all-to-all-start) | async-done | bytes 2097184 | tf_op jit(solution)/shard_map/all_to_all | solution.py:198
  51.7 0.7 fusion.6
  52.4 1.5 %fusion.33 = f32[128,2048]{1,0:T(8,128)} fusion(bf16[512,128]{1,0:T(8,128)(2,1)S(1)} %all_gather.3, bf16[512,2048]{1,0:T(8,128)(2,1)S(1)} %bitcast.50), kind=kOutput, calls=%fused_computation.46 | convolution fusion | flops 268435456 | bytes 3276800 | tf_op jit(solution)/shard_map/dot_general | solution.py:219
  53.9 0.6 constant_dynamic-slice_fusion.own_rk_ref
  54.5 9.2 %fusion.32 = (bf16[512,2048]{1,0:T(8,128)(2,1)}, f32[512,2048]{1,0:T(8,128)S(1)}) fusion(bf16[512,2048]{1,0:T(8,128)(2,1)S(1)} %bitcast.51, bf16[2048,2048]{1,0:T(8,128)(2,1)} %param.14), kind=kOutput, calls=%fused_computation.45 | convolution fusion | flops 4296015872 | bytes 16777216 | tf_op jit(solution)/shard_map/dot_general | solution.py:224
  63.8 1.0 constant_dynamic-slice_fusion.1.own_kv_ref
  64.8 34.7 %shard_map.94 = (f32[128,2048]{1,0:T(8,128)}, f32[128,128]{1,0:T(8,128)}, f32[64,128]{1,0:T(8,128)}) custom-call(bf16[4,128,2048]{2,1,0:T(8,128)(2,1)} %bitcast.54, f32[4,128,128]{2,1,0:T(8,128)} %bitcast.58, f32[128,2048]{1,0:T(8,128)} %constant_dynamic-slice_fusion.1.own_kv_ref, f32[128,128]{1,0:T(8,128)} %constant_dynamic-slice_fusion.own_rk_ref, ...), custom_call_target="tpu_custom_call" | custom-call | tf_op jit(solution)/shard_map/pallas_call | solution.py:139
  99.5 0.9 multiply_bitcast_fusion
  100.4 0.7 copy.17
  101.1 0.9 subtract_convert_fusion
  102.0 2.8 %fusion.1 = f32[1,128,2048]{2,1,0:T(8,128)} fusion(f32[128,2048]{1,0:T(8,128)} %get-tuple-element.30, bf16[128,2048]{1,0:T(8,128)(2,1)} %slice_dynamic-update-slice_fusion, bf16[128,128]{1,0:T(8,128)(2,1)S(1)} %get-tuple-element.39, bf16[128,128]{1,0:T(8,128)(2,1)S(1)} %get-tuple-element.40), kind=kOutput, calls=%fused_computation.4 | convolution fusion | flops 136970240 | bytes 2686976 | tf_op jit(solution)/shard_map/dot_general | solution.py:248
  (19 shorter events, 0.5 us)
Async XLA Ops:
  7.2 44.5 %copy-start = (bf16[1,2048,128]{2,1,0:T(8,128)(2,1)S(1)}, bf16[1,2048,128]{2,1,0:T(8,128)(2,1)}, u32[]{:S(2)}) copy-start(bf16[1,2048,128]{2,1,0:T(8,128)(2,1)} %param.15) | copy-start | bytes 1572868
  7.2 3.5 %copy-start.1 = (bf16[128,8192]{1,0:T(8,128)(2,1)S(1)}, bf16[128,8192]{1,0:T(8,128)(2,1)}, u32[]{:S(2)}) copy-start(bf16[128,8192]{1,0:T(8,128)(2,1)} %param.11) | copy-start | bytes 6291460
  7.2 3.4 %copy-start.4 = (f32[8192]{0:T(1024)S(1)}, f32[8192]{0:T(1024)}, u32[]{:S(2)}) copy-start(f32[8192]{0:T(1024)} %param.12) | copy-start | bytes 98308
  12.8 38.9 %all-to-all-start = ((bf16[32,16,2048]{2,1,0:T(8,128)(2,1)}), bf16[32,16,2048]{2,1,0:T(8,128)(2,1)S(1)}, u32[]{:S(2)}, u32[]{:S(2)}) async-start(bf16[32,16,2048]{2,1,0:T(8,128)(2,1)} %bitcast.53), calls=%async_computation | async-start | bytes 4194304 | tf_op jit(solution)/shard_map/all_to_all | solution.py:198
  21.4 2.9 %copy-start.3 = (bf16[1,64,2048]{2,1,0:T(8,128)(2,1)S(1)}, bf16[1,64,2048]{2,1,0:T(8,128)(2,1)}, u32[]{:S(2)}) copy-start(bf16[1,64,2048]{2,1,0:T(8,128)(2,1)} %param.16) | copy-start | bytes 786436
  21.4 83.4 %reduce-scatter.2.cloned.1.call-start = ((), (), s32[]{:S(2)}) async-start(), calls=%async_computation.2 | async-start | bytes 1179648 | tf_op jit(solution)/shard_map/reduce_scatter | solution.py:255
  52.4 1.5 %copy-start.2 = (f32[512,128]{1,0:T(8,128)}, f32[512,128]{1,0:T(8,128)S(1)}, u32[]{:S(2)}) copy-start(f32[512,128]{1,0:T(8,128)S(1)} %fusion.6) | copy-start | bytes 786436
Sparse Core Ops, SparseCore 0:
  54.0 34.2 reduce-scatter.1

commit v12 on v10

--- a/solution.py
+++ b/solution.py
@@ -14,9 +14,9 @@
 
 
 def _tensor_sum_kernel(
-    n1, n2, kv_ref, rk_ref, own_kv_ref, own_rk_ref, gk_ref, gv_ref,
+    n1, n2, rows_ref, w_ref, rk_ref, own_rk_ref, gk_ref, gv_ref,
     kv_out, rk_out, b_out,
-    recv_kv, recv_rk, terms, recv_b1, partial, recv_b2, forward, sems, kv_sems,
+    recv_kv, recv_rk, terms, recv_b1, partial, recv_b2, forward, outgoing, across_part, sems, kv_sems,
 ):
     me1 = lax.axis_index("tensor")
     me2 = lax.axis_index("dp")
@@ -51,7 +51,7 @@
         target = lax.rem(me1 + shift, n1)
         rk_copies.append(send(rk_ref.at[target], recv_rk, 2, shift, first(target)))
     pieces = kv_sems.shape[2]
-    step = kv_ref.shape[1] // pieces
+    step = kv_out.shape[0] // pieces
 
     def send_piece(src_ref, slot, piece, device):
         rows = pl.ds(piece * step, step)
@@ -66,8 +66,18 @@
         copy.start()
         return copy
 
-    diagonal_copies = [send_piece(kv_ref.at[diagonal], 1, p, first(partner)) for p in range(pieces)]
-    own_copies = [send_piece(kv_ref.at[partner], 0, p, first(partner)) for p in range(pieces)]
+    tokens = kv_out.shape[0]
+
+    def product(member):
+        block = rows_ref[pl.ds(pl.multiple_of(member * tokens, tokens), tokens), :]
+        return jnp.dot(block, w_ref[...], preferred_element_type=jnp.float32)
+
+    outgoing[1] = product(diagonal).astype(outgoing.dtype)
+    diagonal_copies = [send_piece(outgoing.at[1], 1, p, first(partner)) for p in range(pieces)]
+    outgoing[0] = product(partner).astype(outgoing.dtype)
+    own_copies = [send_piece(outgoing.at[0], 0, p, first(partner)) for p in range(pieces)]
+    across_part[...] = product(across)
+    own_part = product(me1)
 
     rk_out[...] = own_rk_ref[...]
     for shift, copy in zip(range(1, n1), rk_copies):
@@ -98,13 +108,14 @@
         rows = pl.ds(p * step, step)
         copy.wait_recv()
         forward[rows, :] = (
-            kv_ref[across, rows, :].astype(jnp.float32) + recv_kv[1, rows, :].astype(jnp.float32)
+            across_part[rows, :] + recv_kv[1, rows, :].astype(jnp.float32)
         ).astype(forward.dtype)
         forward_copies.append(send_piece(forward, 2, p, first(across)))
+    kv_out[...] = own_part
     for p, copy in enumerate(own_copies):
         rows = pl.ds(p * step, step)
         copy.wait_recv()
-        kv_out[rows, :] = own_kv_ref[rows, :] + recv_kv[0, rows, :].astype(jnp.float32)
+        kv_out[rows, :] += recv_kv[0, rows, :].astype(jnp.float32)
 
     summed = terms[me1]
     for shift, copy in zip(range(1, n1), b1_copies):
@@ -129,8 +140,10 @@
         copy.wait_send()
 
 
-def tensor_sum(kv, rk, own_kv, own_rk, gk, gv, n2, collective_id):
-    n1 = kv.shape[0]
+def tensor_sum(rows, w, rk, own_rk, gk, gv, n2, collective_id):
+    n1 = rk.shape[0]
+    tokens = rows.shape[0] // n1
+    kv_width = w.shape[1]
     quarter = n2 // 2
     columns = gk.shape[0]
     lanes = rk.shape[2]
@@ -139,25 +152,27 @@
     return pl.pallas_call(
         functools.partial(_tensor_sum_kernel, n1, n2),
         out_shape=(
-            jax.ShapeDtypeStruct(own_kv.shape, jnp.float32),
+            jax.ShapeDtypeStruct((tokens, kv_width), jnp.float32),
             jax.ShapeDtypeStruct(own_rk.shape, jnp.float32),
             jax.ShapeDtypeStruct((block, lanes), jnp.float32),
         ),
         in_specs=[vmem] * 6,
         out_specs=(vmem, vmem, vmem),
         scratch_shapes=[
-            pltpu.VMEM(kv.shape, kv.dtype),
+            pltpu.VMEM((n1, tokens, kv_width), jnp.bfloat16),
             pltpu.VMEM(rk.shape, rk.dtype),
             pltpu.VMEM((n1, quarter * block, lanes), jnp.float32),
             pltpu.VMEM((n1, quarter * block, lanes), jnp.float32),
             pltpu.VMEM((quarter, block, lanes), jnp.float32),
             pltpu.VMEM((n2, block, lanes), jnp.float32),
-            pltpu.VMEM(kv.shape[1:], kv.dtype),
+            pltpu.VMEM((tokens, kv_width), jnp.bfloat16),
+            pltpu.VMEM((2, tokens, kv_width), jnp.bfloat16),
+            pltpu.VMEM((tokens, kv_width), jnp.float32),
             pltpu.SemaphoreType.DMA((8, max(n1, n2))),
             pltpu.SemaphoreType.DMA((2, 3, 4)),
         ],
         compiler_params=pltpu.CompilerParams(collective_id=collective_id, has_side_effects=True),
-    )(kv, rk, own_kv, own_rk, gk, gv)
+    )(rows, w, rk, own_rk, gk, gv)
 
 
 def shards(
@@ -219,7 +234,6 @@
     )
 
     down_weight = adapter_down_weight[0]
-    keyval = jnp.dot(rows, keyvalue_weight, preferred_element_type=jnp.float32)
     ranks = jnp.dot(rows, down_weight, preferred_element_type=jnp.float32)
     block = tok_dev // tensors
     mine = lax.axis_index("tensor") * block
@@ -228,9 +242,9 @@
     grad_t = keyvalue_gradient[0].T.reshape(2, quarter, tensors, width, tok_dev // tensors)
     grad_t = grad_t.transpose(0, 2, 1, 3, 4).reshape(2, keyvalue_half, tok_dev // tensors)
     frozen_output_local, local_rank_rows, up_block = tensor_sum(
-        keyval.astype(jnp.bfloat16).reshape(tensors, block, kv_width),
+        rows,
+        keyvalue_weight,
         ranks.reshape(tensors, block, ranks.shape[1]),
-        lax.dynamic_slice_in_dim(keyval, mine, block, 0),
         lax.dynamic_slice_in_dim(ranks, mine, block, 0),
         grad_t[0],
         grad_t[1],

time: 112 us -> 110 us (0.982)
  matrix products: 16.8 us -> 9.6 us
  Pallas kernels: 34.5 us -> 37.2 us
  other arithmetic: 4.15 us -> 6.31 us
  local copies, waits for them, and re-layouts: 6.82 us -> 5.09 us
  blocking collectives: 16 us -> 17.5 us
    dot_general x1 -> x0, matrix products: 9.22 us -> none  [shards(): keyval = jnp.dot(rows, keyvalue_weight, preferred_element_type=jnp.float32)]
    pallas_call x1, Pallas kernels: 34.5 us -> 37.2 us  [tensor_sum(): pl.pallas_call(functools.partial(_tensor_sum_kernel, n1, n2), out_shape=(...]
    convert_element_type x1, other arithmetic: 2 us -> 4.16 us  [shards(): chosen = (wide * lax.rsqrt(msq + norm_eps) * gain).astype(jnp.bfloat16)]
    dot_general x1, matrix products: 2.42 us -> 4.29 us  [shards(): jnp.einsum('tsr,rkf->tksf', onehot.reshape(trials, select, pool_dev), res...]
    all_gather x1, blocking collectives: 16 us -> 17.5 us  [shards(): every_rank = lax.all_gather(rank_gradient, 'tensor', axis=0, tiled=True)]
  transfers between devices with their start and end apart: 2 -> 2, of which waited for: 1 -> 1; matrix products, arithmetic and copies ran while one was open for 17% -> 9% of each run, Pallas kernels for 31% -> 34%
where the time goes in v12:
time: 110 us; the launch traced here: 109 us
  Pallas kernels  37.2 us (34%)
  blocking collectives  17.5 us (16%)
  between operations  14.2 us (13%)
  waiting for transfers between devices  10.8 us (10%)
  matrix products  9.6 us (9%)
  starting transfers between devices  8.76 us (8%)
  other arithmetic  6.31 us (6%)
  local copies, waits for them, and re-layouts  5.09 us (5%)
    pallas_call x1, Pallas kernels, tensor_sum(): pl.pallas_call(functools.partial(_tensor_sum_kernel, n1, n2), out_shape=(...  37.2 us
    all_gather x1, blocking collectives, shards(): every_rank = lax.all_gather(rank_gradient, 'tensor', axis=0, tiled=True)  17.5 us
    all_to_all x1, waiting for transfers between devices, shards(): lax.all_to_all(chosen.reshape(trials * tensors, select, normed_input), ('...  10.8 us
    all_to_all x1, starting transfers between devices, shards(): lax.all_to_all(chosen.reshape(trials * tensors, select, normed_input), ('...  8.72 us
    dot_general x1, matrix products, shards(): jnp.einsum('tsr,rkf->tksf', onehot.reshape(trials, select, pool_dev), res...  4.29 us
    convert_element_type x1, other arithmetic, shards(): chosen = (wide * lax.rsqrt(msq + norm_eps) * gain).astype(jnp.bfloat16)  4.16 us
  transfers between devices with their start and end apart: 2, of which 1 were waited for; matrix products, arithmetic and copies ran while one was open for 9% of the time, Pallas kernels for 34%

profile of v12, /device:TPU:1, one launch (start us, length us, event | category | flops | bytes accessed | tf_op | source)
XLA Modules:
  0.0 109.4 jit_solution(4855691506109440951)
XLA Ops:
  7.2 0.8 constant_dynamic-slice_fusion.1
  8.0 4.3 %multiply_reduce_fusion = (f32[8,16]{1,0:T(8,128)S(1)}, f32[8,16,4,2048]{3,1,2,0:T(8,128)}) fusion(bf16[16,4,8,2048]{3,2,1,0:T(8,128)(2,1)} %bitcast.51, s32[8,16]{1,0:T(8,128)S(1)} %constant_dynamic-slice_fusion.1), kind=kOutput, calls=%fused_computation.1 | convolution fusion | flops 270548864 | bytes 6292480 | tf_op jit(solution)/shard_map/tsr,rkf->tksf/dot_general | solution.py:202
  12.3 4.2 %multiply_convert_fusion = bf16[8,16,4,2048]{3,1,2,0:T(8,128)(2,1)} fusion(f32[8,16,4,2048]{3,1,2,0:T(8,128)} %get-tuple-element.18, f32[4,2048]{1,0:T(4,128)S(1)} %mul.59, f32[8,16]{1,0:T(8,128)S(1)} %add_rsqrt_fusion), kind=kLoop, calls=%fused_computation | loop fusion | flops 3145728 | bytes 6324736 | tf_op jit(solution)/shard_map/convert_element_type | solution.py:210
  16.5 8.7 %all-to-all-start = ((bf16[32,16,2048]{2,1,0:T(8,128)(2,1)}), bf16[32,16,2048]{2,1,0:T(8,128)(2,1)S(1)}, u32[]{:S(2)}, u32[]{:S(2)}) async-start(bf16[32,16,2048]{2,1,0:T(8,128)(2,1)} %bitcast.50), calls=%async_computation | async-start | bytes 4194304 | tf_op jit(solution)/shard_map/all_to_all | solution.py:211
  25.2 0.0 reduce-scatter.2.cloned.1.call-start
  25.3 1.3 %copy.14 = bf16[1,128,2048]{1,2,0:T(8,128)(2,1)S(1)} copy(bf16[1,128,2048]{2,1,0:T(8,128)(2,1)} %param.13) | data formatting | bytes 1048576 | tf_op args[6]
  26.6 0.3 fusion.6
  26.9 0.3 fusion.8
  27.1 0.1 fusion.16
  27.2 17.5 %all_gather.3 = bf16[512,128]{1,0:T(8,128)(2,1)S(1)} all-gather(bf16[128,128]{1,0:T(8,128)(2,1)S(1)} %fusion.16), channel_id=1, replica_groups=mesh['trial'=8,'dp'=8,'tensor'=4] {'tensor'}, dimensions={0}, use_global_device_ids=true | all-gather | bytes 163840 | tf_op jit(solution)/shard_map/all_gather | solution.py:231
  44.7 10.8 %all-to-all-done = bf16[32,16,2048]{2,1,0:T(8,128)(2,1)S(1)} async-done(((bf16[32,16,2048]{2,1,0:T(8,128)(2,1)}), bf16[32,16,2048]{2,1,0:T(8,128)(2,1)S(1)}, u32[]{:S(2)}, u32[]{:S(2)}) %all-to-all-start) | async-done | bytes 2097184 | tf_op jit(solution)/shard_map/all_to_all | solution.py:211
  55.5 1.6 %fusion.23 = f32[128,2048]{1,0:T(8,128)} fusion(bf16[512,128]{1,0:T(8,128)(2,1)S(1)} %all_gather.3, bf16[512,2048]{1,0:T(8,128)(2,1)S(1)} %bitcast.47), kind=kOutput, calls=%fused_computation.32 | convolution fusion | flops 268435456 | bytes 3276800 | tf_op jit(solution)/shard_map/dot_general | solution.py:232
  57.2 0.0 reduce-scatter.2.cloned.1.call-update
  57.2 0.7 copy.15
  58.0 0.7 copy.16
  58.7 0.7 fusion.4
  59.4 0.7 constant_dynamic-slice_fusion.own_rk_ref
  60.1 0.0 copy-done.2
  60.1 37.2 %shard_map.94 = (f32[128,2048]{1,0:T(8,128)}, f32[128,128]{1,0:T(8,128)}, f32[64,128]{1,0:T(8,128)}) custom-call(bf16[512,2048]{1,0:T(8,128)(2,1)} %bitcast.49, bf16[2048,2048]{1,0:T(8,128)(2,1)} %w_ref.1, f32[4,128,128]{2,1,0:T(8,128)} %bitcast.55, f32[128,128]{1,0:T(8,128)} %constant_dynamic-slice_fusion.own_rk_ref, bf16[1024,128]{1,0:T(8,128)(2,1)} %bitcast.56, ...), custom_call_target="tpu_custom_call" | custom-call | tf_op jit(solution)/shard_map/pallas_call | solution.py:152
  97.3 0.9 multiply_bitcast_fusion
  98.3 0.7 copy.17
  99.0 1.3 %fusion.11 = f32[128,1024]{1,0:T(8,128)S(1)} fusion(bf16[64,2048]{1,0:T(8,128)(2,1)S(1)} %bitcast.60, f32[128,128]{1,0:T(8,128)} %get-tuple-element.7), kind=kOutput, calls=%fused_computation.15 | convolution fusion | flops 100663296 | bytes 720896 | tf_op jit(solution)/shard_map/dot_general | solution.py:257
  100.2 1.2 %fusion.14 = f32[128,1024]{1,0:T(8,128)S(1)} fusion(bf16[64,2048]{1,0:T(8,128)(2,1)S(1)} %bitcast.61, f32[128,128]{1,0:T(8,128)} %get-tuple-element.7), kind=kOutput, calls=%fused_computation.18 | convolution fusion | flops 100663296 | bytes 720896 | tf_op jit(solution)/shard_map/dot_general | solution.py:254
  101.4 1.1 %fusion.3 = f32[1,128,2048]{2,1,0:T(8,128)} fusion(f32[128,2048]{1,0:T(8,128)S(1)} %copy-done.3, f32[128,1024]{1,0:T(8,128)S(1)} %fusion.11, f32[128,1024]{1,0:T(8,128)S(1)} %fusion.14), kind=kLoop, calls=%fused_computation.7 | loop fusion | flops 786432 | bytes 3145728 | tf_op jit(solution)/shard_map/broadcast_in_dim | solution.py:269
  (15 shorter events, 0.1 us)
Async XLA Ops:
  7.2 51.5 %copy-start = (bf16[1,2048,128]{2,1,0:T(8,128)(2,1)S(1)}, bf16[1,2048,128]{2,1,0:T(8,128)(2,1)}, u32[]{:S(2)}) copy-start(bf16[1,2048,128]{2,1,0:T(8,128)(2,1)} %param.11) | copy-start | bytes 1572868
  8.0 4.3 %copy-start.5 = (f32[8192]{0:T(1024)S(1)}, f32[8192]{0:T(1024)}, u32[]{:S(2)}) copy-start(f32[8192]{0:T(1024)} %param.8) | copy-start | bytes 98308
  16.5 10.1 %copy-start.4 = (bf16[1,64,2048]{2,1,0:T(8,128)(2,1)S(1)}, bf16[1,64,2048]{2,1,0:T(8,128)(2,1)}, u32[]{:S(2)}) copy-start(bf16[1,64,2048]{2,1,0:T(8,128)(2,1)} %param.12) | copy-start | bytes 786436
  16.5 39.0 %all-to-all-start = ((bf16[32,16,2048]{2,1,0:T(8,128)(2,1)}), bf16[32,16,2048]{2,1,0:T(8,128)(2,1)S(1)}, u32[]{:S(2)}, u32[]{:S(2)}) async-start(bf16[32,16,2048]{2,1,0:T(8,128)(2,1)} %bitcast.50), calls=%async_computation | async-start | bytes 4194304 | tf_op jit(solution)/shard_map/all_to_all | solution.py:211
  25.2 77.3 %reduce-scatter.2.cloned.1.call-start = ((), (), s32[]{:S(2)}) async-start(), calls=%async_computation.2 | async-start | bytes 1179648 | tf_op jit(solution)/shard_map/reduce_scatter | solution.py:264
  55.5 3.2 %copy-start.1 = (bf16[32,16,2048]{2,1,0:T(8,128)(2,1)}, bf16[32,16,2048]{2,1,0:T(8,128)(2,1)S(1)}, u32[]{:S(2)}) copy-start(bf16[32,16,2048]{2,1,0:T(8,128)(2,1)S(1)} %all-to-all-done) | copy-start | bytes 6291460
  59.4 0.7 copy-start.2
  97.3 4.1 %copy-start.3 = (f32[128,2048]{1,0:T(8,128)S(1)}, f32[128,2048]{1,0:T(8,128)}, u32[]{:S(2)}) copy-start(f32[128,2048]{1,0:T(8,128)} %get-tuple-element.6) | copy-start | bytes 3145732
Sparse Core Ops, SparseCore 0:
  57.3 36.6 reduce-scatter.1

commit v13 on v12

--- a/solution.py
+++ b/solution.py
@@ -205,9 +205,11 @@
         residual_rows.reshape(pool_dev, tensors, normed_input),
         preferred_element_type=jnp.float32,
     )
-    msq = jnp.mean(wide * wide, axis=(1, 3), keepdims=True)
+    raw = residual_rows.astype(jnp.float32)
+    row_scale = lax.rsqrt(jnp.mean(raw * raw, axis=1) + norm_eps)
+    picked_scale = jnp.take(row_scale, picks, axis=0)
     gain = input_norm_weight.reshape(1, tensors, 1, normed_input)
-    chosen = (wide * lax.rsqrt(msq + norm_eps) * gain).astype(jnp.bfloat16)
+    chosen = (wide * picked_scale.reshape(trials, 1, select, 1) * gain).astype(jnp.bfloat16)
     arrived = lax.all_to_all(
         chosen.reshape(trials * tensors, select, normed_input),
         ("trial", "tensor"),

time: 110 us -> 106 us (0.964)
  matrix products: 9.6 us -> 7.41 us
  other arithmetic: 6.31 us -> 4.47 us
    convert_element_type x1 -> x0, other arithmetic: 4.16 us -> none  [shards(): chosen = (wide * lax.rsqrt(msq + norm_eps) * gain).astype(jnp.bfloat16)]
    reduce_sum x0 -> x1, other arithmetic: none -> 2.23 us  [shards(): row_scale = lax.rsqrt(jnp.mean(raw * raw, axis=1) + norm_eps)]
    dot_general x1, matrix products: 4.29 us -> 2.11 us  [shards(): jnp.einsum('tsr,rkf->tksf', onehot.reshape(trials, select, pool_dev), res...]
    gather x0 -> x2, local copies, waits for them, and re-layouts: none -> 1.3 us  [shards(): picked_scale = jnp.take(row_scale, picks, axis=0)]
  transfers between devices with their start and end apart: 2 -> 2, of which waited for: 1 -> 1; matrix products, arithmetic and copies ran while one was open for 9% -> 9% of each run, Pallas kernels for 34% -> 35%
where the time goes in v13:
time: 106 us
  Pallas kernels  37.2 us (35%)
  blocking collectives  17.5 us (17%)
  between operations  14.2 us (13%)
  waiting for transfers between devices  10.8 us (10%)
  starting transfers between devices  8.76 us (8%)
  matrix products  7.41 us (7%)
  local copies, waits for them, and re-layouts  5.74 us (5%)
  other arithmetic  4.47 us (4%)
    pallas_call x1, Pallas kernels, tensor_sum(): pl.pallas_call(functools.partial(_tensor_sum_kernel, n1, n2), out_shape=(...  37.2 us
    all_gather x1, blocking collectives, shards(): every_rank = lax.all_gather(rank_gradient, 'tensor', axis=0, tiled=True)  17.5 us
    all_to_all x1, waiting for transfers between devices, shards(): lax.all_to_all(chosen.reshape(trials * tensors, select, normed_input), ('...  10.8 us
    all_to_all x1, starting transfers between devices, shards(): lax.all_to_all(chosen.reshape(trials * tensors, select, normed_input), ('...  8.72 us
    reduce_sum x1, other arithmetic, shards(): row_scale = lax.rsqrt(jnp.mean(raw * raw, axis=1) + norm_eps)  2.23 us
  transfers between devices with their start and end apart: 2, of which 1 were waited for; matrix products, arithmetic and copies ran while one was open for 9% of the time, Pallas kernels for 35%

profile of v13, /device:TPU:1, one launch (start us, length us, event | category | flops | bytes accessed | tf_op | source)
XLA Modules:
  0.0 106.1 jit_solution(5217606302147856939)
XLA Ops:
  7.2 2.2 %multiply_reduce_fusion = f32[128]{0:T(128)S(1)} fusion(bf16[128,8192]{1,0:T(8,128)(2,1)} %param.7), kind=kLoop, calls=%fused_computation.2 | loop fusion | flops 3145600 | bytes 2097664 | tf_op jit(solution)/shard_map/reduce_sum | solution.py:209
  9.5 0.1 constant_dynamic-slice_fusion.1
  9.5 0.1 reshape.100
  9.6 1.2 %gather_fusion = f32[128]{0:T(128)S(1)} fusion(f32[128]{0:T(128)S(1)} %add_rsqrt_fusion, s32[1024]{0:T(1024)S(1)} %pad_clamp_fusion), kind=kCustom, calls=%fused_computation | custom fusion | bytes 1536 | tf_op jit(solution)/shard_map/jit(_take)/gather | solution.py:210
  11.0 0.1 and_select_fusion
  11.1 2.1 %multiply_convert_fusion = bf16[8,16,4,2048]{3,1,2,0:T(8,128)(2,1)} fusion(bf16[16,4,8,2048]{3,2,1,0:T(8,128)(2,1)S(1)} %bitcast.46, f32[4,2048]{1,0:T(4,128)S(1)} %mul.58, f32[8,16]{1,0:T(8,128)S(1)} %and_select_fusion, s32[8,16]{1,0:T(8,128)S(1)} %constant_dynamic-slice_fusion.1), kind=kOutput, calls=%fused_computation.1 | convolution fusion | flops 271597568 | bytes 4228096 | tf_op jit(solution)/shard_map/tsr,rkf->tksf/dot_general | solution.py:202
  13.2 8.7 %all-to-all-start = ((bf16[32,16,2048]{2,1,0:T(8,128)(2,1)}), bf16[32,16,2048]{2,1,0:T(8,128)(2,1)S(1)}, u32[]{:S(2)}, u32[]{:S(2)}) async-start(bf16[32,16,2048]{2,1,0:T(8,128)(2,1)} %bitcast.47), calls=%async_computation | async-start | bytes 4194304 | tf_op jit(solution)/shard_map/all_to_all | solution.py:213
  22.0 1.3 %copy.14 = bf16[1,128,2048]{1,2,0:T(8,128)(2,1)S(1)} copy(bf16[1,128,2048]{2,1,0:T(8,128)(2,1)} %param.13) | data formatting | bytes 1048576 | tf_op args[6]
  23.3 0.3 fusion.7
  23.6 0.3 fusion.5
  23.8 0.1 fusion.15
  23.9 17.5 %all_gather.3 = bf16[512,128]{1,0:T(8,128)(2,1)S(1)} all-gather(bf16[128,128]{1,0:T(8,128)(2,1)S(1)} %fusion.15), channel_id=1, replica_groups=mesh['trial'=8,'dp'=8,'tensor'=4] {'tensor'}, dimensions={0}, use_global_device_ids=true | all-gather | bytes 163840 | tf_op jit(solution)/shard_map/all_gather | solution.py:233
  41.4 10.8 %all-to-all-done = bf16[32,16,2048]{2,1,0:T(8,128)(2,1)S(1)} async-done(((bf16[32,16,2048]{2,1,0:T(8,128)(2,1)}), bf16[32,16,2048]{2,1,0:T(8,128)(2,1)S(1)}, u32[]{:S(2)}, u32[]{:S(2)}) %all-to-all-start) | async-done | bytes 2097184 | tf_op jit(solution)/shard_map/all_to_all | solution.py:213
  52.2 1.6 %fusion.23 = f32[128,2048]{1,0:T(8,128)} fusion(bf16[512,128]{1,0:T(8,128)(2,1)S(1)} %all_gather.3, bf16[512,2048]{1,0:T(8,128)(2,1)S(1)} %bitcast.43), kind=kOutput, calls=%fused_computation.37 | convolution fusion | flops 268435456 | bytes 3276800 | tf_op jit(solution)/shard_map/dot_general | solution.py:234
  53.9 0.7 copy.16
  54.7 0.7 copy.15
  55.4 0.7 fusion.3
  56.1 0.7 constant_dynamic-slice_fusion.own_rk_ref
  56.8 37.2 %shard_map.94 = (f32[128,2048]{1,0:T(8,128)}, f32[128,128]{1,0:T(8,128)}, f32[64,128]{1,0:T(8,128)}) custom-call(bf16[512,2048]{1,0:T(8,128)(2,1)} %bitcast.45, bf16[2048,2048]{1,0:T(8,128)(2,1)} %w_ref.1, f32[4,128,128]{2,1,0:T(8,128)} %bitcast.51, f32[128,128]{1,0:T(8,128)} %constant_dynamic-slice_fusion.own_rk_ref, bf16[1024,128]{1,0:T(8,128)(2,1)} %bitcast.53, ...), custom_call_target="tpu_custom_call" | custom-call | tf_op jit(solution)/shard_map/pallas_call | solution.py:152
  94.0 0.9 multiply_bitcast_fusion
  95.0 0.7 copy.17
  95.7 1.3 %fusion.10 = f32[128,1024]{1,0:T(8,128)S(1)} fusion(bf16[64,2048]{1,0:T(8,128)(2,1)S(1)} %bitcast.56, f32[128,128]{1,0:T(8,128)} %get-tuple-element.7), kind=kOutput, calls=%fused_computation.15 | convolution fusion | flops 100663296 | bytes 720896 | tf_op jit(solution)/shard_map/dot_general | solution.py:259
  96.9 1.2 %fusion.13 = f32[128,1024]{1,0:T(8,128)S(1)} fusion(bf16[64,2048]{1,0:T(8,128)(2,1)S(1)} %bitcast.57, f32[128,128]{1,0:T(8,128)} %get-tuple-element.7), kind=kOutput, calls=%fused_computation.18 | convolution fusion | flops 100663296 | bytes 720896 | tf_op jit(solution)/shard_map/dot_general | solution.py:256
  98.1 1.1 %fusion.2 = f32[1,128,2048]{2,1,0:T(8,128)} fusion(f32[128,2048]{1,0:T(8,128)S(1)} %copy-done.4, f32[128,1024]{1,0:T(8,128)S(1)} %fusion.10, f32[128,1024]{1,0:T(8,128)S(1)} %fusion.13), kind=kLoop, calls=%fused_computation.7 | loop fusion | flops 786432 | bytes 3145728 | tf_op jit(solution)/shard_map/broadcast_in_dim | solution.py:271
  (25 shorter events, 0.3 us)
Async XLA Ops:
  7.2 48.2 %copy-start = (bf16[1,2048,128]{2,1,0:T(8,128)(2,1)S(1)}, bf16[1,2048,128]{2,1,0:T(8,128)(2,1)}, u32[]{:S(2)}) copy-start(bf16[1,2048,128]{2,1,0:T(8,128)(2,1)} %param.11) | copy-start | bytes 1572868
  7.2 3.9 %copy-start.2 = (bf16[128,8192]{1,0:T(8,128)(2,1)S(1)}, bf16[128,8192]{1,0:T(8,128)(2,1)}, u32[]{:S(2)}) copy-start(bf16[128,8192]{1,0:T(8,128)(2,1)} %param.7) | copy-start | bytes 6291460
  7.2 2.3 %copy-start.7 = (s32[8,512]{1,0:T(8,128)S(1)}, s32[8,512]{1,0:T(8,128)}, u32[]{:S(2)}) copy-start(s32[8,512]{1,0:T(8,128)} %param.9) | copy-start | bytes 49156
  7.2 3.8 %copy-start.6 = (f32[8192]{0:T(1024)S(1)}, f32[8192]{0:T(1024)}, u32[]{:S(2)}) copy-start(f32[8192]{0:T(1024)} %param.8) | copy-start | bytes 98308
  13.2 10.1 %copy-start.5 = (bf16[1,64,2048]{2,1,0:T(8,128)(2,1)S(1)}, bf16[1,64,2048]{2,1,0:T(8,128)(2,1)}, u32[]{:S(2)}) copy-start(bf16[1,64,2048]{2,1,0:T(8,128)(2,1)} %param.12) | copy-start | bytes 786436
  13.2 39.0 %all-to-all-start = ((bf16[32,16,2048]{2,1,0:T(8,128)(2,1)}), bf16[32,16,2048]{2,1,0:T(8,128)(2,1)S(1)}, u32[]{:S(2)}, u32[]{:S(2)}) async-start(bf16[32,16,2048]{2,1,0:T(8,128)(2,1)} %bitcast.47), calls=%async_computation | async-start | bytes 4194304 | tf_op jit(solution)/shard_map/all_to_all | solution.py:213
  21.9 77.3 %reduce-scatter.2.cloned.1.call-start = ((), (), s32[]{:S(2)}) async-start(), calls=%async_computation.2 | async-start | bytes 1179648 | tf_op jit(solution)/shard_map/reduce_scatter | solution.py:266
  52.2 3.2 %copy-start.1 = (bf16[32,16,2048]{2,1,0:T(8,128)(2,1)}, bf16[32,16,2048]{2,1,0:T(8,128)(2,1)S(1)}, u32[]{:S(2)}) copy-start(bf16[32,16,2048]{2,1,0:T(8,128)(2,1)S(1)} %all-to-all-done) | copy-start | bytes 6291460
  56.1 0.7 copy-start.3
  94.0 4.1 %copy-start.4 = (f32[128,2048]{1,0:T(8,128)S(1)}, f32[128,2048]{1,0:T(8,128)}, u32[]{:S(2)}) copy-start(f32[128,2048]{1,0:T(8,128)} %get-tuple-element.6) | copy-start | bytes 3145732
Sparse Core Ops, SparseCore 0:
  54.0 36.7 reduce-scatter.1

commit v14 on v13

--- a/solution.py
+++ b/solution.py
@@ -14,7 +14,7 @@
 
 
 def _tensor_sum_kernel(
-    n1, n2, rows_ref, w_ref, rk_ref, own_rk_ref, gk_ref, gv_ref,
+    n1, n2, rows_ref, w_ref, rk_ref, g_ref,
     kv_out, rk_out, b_out,
     recv_kv, recv_rk, terms, recv_b1, partial, recv_b2, forward, outgoing, across_part, sems, kv_sems,
 ):
@@ -79,7 +79,7 @@
     across_part[...] = product(across)
     own_part = product(me1)
 
-    rk_out[...] = own_rk_ref[...]
+    rk_out[...] = rk_ref[me1]
     for shift, copy in zip(range(1, n1), rk_copies):
         copy.wait_recv()
         rk_out[...] += recv_rk[shift]
@@ -88,11 +88,11 @@
     lane = lax.broadcasted_iota(jnp.int32, xa.shape, 1)
     half = xa.shape[1] // 2
     total = None
-    for g_ref, keep in ((gk_ref, lane < half), (gv_ref, lane >= half)):
+    for which, keep in enumerate((lane < half, lane >= half)):
         part = jnp.where(keep, xa, 0.0)
         high = part.astype(jnp.bfloat16)
         low = (part - high.astype(jnp.float32)).astype(jnp.bfloat16)
-        g = g_ref[...]
+        g = g_ref[which]
         for piece in (high, low):
             term = jnp.dot(g, piece, preferred_element_type=jnp.float32)
             total = term if total is None else total + term
@@ -140,12 +140,12 @@
         copy.wait_send()
 
 
-def tensor_sum(rows, w, rk, own_rk, gk, gv, n2, collective_id):
+def tensor_sum(rows, w, rk, g, n2, collective_id):
     n1 = rk.shape[0]
     tokens = rows.shape[0] // n1
     kv_width = w.shape[1]
     quarter = n2 // 2
-    columns = gk.shape[0]
+    columns = g.shape[1]
     lanes = rk.shape[2]
     block = columns // (n1 * quarter)
     vmem = pl.BlockSpec(memory_space=pltpu.VMEM)
@@ -153,10 +153,10 @@
         functools.partial(_tensor_sum_kernel, n1, n2),
         out_shape=(
             jax.ShapeDtypeStruct((tokens, kv_width), jnp.float32),
-            jax.ShapeDtypeStruct(own_rk.shape, jnp.float32),
+            jax.ShapeDtypeStruct(rk.shape[1:], jnp.float32),
             jax.ShapeDtypeStruct((block, lanes), jnp.float32),
         ),
-        in_specs=[vmem] * 6,
+        in_specs=[vmem] * 4,
         out_specs=(vmem, vmem, vmem),
         scratch_shapes=[
             pltpu.VMEM((n1, tokens, kv_width), jnp.bfloat16),
@@ -172,7 +172,7 @@
             pltpu.SemaphoreType.DMA((2, 3, 4)),
         ],
         compiler_params=pltpu.CompilerParams(collective_id=collective_id, has_side_effects=True),
-    )(rows, w, rk, own_rk, gk, gv)
+    )(rows, w, rk, g)
 
 
 def shards(
@@ -238,7 +238,6 @@
     down_weight = adapter_down_weight[0]
     ranks = jnp.dot(rows, down_weight, preferred_element_type=jnp.float32)
     block = tok_dev // tensors
-    mine = lax.axis_index("tensor") * block
     quarter = dps // 2
     width = kv_width // (dps * tensors)
     grad_t = keyvalue_gradient[0].T.reshape(2, quarter, tensors, width, tok_dev // tensors)
@@ -247,9 +246,7 @@
         rows,
         keyvalue_weight,
         ranks.reshape(tensors, block, ranks.shape[1]),
-        lax.dynamic_slice_in_dim(ranks, mine, block, 0),
-        grad_t[0],
-        grad_t[1],
+        grad_t,
         dps,
         0,
     )

time: 106 us -> 106 us (level)
  local copies, waits for them, and re-layouts: 5.74 us -> 4.37 us
    slice x3 -> x0, local copies, waits for them, and re-layouts: 1.49 us -> none  [the longest x2 0.77 us: shards(): grad_t[1]]
where the time goes in v14:
time: 106 us; the launch traced here: 105 us
  Pallas kernels  37 us (35%)
  blocking collectives  17.5 us (17%)
  between operations  14.2 us (13%)
  waiting for transfers between devices  10.8 us (10%)
  starting transfers between devices  8.76 us (8%)
  matrix products  8.14 us (8%)
  other arithmetic  4.47 us (4%)
  local copies, waits for them, and re-layouts  4.37 us (4%)
    pallas_call x1, Pallas kernels, tensor_sum(): pl.pallas_call(functools.partial(_tensor_sum_kernel, n1, n2), out_shape=(...  37 us
    all_gather x1, blocking collectives, shards(): every_rank = lax.all_gather(rank_gradient, 'tensor', axis=0, tiled=True)  17.5 us
    all_to_all x1, waiting for transfers between devices, shards(): lax.all_to_all(chosen.reshape(trials * tensors, select, normed_input), ('...  10.8 us
    all_to_all x1, starting transfers between devices, shards(): lax.all_to_all(chosen.reshape(trials * tensors, select, normed_input), ('...  8.72 us
    reduce_sum x1, other arithmetic, shards(): row_scale = lax.rsqrt(jnp.mean(raw * raw, axis=1) + norm_eps)  2.23 us
    dot_general x1, matrix products, shards(): jnp.einsum('tsr,rkf->tksf', onehot.reshape(trials, select, pool_dev), res...  2.12 us
  transfers between devices with their start and end apart: 2, of which 1 were waited for; matrix products, arithmetic and copies ran while one was open for 9% of the time, Pallas kernels for 35%

profile of v14, /device:TPU:1, one launch (start us, length us, event | category | flops | bytes accessed | tf_op | source)
XLA Modules:
  0.0 105.3 jit_solution(15386719925448046214)
XLA Ops:
  7.2 2.2 %multiply_reduce_fusion = f32[128]{0:T(128)S(1)} fusion(bf16[128,8192]{1,0:T(8,128)(2,1)} %param.7), kind=kLoop, calls=%fused_computation.2 | loop fusion | flops 3145600 | bytes 2097664 | tf_op jit(solution)/shard_map/reduce_sum | solution.py:209
  9.5 0.1 constant_dynamic-slice_fusion
  9.5 0.1 reshape.98
  9.6 1.2 %gather_fusion = f32[128]{0:T(128)S(1)} fusion(f32[128]{0:T(128)S(1)} %add_rsqrt_fusion, s32[1024]{0:T(1024)S(1)} %pad_clamp_fusion), kind=kCustom, calls=%fused_computation | custom fusion | bytes 1536 | tf_op jit(solution)/shard_map/jit(_take)/gather | solution.py:210
  10.9 0.1 gather.7
  11.0 0.1 and_select_fusion
  11.1 2.1 %multiply_convert_fusion = bf16[8,16,4,2048]{3,1,2,0:T(8,128)(2,1)} fusion(bf16[16,4,8,2048]{3,2,1,0:T(8,128)(2,1)S(1)} %bitcast.47, f32[4,2048]{1,0:T(4,128)S(1)} %mul.55, f32[8,16]{1,0:T(8,128)S(1)} %and_select_fusion, s32[8,16]{1,0:T(8,128)S(1)} %constant_dynamic-slice_fusion), kind=kOutput, calls=%fused_computation.1 | convolution fusion | flops 271597568 | bytes 4228096 | tf_op jit(solution)/shard_map/tsr,rkf->tksf/dot_general | solution.py:202
  13.2 8.7 %all-to-all-start = ((bf16[32,16,2048]{2,1,0:T(8,128)(2,1)}), bf16[32,16,2048]{2,1,0:T(8,128)(2,1)S(1)}, u32[]{:S(2)}, u32[]{:S(2)}) async-start(bf16[32,16,2048]{2,1,0:T(8,128)(2,1)} %bitcast.48), calls=%async_computation | async-start | bytes 4194304 | tf_op jit(solution)/shard_map/all_to_all | solution.py:213
  21.9 0.0 reduce-scatter.2.cloned.1.call-start
  22.0 1.3 %copy.14 = bf16[1,128,2048]{1,2,0:T(8,128)(2,1)S(1)} copy(bf16[1,128,2048]{2,1,0:T(8,128)(2,1)} %param.13) | data formatting | bytes 1048576 | tf_op args[6]
  23.3 0.3 fusion.7
  23.6 0.3 fusion.5
  23.8 0.1 fusion.15
  23.9 17.5 %all_gather.3 = bf16[512,128]{1,0:T(8,128)(2,1)S(1)} all-gather(bf16[128,128]{1,0:T(8,128)(2,1)S(1)} %fusion.15), channel_id=1, replica_groups=mesh['trial'=8,'dp'=8,'tensor'=4] {'tensor'}, dimensions={0}, use_global_device_ids=true | all-gather | bytes 163840 | tf_op jit(solution)/shard_map/all_gather | solution.py:233
  41.5 10.8 %all-to-all-done = bf16[32,16,2048]{2,1,0:T(8,128)(2,1)S(1)} async-done(((bf16[32,16,2048]{2,1,0:T(8,128)(2,1)}), bf16[32,16,2048]{2,1,0:T(8,128)(2,1)S(1)}, u32[]{:S(2)}, u32[]{:S(2)}) %all-to-all-start) | async-done | bytes 2097184 | tf_op jit(solution)/shard_map/all_to_all | solution.py:213
  52.2 1.6 %fusion.22 = f32[128,2048]{1,0:T(8,128)} fusion(bf16[512,128]{1,0:T(8,128)(2,1)S(1)} %all_gather.3, bf16[512,2048]{1,0:T(8,128)(2,1)S(1)} %bitcast.43), kind=kOutput, calls=%fused_computation.35 | convolution fusion | flops 268435456 | bytes 3276800 | tf_op jit(solution)/shard_map/dot_general | solution.py:234
  53.9 0.8 copy.15
  54.8 1.4 %fusion.3.rk_ref = f32[4,128,128]{2,1,0:T(8,128)} fusion(bf16[4,128,2048]{2,1,0:T(8,128)(2,1)S(1)} %bitcast.44, bf16[1,2048,128]{2,1,0:T(8,128)(2,1)S(1)} %copy-done), kind=kOutput, calls=%fused_computation.8 | convolution fusion | flops 268435456 | bytes 2883584 | tf_op jit(solution)/shard_map/dot_general | solution.py:239
  56.2 37.0 %shard_map.94 = (f32[128,2048]{1,0:T(8,128)}, f32[128,128]{1,0:T(8,128)}, f32[64,128]{1,0:T(8,128)}) custom-call(bf16[512,2048]{1,0:T(8,128)(2,1)} %bitcast.45, bf16[2048,2048]{1,0:T(8,128)(2,1)} %w_ref.1, f32[4,128,128]{2,1,0:T(8,128)} %fusion.3.rk_ref, bf16[2,1024,128]{2,1,0:T(8,128)(2,1)} %bitcast.46), custom_call_target="tpu_custom_call" | custom-call | tf_op jit(solution)/shard_map/pallas_call | solution.py:152
  93.2 0.9 multiply_bitcast_fusion
  94.1 0.7 copy.16
  94.8 1.3 %fusion.10 = f32[128,1024]{1,0:T(8,128)S(1)} fusion(bf16[64,2048]{1,0:T(8,128)(2,1)S(1)} %bitcast.54, f32[128,128]{1,0:T(8,128)} %get-tuple-element.7), kind=kOutput, calls=%fused_computation.15 | convolution fusion | flops 100663296 | bytes 720896 | tf_op jit(solution)/shard_map/dot_general | solution.py:256
  96.1 1.2 %fusion.13 = f32[128,1024]{1,0:T(8,128)S(1)} fusion(bf16[64,2048]{1,0:T(8,128)(2,1)S(1)} %bitcast.55, f32[128,128]{1,0:T(8,128)} %get-tuple-element.7), kind=kOutput, calls=%fused_computation.18 | convolution fusion | flops 100663296 | bytes 720896 | tf_op jit(solution)/shard_map/dot_general | solution.py:253
  97.3 1.1 %fusion.2 = f32[1,128,2048]{2,1,0:T(8,128)} fusion(f32[128,2048]{1,0:T(8,128)S(1)} %copy-done.3, f32[128,1024]{1,0:T(8,128)S(1)} %fusion.10, f32[128,1024]{1,0:T(8,128)S(1)} %fusion.13), kind=kLoop, calls=%fused_computation.7 | loop fusion | flops 786432 | bytes 3145728 | tf_op jit(solution)/shard_map/broadcast_in_dim | solution.py:268
  (20 shorter events, 0.1 us)
Async XLA Ops:
  7.2 47.6 %copy-start = (bf16[1,2048,128]{2,1,0:T(8,128)(2,1)S(1)}, bf16[1,2048,128]{2,1,0:T(8,128)(2,1)}, u32[]{:S(2)}) copy-start(bf16[1,2048,128]{2,1,0:T(8,128)(2,1)} %param.11) | copy-start | bytes 1572868
  7.2 3.9 %copy-start.2 = (bf16[128,8192]{1,0:T(8,128)(2,1)S(1)}, bf16[128,8192]{1,0:T(8,128)(2,1)}, u32[]{:S(2)}) copy-start(bf16[128,8192]{1,0:T(8,128)(2,1)} %param.7) | copy-start | bytes 6291460
  7.2 2.3 %copy-start.6 = (s32[8,512]{1,0:T(8,128)S(1)}, s32[8,512]{1,0:T(8,128)}, u32[]{:S(2)}) copy-start(s32[8,512]{1,0:T(8,128)} %param.9) | copy-start | bytes 49156
  7.2 3.8 %copy-start.5 = (f32[8192]{0:T(1024)S(1)}, f32[8192]{0:T(1024)}, u32[]{:S(2)}) copy-start(f32[8192]{0:T(1024)} %param.8) | copy-start | bytes 98308
  13.2 10.1 %copy-start.4 = (bf16[1,64,2048]{2,1,0:T(8,128)(2,1)S(1)}, bf16[1,64,2048]{2,1,0:T(8,128)(2,1)}, u32[]{:S(2)}) copy-start(bf16[1,64,2048]{2,1,0:T(8,128)(2,1)} %param.12) | copy-start | bytes 786436
  13.2 39.0 %all-to-all-start = ((bf16[32,16,2048]{2,1,0:T(8,128)(2,1)}), bf16[32,16,2048]{2,1,0:T(8,128)(2,1)S(1)}, u32[]{:S(2)}, u32[]{:S(2)}) async-start(bf16[32,16,2048]{2,1,0:T(8,128)(2,1)} %bitcast.48), calls=%async_computation | async-start | bytes 4194304 | tf_op jit(solution)/shard_map/all_to_all | solution.py:213
  21.9 76.5 %reduce-scatter.2.cloned.1.call-start = ((), (), s32[]{:S(2)}) async-start(), calls=%async_computation.2 | async-start | bytes 1179648 | tf_op jit(solution)/shard_map/reduce_scatter | solution.py:263
  52.2 2.5 %copy-start.1 = (bf16[32,16,2048]{2,1,0:T(8,128)(2,1)}, bf16[32,16,2048]{2,1,0:T(8,128)(2,1)S(1)}, u32[]{:S(2)}) copy-start(bf16[32,16,2048]{2,1,0:T(8,128)(2,1)S(1)} %all-to-all-done) | copy-start | bytes 6291460
  93.2 4.1 %copy-start.3 = (f32[128,2048]{1,0:T(8,128)S(1)}, f32[128,2048]{1,0:T(8,128)}, u32[]{:S(2)}) copy-start(f32[128,2048]{1,0:T(8,128)} %get-tuple-element.6) | copy-start | bytes 3145732
Sparse Core Ops, SparseCore 0:
  54.0 36.6 reduce-scatter.1

commit v15 on v14

--- a/solution.py
+++ b/solution.py
@@ -131,10 +131,15 @@
         rows = pl.ds(p * step, step)
         copy.wait_recv()
         kv_out[rows, :] += recv_kv[2, rows, :].astype(jnp.float32)
-    b_out[...] = partial[lax.rem(me2, quarter)]
+    reduced = partial[lax.rem(me2, quarter)]
     for shift, copy in zip(range(1, n2), b2_copies):
         copy.wait_recv()
-        b_out[...] += recv_b2[shift]
+        reduced = reduced + recv_b2[shift]
+    by_rank = reduced.T
+    ranks_here = b_out.shape[0]
+    b_out[...] = adapter_scale * jnp.where(
+        me2 < quarter, by_rank[:ranks_here, :], by_rank[ranks_here:, :]
+    )
 
     for copy in rk_copies + diagonal_copies + own_copies + forward_copies + b1_copies + b2_copies:
         copy.wait_send()
@@ -154,7 +159,7 @@
         out_shape=(
             jax.ShapeDtypeStruct((tokens, kv_width), jnp.float32),
             jax.ShapeDtypeStruct(rk.shape[1:], jnp.float32),
-            jax.ShapeDtypeStruct((block, lanes), jnp.float32),
+            jax.ShapeDtypeStruct((lanes // 2, block), jnp.float32),
         ),
         in_specs=[vmem] * 4,
         out_specs=(vmem, vmem, vmem),
@@ -262,9 +267,7 @@
 
     grad_a = lax.psum_scatter(grad_a_term, "dp", scatter_dimension=0, tiled=True)
 
-    grad_b = adapter_scale * jnp.where(
-        lax.axis_index("dp") < quarter, up_block[:, :rank_index], up_block[:, rank_index:]
-    ).T
+    grad_b = up_block
     return (keyvalue_output[None], grad_a[None], grad_b[None])
 
 

time: 106 us -> 105 us (level)
  transfers between devices with their start and end apart: 2 -> 2, of which waited for: 1 -> 1; matrix products, arithmetic and copies ran while one was open for 9% -> 7% of each run, Pallas kernels for 35% -> 35%
where the time goes in v15:
time: 105 us; the launch traced here: 104 us
  Pallas kernels  37 us (35%)
  blocking collectives  17.5 us (17%)
  between operations  14.2 us (14%)
  waiting for transfers between devices  10.8 us (10%)
  starting transfers between devices  8.76 us (8%)
  matrix products  8.22 us (8%)
  local copies, waits for them, and re-layouts  4.29 us (4%)
  other arithmetic  3.52 us (3%)
    pallas_call x1, Pallas kernels, tensor_sum(): pl.pallas_call(functools.partial(_tensor_sum_kernel, n1, n2), out_shape=(...  37 us
    all_gather x1, blocking collectives, shards(): every_rank = lax.all_gather(rank_gradient, 'tensor', axis=0, tiled=True)  17.5 us
    all_to_all x1, waiting for transfers between devices, shards(): lax.all_to_all(chosen.reshape(trials * tensors, select, normed_input), ('...  10.8 us
    all_to_all x1, starting transfers between devices, shards(): lax.all_to_all(chosen.reshape(trials * tensors, select, normed_input), ('...  8.72 us
    reduce_sum x1, other arithmetic, shards(): row_scale = lax.rsqrt(jnp.mean(raw * raw, axis=1) + norm_eps)  2.23 us
    dot_general x1, matrix products, shards(): jnp.einsum('tsr,rkf->tksf', onehot.reshape(trials, select, pool_dev), res...  2.11 us
  transfers between devices with their start and end apart: 2, of which 1 were waited for; matrix products, arithmetic and copies ran while one was open for 7% of the time, Pallas kernels for 35%

profile of v15, /device:TPU:1, one launch (start us, length us, event | category | flops | bytes accessed | tf_op | source)
XLA Modules:
  0.0 104.4 jit_solution(8891620136158441442)
XLA Ops:
  7.2 2.2 %multiply_reduce_fusion = f32[128]{0:T(128)S(1)} fusion(bf16[128,8192]{1,0:T(8,128)(2,1)} %param.7), kind=kLoop, calls=%fused_computation.2 | loop fusion | flops 3145600 | bytes 2097664 | tf_op jit(solution)/shard_map/reduce_sum | solution.py:214
  9.5 0.1 constant_dynamic-slice_fusion
  9.5 0.1 reshape.98
  9.6 1.2 %gather_fusion = f32[128]{0:T(128)S(1)} fusion(f32[128]{0:T(128)S(1)} %add_rsqrt_fusion, s32[1024]{0:T(1024)S(1)} %pad_clamp_fusion), kind=kCustom, calls=%fused_computation | custom fusion | bytes 1536 | tf_op jit(solution)/shard_map/jit(_take)/gather | solution.py:215
  10.9 0.1 gather.7
  11.0 0.1 and_select_fusion
  11.1 2.1 %multiply_convert_fusion = bf16[8,16,4,2048]{3,1,2,0:T(8,128)(2,1)} fusion(bf16[16,4,8,2048]{3,2,1,0:T(8,128)(2,1)S(1)} %bitcast.44, f32[4,2048]{1,0:T(4,128)S(1)} %mul.46, f32[8,16]{1,0:T(8,128)S(1)} %and_select_fusion, s32[8,16]{1,0:T(8,128)S(1)} %constant_dynamic-slice_fusion), kind=kOutput, calls=%fused_computation.1 | convolution fusion | flops 271597568 | bytes 4228096 | tf_op jit(solution)/shard_map/tsr,rkf->tksf/dot_general | solution.py:207
  13.2 8.7 %all-to-all-start = ((bf16[32,16,2048]{2,1,0:T(8,128)(2,1)}), bf16[32,16,2048]{2,1,0:T(8,128)(2,1)S(1)}, u32[]{:S(2)}, u32[]{:S(2)}) async-start(bf16[32,16,2048]{2,1,0:T(8,128)(2,1)} %bitcast.45), calls=%async_computation | async-start | bytes 4194304 | tf_op jit(solution)/shard_map/all_to_all | solution.py:218
  21.9 0.0 reduce-scatter.2.cloned.1.call-start
  22.0 1.3 %copy.13 = bf16[1,128,2048]{1,2,0:T(8,128)(2,1)S(1)} copy(bf16[1,128,2048]{2,1,0:T(8,128)(2,1)} %param.13) | data formatting | bytes 1048576 | tf_op args[6]
  23.3 0.3 fusion.7
  23.6 0.3 fusion.5
  23.8 0.1 fusion.15
  23.9 17.5 %all_gather.3 = bf16[512,128]{1,0:T(8,128)(2,1)S(1)} all-gather(bf16[128,128]{1,0:T(8,128)(2,1)S(1)} %fusion.15), channel_id=1, replica_groups=mesh['trial'=8,'dp'=8,'tensor'=4] {'tensor'}, dimensions={0}, use_global_device_ids=true | all-gather | bytes 163840 | tf_op jit(solution)/shard_map/all_gather | solution.py:238
  41.4 10.8 %all-to-all-done = bf16[32,16,2048]{2,1,0:T(8,128)(2,1)S(1)} async-done(((bf16[32,16,2048]{2,1,0:T(8,128)(2,1)}), bf16[32,16,2048]{2,1,0:T(8,128)(2,1)S(1)}, u32[]{:S(2)}, u32[]{:S(2)}) %all-to-all-start) | async-done | bytes 2097184 | tf_op jit(solution)/shard_map/all_to_all | solution.py:218
  52.2 1.6 %fusion.22 = f32[128,2048]{1,0:T(8,128)} fusion(bf16[512,128]{1,0:T(8,128)(2,1)S(1)} %all_gather.3, bf16[512,2048]{1,0:T(8,128)(2,1)S(1)} %bitcast.40), kind=kOutput, calls=%fused_computation.34 | convolution fusion | flops 268435456 | bytes 3276800 | tf_op jit(solution)/shard_map/dot_general | solution.py:239
  53.9 0.0 reduce-scatter.2.cloned.1.call-update
  53.9 0.8 copy.14
  54.7 1.4 %fusion.3.rk_ref = f32[4,128,128]{2,1,0:T(8,128)} fusion(bf16[4,128,2048]{2,1,0:T(8,128)(2,1)S(1)} %bitcast.41, bf16[1,2048,128]{2,1,0:T(8,128)(2,1)S(1)} %copy-done), kind=kOutput, calls=%fused_computation.8 | convolution fusion | flops 268435456 | bytes 2883584 | tf_op jit(solution)/shard_map/dot_general | solution.py:244
  56.1 37.0 %shard_map.94 = (f32[128,2048]{1,0:T(8,128)}, f32[128,128]{1,0:T(8,128)}, f32[64,64]{1,0:T(8,128)}) custom-call(bf16[512,2048]{1,0:T(8,128)(2,1)} %bitcast.42, bf16[2048,2048]{1,0:T(8,128)(2,1)} %w_ref.1, f32[4,128,128]{2,1,0:T(8,128)} %fusion.3.rk_ref, bf16[2,1024,128]{2,1,0:T(8,128)(2,1)} %bitcast.43), custom_call_target="tpu_custom_call" | custom-call | tf_op jit(solution)/shard_map/pallas_call | solution.py:157
  93.2 1.3 %fusion.10 = f32[128,1024]{1,0:T(8,128)S(1)} fusion(bf16[64,2048]{1,0:T(8,128)(2,1)S(1)} %bitcast.51, f32[128,128]{1,0:T(8,128)} %get-tuple-element.7), kind=kOutput, calls=%fused_computation.15 | convolution fusion | flops 100663296 | bytes 720896 | tf_op jit(solution)/shard_map/dot_general | solution.py:261
  94.6 1.2 %fusion.13 = f32[128,1024]{1,0:T(8,128)S(1)} fusion(bf16[64,2048]{1,0:T(8,128)(2,1)S(1)} %bitcast.52, f32[128,128]{1,0:T(8,128)} %get-tuple-element.7), kind=kOutput, calls=%fused_computation.18 | convolution fusion | flops 100663296 | bytes 720896 | tf_op jit(solution)/shard_map/dot_general | solution.py:258
  95.8 1.1 %fusion.2 = f32[1,128,2048]{2,1,0:T(8,128)} fusion(f32[128,2048]{1,0:T(8,128)S(1)} %copy-done.3, f32[128,1024]{1,0:T(8,128)S(1)} %fusion.10, f32[128,1024]{1,0:T(8,128)S(1)} %fusion.13), kind=kLoop, calls=%fused_computation.7 | loop fusion | flops 786432 | bytes 3145728 | tf_op jit(solution)/shard_map/broadcast_in_dim | solution.py:271
  96.9 0.6 copy.22
  (21 shorter events, 0.1 us)
Async XLA Ops:
  7.2 47.6 %copy-start = (bf16[1,2048,128]{2,1,0:T(8,128)(2,1)S(1)}, bf16[1,2048,128]{2,1,0:T(8,128)(2,1)}, u32[]{:S(2)}) copy-start(bf16[1,2048,128]{2,1,0:T(8,128)(2,1)} %param.11) | copy-start | bytes 1572868
  7.2 3.9 %copy-start.2 = (bf16[128,8192]{1,0:T(8,128)(2,1)S(1)}, bf16[128,8192]{1,0:T(8,128)(2,1)}, u32[]{:S(2)}) copy-start(bf16[128,8192]{1,0:T(8,128)(2,1)} %param.7) | copy-start | bytes 6291460
  7.2 2.3 %copy-start.7 = (s32[8,512]{1,0:T(8,128)S(1)}, s32[8,512]{1,0:T(8,128)}, u32[]{:S(2)}) copy-start(s32[8,512]{1,0:T(8,128)} %param.9) | copy-start | bytes 49156
  7.2 3.8 %copy-start.5 = (f32[8192]{0:T(1024)S(1)}, f32[8192]{0:T(1024)}, u32[]{:S(2)}) copy-start(f32[8192]{0:T(1024)} %param.8) | copy-start | bytes 98308
  13.2 10.1 %copy-start.4 = (bf16[1,64,2048]{2,1,0:T(8,128)(2,1)S(1)}, bf16[1,64,2048]{2,1,0:T(8,128)(2,1)}, u32[]{:S(2)}) copy-start(bf16[1,64,2048]{2,1,0:T(8,128)(2,1)} %param.12) | copy-start | bytes 786436
  13.2 39.0 %all-to-all-start = ((bf16[32,16,2048]{2,1,0:T(8,128)(2,1)}), bf16[32,16,2048]{2,1,0:T(8,128)(2,1)S(1)}, u32[]{:S(2)}, u32[]{:S(2)}) async-start(bf16[32,16,2048]{2,1,0:T(8,128)(2,1)} %bitcast.45), calls=%async_computation | async-start | bytes 4194304 | tf_op jit(solution)/shard_map/all_to_all | solution.py:218
  21.9 75.0 %reduce-scatter.2.cloned.1.call-start = ((), (), s32[]{:S(2)}) async-start(), calls=%async_computation.2 | async-start | bytes 1179648 | tf_op jit(solution)/shard_map/reduce_scatter | solution.py:268
  52.2 2.5 %copy-start.1 = (bf16[32,16,2048]{2,1,0:T(8,128)(2,1)}, bf16[32,16,2048]{2,1,0:T(8,128)(2,1)S(1)}, u32[]{:S(2)}) copy-start(bf16[32,16,2048]{2,1,0:T(8,128)(2,1)S(1)} %all-to-all-done) | copy-start | bytes 6291460
  93.2 2.6 %copy-start.3 = (f32[128,2048]{1,0:T(8,128)S(1)}, f32[128,2048]{1,0:T(8,128)}, u32[]{:S(2)}) copy-start(f32[128,2048]{1,0:T(8,128)} %get-tuple-element.6) | copy-start | bytes 3145732
  94.6 2.3 %copy-start.6 = (f32[64,64]{1,0:T(8,128)S(1)}, f32[64,64]{1,0:T(8,128)}, u32[]{:S(2)}) copy-start(f32[64,64]{1,0:T(8,128)} %get-tuple-element.8) | copy-start | bytes 49156
Sparse Core Ops, SparseCore 0:
  54.0 36.6 reduce-scatter.1

commit v16 on v15

--- a/solution.py
+++ b/solution.py
@@ -255,14 +255,11 @@
         dps,
         0,
     )
-    adapter_key = jnp.dot(
-        local_rank_rows[:, :rank_index], up_weight[:, :keyvalue_half], precision=highest_precision
-    )
-    adapter_value = jnp.dot(
-        local_rank_rows[:, rank_index:], up_weight[:, keyvalue_half:], precision=highest_precision
-    )
-    keyvalue_output = frozen_output_local + adapter_scale * jnp.concatenate(
-        [adapter_key, adapter_value], axis=1
+    block_up = jnp.zeros((2 * rank_index, kv_width), jnp.float32)
+    block_up = block_up.at[:rank_index, :keyvalue_half].set(up_weight[:, :keyvalue_half])
+    block_up = block_up.at[rank_index:, keyvalue_half:].set(up_weight[:, keyvalue_half:])
+    keyvalue_output = frozen_output_local + adapter_scale * jnp.dot(
+        local_rank_rows, block_up, precision=highest_precision
     )
 
     grad_a = lax.psum_scatter(grad_a_term, "dp", scatter_dimension=0, tiled=True)

time: 105 us -> 106 us (level)
  local copies, waits for them, and re-layouts: 4.29 us -> 6.09 us
  other arithmetic: 3.52 us -> 2.45 us
    scatter x0 -> x2, local copies, waits for them, and re-layouts: none -> 1.79 us  [the longest x1 1.06 us: shards(): block_up.at[:rank_index, :keyvalue_half].set(up_weight[:, :keyvalue_half])]
    broadcast_in_dim x1 -> x0, other arithmetic: 1.11 us -> none  [shards(): return (keyvalue_output[None], grad_a[None], grad_b[None])]
    dot_general x2 -> x1, matrix products: 2.54 us -> 3.53 us  [shards(): jnp.dot(local_rank_rows, block_up, precision=highest_precision)]
  transfers between devices with their start and end apart: 2 -> 2, of which waited for: 1 -> 1; matrix products, arithmetic and copies ran while one was open for 7% -> 9% of each run, Pallas kernels for 35% -> 35%
where the time goes in v16:
time: 106 us
  Pallas kernels  37.1 us (35%)
  blocking collectives  17.5 us (17%)
  between operations  14.2 us (13%)
  waiting for transfers between devices  10.8 us (10%)
  matrix products  9.23 us (9%)
  starting transfers between devices  8.76 us (8%)
  local copies, waits for them, and re-layouts  6.09 us (6%)
  other arithmetic  2.45 us (2%)
    pallas_call x1, Pallas kernels, tensor_sum(): pl.pallas_call(functools.partial(_tensor_sum_kernel, n1, n2), out_shape=(...  37.1 us
    all_gather x1, blocking collectives, shards(): every_rank = lax.all_gather(rank_gradient, 'tensor', axis=0, tiled=True)  17.5 us
    all_to_all x1, waiting for transfers between devices, shards(): lax.all_to_all(chosen.reshape(trials * tensors, select, normed_input), ('...  10.8 us
    all_to_all x1, starting transfers between devices, shards(): lax.all_to_all(chosen.reshape(trials * tensors, select, normed_input), ('...  8.72 us
    dot_general x1, matrix products, shards(): jnp.dot(local_rank_rows, block_up, precision=highest_precision)  3.53 us
    reduce_sum x1, other arithmetic, shards(): row_scale = lax.rsqrt(jnp.mean(raw * raw, axis=1) + norm_eps)  2.23 us
  transfers between devices with their start and end apart: 2, of which 1 were waited for; matrix products, arithmetic and copies ran while one was open for 9% of the time, Pallas kernels for 35%

profile of v16, /device:TPU:1, one launch (start us, length us, event | category | flops | bytes accessed | tf_op | source)
XLA Modules:
  0.0 106.1 jit_solution(15326421709869038184)
XLA Ops:
  7.2 2.2 %multiply_reduce_fusion = f32[128]{0:T(128)S(1)} fusion(bf16[128,8192]{1,0:T(8,128)(2,1)} %param.11), kind=kLoop, calls=%fused_computation.2 | loop fusion | flops 3145600 | bytes 2097664 | tf_op jit(solution)/shard_map/reduce_sum | solution.py:214
  9.5 0.1 constant_dynamic-slice_fusion
  9.5 0.1 reshape.159
  9.6 1.2 %gather_fusion = f32[128]{0:T(128)S(1)} fusion(f32[128]{0:T(128)S(1)} %add_rsqrt_fusion, s32[1024]{0:T(1024)S(1)} %pad_clamp_fusion), kind=kCustom, calls=%fused_computation | custom fusion | bytes 1536 | tf_op jit(solution)/shard_map/jit(_take)/gather | solution.py:215
  10.9 0.1 gather.7
  11.0 0.1 and_select_fusion
  11.1 2.1 %multiply_convert_fusion = bf16[8,16,4,2048]{3,1,2,0:T(8,128)(2,1)} fusion(bf16[16,4,8,2048]{3,2,1,0:T(8,128)(2,1)S(1)} %bitcast.47, f32[4,2048]{1,0:T(4,128)S(1)} %mul.46, f32[8,16]{1,0:T(8,128)S(1)} %and_select_fusion, s32[8,16]{1,0:T(8,128)S(1)} %constant_dynamic-slice_fusion), kind=kOutput, calls=%fused_computation.1 | convolution fusion | flops 271597568 | bytes 4228096 | tf_op jit(solution)/shard_map/tsr,rkf->tksf/dot_general | solution.py:207
  13.2 8.7 %all-to-all-start = ((bf16[32,16,2048]{2,1,0:T(8,128)(2,1)}), bf16[32,16,2048]{2,1,0:T(8,128)(2,1)S(1)}, u32[]{:S(2)}, u32[]{:S(2)}) async-start(bf16[32,16,2048]{2,1,0:T(8,128)(2,1)} %bitcast.48), calls=%async_computation | async-start | bytes 4194304 | tf_op jit(solution)/shard_map/all_to_all | solution.py:218
  21.9 0.0 reduce-scatter.2.cloned.1.call-start
  22.0 1.3 %copy.13 = bf16[1,128,2048]{1,2,0:T(8,128)(2,1)S(1)} copy(bf16[1,128,2048]{2,1,0:T(8,128)(2,1)} %param.17) | data formatting | bytes 1048576 | tf_op args[6]
  23.3 0.3 fusion.7
  23.6 0.3 fusion.5
  23.8 0.1 fusion.11
  23.9 17.5 %all_gather.3 = bf16[512,128]{1,0:T(8,128)(2,1)S(1)} all-gather(bf16[128,128]{1,0:T(8,128)(2,1)S(1)} %fusion.11), channel_id=1, replica_groups=mesh['trial'=8,'dp'=8,'tensor'=4] {'tensor'}, dimensions={0}, use_global_device_ids=true | all-gather | bytes 163840 | tf_op jit(solution)/shard_map/all_gather | solution.py:238
  41.5 10.8 %all-to-all-done = bf16[32,16,2048]{2,1,0:T(8,128)(2,1)S(1)} async-done(((bf16[32,16,2048]{2,1,0:T(8,128)(2,1)}), bf16[32,16,2048]{2,1,0:T(8,128)(2,1)S(1)}, u32[]{:S(2)}, u32[]{:S(2)}) %all-to-all-start) | async-done | bytes 2097184 | tf_op jit(solution)/shard_map/all_to_all | solution.py:218
  52.2 1.6 %fusion.16 = f32[128,2048]{1,0:T(8,128)} fusion(bf16[512,128]{1,0:T(8,128)(2,1)S(1)} %all_gather.3, bf16[512,2048]{1,0:T(8,128)(2,1)S(1)} %bitcast.43), kind=kOutput, calls=%fused_computation.30 | convolution fusion | flops 268435456 | bytes 3276800 | tf_op jit(solution)/shard_map/dot_general | solution.py:239
  53.9 0.0 reduce-scatter.2.cloned.1.call-update
  54.0 0.8 copy.14
  54.8 1.1 %scatter.6 = f32[128,2048]{1,0:T(8,128)} pad(f32[64,1024]{1,0:T(8,128)S(1)} %slice.69, f32[]{:T(128)} %constant.90.clone.1), padding=0_64x0_1024 | pad | bytes 1310724 | tf_op jit(solution)/shard_map/scatter | solution.py:259
  55.9 0.7 slice_dynamic-update-slice_fusion
  56.6 1.4 %fusion.3.rk_ref = f32[4,128,128]{2,1,0:T(8,128)} fusion(bf16[4,128,2048]{2,1,0:T(8,128)(2,1)S(1)} %bitcast.44, bf16[1,2048,128]{2,1,0:T(8,128)(2,1)S(1)} %copy-done), kind=kOutput, calls=%fused_computation.8 | convolution fusion | flops 268435456 | bytes 2883584 | tf_op jit(solution)/shard_map/dot_general | solution.py:244
  58.0 37.1 %shard_map.94 = (f32[128,2048]{1,0:T(8,128)}, f32[128,128]{1,0:T(8,128)}, f32[64,64]{1,0:T(8,128)}) custom-call(bf16[512,2048]{1,0:T(8,128)(2,1)} %bitcast.45, bf16[2048,2048]{1,0:T(8,128)(2,1)} %w_ref.1, f32[4,128,128]{2,1,0:T(8,128)} %fusion.3.rk_ref, bf16[2,1024,128]{2,1,0:T(8,128)(2,1)} %bitcast.46), custom_call_target="tpu_custom_call" | custom-call | tf_op jit(solution)/shard_map/pallas_call | solution.py:157
  95.1 3.5 %fusion.1 = f32[1,128,2048]{2,1,0:T(8,128)} fusion(f32[128,2048]{1,0:T(8,128)} %get-tuple-element.30, f32[128,128]{1,0:T(8,128)} %get-tuple-element.31, f32[128,2048]{1,0:T(8,128)} %slice_dynamic-update-slice_fusion), kind=kOutput, calls=%fused_computation.5 | convolution fusion | flops 403177472 | bytes 3211264 | tf_op jit(solution)/shard_map/dot_general | solution.py:261
  98.7 0.6 copy.23
  (21 shorter events, 0.1 us)
Async XLA Ops:
  7.2 49.4 %copy-start = (bf16[1,2048,128]{2,1,0:T(8,128)(2,1)S(1)}, bf16[1,2048,128]{2,1,0:T(8,128)(2,1)}, u32[]{:S(2)}) copy-start(bf16[1,2048,128]{2,1,0:T(8,128)(2,1)} %param.15) | copy-start | bytes 1572868
  7.2 3.9 %copy-start.2 = (bf16[128,8192]{1,0:T(8,128)(2,1)S(1)}, bf16[128,8192]{1,0:T(8,128)(2,1)}, u32[]{:S(2)}) copy-start(bf16[128,8192]{1,0:T(8,128)(2,1)} %param.11) | copy-start | bytes 6291460
  7.2 2.3 %copy-start.6 = (s32[8,512]{1,0:T(8,128)S(1)}, s32[8,512]{1,0:T(8,128)}, u32[]{:S(2)}) copy-start(s32[8,512]{1,0:T(8,128)} %param.13) | copy-start | bytes 49156
  7.2 3.8 %copy-start.4 = (f32[8192]{0:T(1024)S(1)}, f32[8192]{0:T(1024)}, u32[]{:S(2)}) copy-start(f32[8192]{0:T(1024)} %param.12) | copy-start | bytes 98308
  13.2 10.1 %copy-start.3 = (bf16[1,64,2048]{2,1,0:T(8,128)(2,1)S(1)}, bf16[1,64,2048]{2,1,0:T(8,128)(2,1)}, u32[]{:S(2)}) copy-start(bf16[1,64,2048]{2,1,0:T(8,128)(2,1)} %param.16) | copy-start | bytes 786436
  13.2 39.0 %all-to-all-start = ((bf16[32,16,2048]{2,1,0:T(8,128)(2,1)}), bf16[32,16,2048]{2,1,0:T(8,128)(2,1)S(1)}, u32[]{:S(2)}, u32[]{:S(2)}) async-start(bf16[32,16,2048]{2,1,0:T(8,128)(2,1)} %bitcast.48), calls=%async_computation | async-start | bytes 4194304 | tf_op jit(solution)/shard_map/all_to_all | solution.py:218
  21.9 76.7 %reduce-scatter.2.cloned.1.call-start = ((), (), s32[]{:S(2)}) async-start(), calls=%async_computation.2 | async-start | bytes 1179648 | tf_op jit(solution)/shard_map/reduce_scatter | solution.py:265
  52.2 4.4 %copy-start.1 = (bf16[32,16,2048]{2,1,0:T(8,128)(2,1)}, bf16[32,16,2048]{2,1,0:T(8,128)(2,1)S(1)}, u32[]{:S(2)}) copy-start(bf16[32,16,2048]{2,1,0:T(8,128)(2,1)S(1)} %all-to-all-done) | copy-start | bytes 6291460
  95.1 3.5 %copy-start.5 = (f32[64,64]{1,0:T(8,128)S(1)}, f32[64,64]{1,0:T(8,128)}, u32[]{:S(2)}) copy-start(f32[64,64]{1,0:T(8,128)} %get-tuple-element.32) | copy-start | bytes 49156
Sparse Core Ops, SparseCore 0:
  54.0 35.8 reduce-scatter.1

commit v17 on v15

--- a/solution.py
+++ b/solution.py
@@ -14,9 +14,9 @@
 
 
 def _tensor_sum_kernel(
-    n1, n2, rows_ref, w_ref, rk_ref, g_ref,
+    n1, n2, rows_ref, w_ref, dw_ref, g_ref,
     kv_out, rk_out, b_out,
-    recv_kv, recv_rk, terms, recv_b1, partial, recv_b2, forward, outgoing, across_part, sems, kv_sems,
+    recv_kv, recv_rk, terms, recv_b1, partial, recv_b2, forward, outgoing, across_part, rk_ref, sems, kv_sems,
 ):
     me1 = lax.axis_index("tensor")
     me2 = lax.axis_index("dp")
@@ -29,6 +29,7 @@
         pl.semaphore_signal(barrier, inc=1, device_id=first(lax.rem(me1 + shift, n1)), device_id_type=MESH)
     for shift in range(1, n2):
         pl.semaphore_signal(barrier, inc=1, device_id=second(lax.rem(me2 + shift, n2)), device_id_type=MESH)
+    rk_ref[...] = jnp.dot(rows_ref[...], dw_ref[...], preferred_element_type=jnp.float32).reshape(rk_ref.shape)
     pl.semaphore_wait(barrier, n1 + n2 - 2)
 
     def send(src_ref, dst_ref, row, shift, device):
@@ -145,27 +146,26 @@
         copy.wait_send()
 
 
-def tensor_sum(rows, w, rk, g, n2, collective_id):
-    n1 = rk.shape[0]
+def tensor_sum(rows, w, dw, g, n1, n2, collective_id):
     tokens = rows.shape[0] // n1
     kv_width = w.shape[1]
     quarter = n2 // 2
     columns = g.shape[1]
-    lanes = rk.shape[2]
+    lanes = dw.shape[1]
     block = columns // (n1 * quarter)
     vmem = pl.BlockSpec(memory_space=pltpu.VMEM)
     return pl.pallas_call(
         functools.partial(_tensor_sum_kernel, n1, n2),
         out_shape=(
             jax.ShapeDtypeStruct((tokens, kv_width), jnp.float32),
-            jax.ShapeDtypeStruct(rk.shape[1:], jnp.float32),
+            jax.ShapeDtypeStruct((tokens, lanes), jnp.float32),
             jax.ShapeDtypeStruct((lanes // 2, block), jnp.float32),
         ),
         in_specs=[vmem] * 4,
         out_specs=(vmem, vmem, vmem),
         scratch_shapes=[
             pltpu.VMEM((n1, tokens, kv_width), jnp.bfloat16),
-            pltpu.VMEM(rk.shape, rk.dtype),
+            pltpu.VMEM((n1, tokens, lanes), jnp.float32),
             pltpu.VMEM((n1, quarter * block, lanes), jnp.float32),
             pltpu.VMEM((n1, quarter * block, lanes), jnp.float32),
             pltpu.VMEM((quarter, block, lanes), jnp.float32),
@@ -173,11 +173,12 @@
             pltpu.VMEM((tokens, kv_width), jnp.bfloat16),
             pltpu.VMEM((2, tokens, kv_width), jnp.bfloat16),
             pltpu.VMEM((tokens, kv_width), jnp.float32),
+            pltpu.VMEM((n1, tokens, lanes), jnp.float32),
             pltpu.SemaphoreType.DMA((8, max(n1, n2))),
             pltpu.SemaphoreType.DMA((2, 3, 4)),
         ],
         compiler_params=pltpu.CompilerParams(collective_id=collective_id, has_side_effects=True),
-    )(rows, w, rk, g)
+    )(rows, w, dw, g)
 
 
 def shards(
@@ -235,23 +236,22 @@
     rank_gradient = (
         adapter_scale * jnp.concatenate([key_gradient_full, value_gradient_full], axis=1)
     ).astype(jnp.bfloat16)
-    every_rank = lax.all_gather(rank_gradient, "tensor", axis=0, tiled=True)
-    grad_a_term = lax.dot_general(
-        every_rank, rows, (((0,), (0,)), ((), ())), preferred_element_type=jnp.float32
-    )
-
-    down_weight = adapter_down_weight[0]
-    ranks = jnp.dot(rows, down_weight, preferred_element_type=jnp.float32)
-    block = tok_dev // tensors
     quarter = dps // 2
     width = kv_width // (dps * tensors)
     grad_t = keyvalue_gradient[0].T.reshape(2, quarter, tensors, width, tok_dev // tensors)
     grad_t = grad_t.transpose(0, 2, 1, 3, 4).reshape(2, keyvalue_half, tok_dev // tensors)
+    grad_t, rank_gradient = lax.optimization_barrier((grad_t, rank_gradient))
+    every_rank = lax.all_gather(rank_gradient, "tensor", axis=0, tiled=True)
+    grad_a_term = lax.dot_general(
+        every_rank, rows, (((0,), (0,)), ((), ())), preferred_element_type=jnp.float32
+    )
+
     frozen_output_local, local_rank_rows, up_block = tensor_sum(
         rows,
         keyvalue_weight,
-        ranks.reshape(tensors, block, ranks.shape[1]),
+        adapter_down_weight[0],
         grad_t,
+        tensors,
         dps,
         0,
     )

time: 105 us -> 103 us (0.981)
  matrix products: 8.22 us -> 6.64 us
    dot_general x1 -> x0, matrix products: 1.41 us -> none  [shards(): ranks = jnp.dot(rows, down_weight, preferred_element_type=jnp.float32)]
  transfers between devices with their start and end apart: 2 -> 2, of which waited for: 1 -> 1; matrix products, arithmetic and copies ran while one was open for 7% -> 5% of each run, Pallas kernels for 35% -> 36%
where the time goes in v17:
time: 103 us; the launch traced here: 102 us
  Pallas kernels  37.2 us (36%)
  blocking collectives  18.1 us (18%)
  between operations  14.2 us (14%)
  waiting for transfers between devices  10.8 us (10%)
  starting transfers between devices  8.76 us (9%)
  matrix products  6.64 us (6%)
  other arithmetic  3.44 us (3%)
  local copies, waits for them, and re-layouts  3.25 us (3%)
    pallas_call x1, Pallas kernels, tensor_sum(): pl.pallas_call(functools.partial(_tensor_sum_kernel, n1, n2), out_shape=(...  37.2 us
    all_gather x1, blocking collectives, shards(): every_rank = lax.all_gather(rank_gradient, 'tensor', axis=0, tiled=True)  18.1 us
    all_to_all x1, waiting for transfers between devices, shards(): lax.all_to_all(chosen.reshape(trials * tensors, select, normed_input), ('...  10.7 us
    all_to_all x1, starting transfers between devices, shards(): lax.all_to_all(chosen.reshape(trials * tensors, select, normed_input), ('...  8.72 us
    reduce_sum x1, other arithmetic, shards(): row_scale = lax.rsqrt(jnp.mean(raw * raw, axis=1) + norm_eps)  2.22 us
    dot_general x1, matrix products, shards(): jnp.einsum('tsr,rkf->tksf', onehot.reshape(trials, select, pool_dev), res...  2.12 us
  transfers between devices with their start and end apart: 2, of which 1 were waited for; matrix products, arithmetic and copies ran while one was open for 5% of the time, Pallas kernels for 36%

profile of v17, /device:TPU:1, one launch (start us, length us, event | category | flops | bytes accessed | tf_op | source)
XLA Modules:
  0.0 102.3 jit_solution(4728675052782203418)
XLA Ops:
  7.2 0.0 copy-start.1
  7.2 2.2 %multiply_reduce_fusion = f32[128]{0:T(128)S(1)} fusion(bf16[128,8192]{1,0:T(8,128)(2,1)} %param.7), kind=kLoop, calls=%fused_computation.2 | loop fusion | flops 3145600 | bytes 2097664 | tf_op jit(solution)/shard_map/reduce_sum | solution.py:215
  9.4 0.1 constant_dynamic-slice_fusion
  9.5 0.1 reshape.95
  9.6 1.2 %gather_fusion = f32[128]{0:T(128)S(1)} fusion(f32[128]{0:T(128)S(1)} %add_rsqrt_fusion, s32[1024]{0:T(1024)S(1)} %pad_clamp_fusion), kind=kCustom, calls=%fused_computation | custom fusion | bytes 1536 | tf_op jit(solution)/shard_map/jit(_take)/gather | solution.py:216
  10.9 0.1 gather.7
  10.9 0.1 and_select_fusion
  11.0 2.1 %multiply_convert_fusion = bf16[8,16,4,2048]{3,1,2,0:T(8,128)(2,1)} fusion(bf16[16,4,8,2048]{3,2,1,0:T(8,128)(2,1)S(1)} %bitcast.38, f32[4,2048]{1,0:T(4,128)S(1)} %mul.46, f32[8,16]{1,0:T(8,128)S(1)} %and_select_fusion, s32[8,16]{1,0:T(8,128)S(1)} %constant_dynamic-slice_fusion), kind=kOutput, calls=%fused_computation.1 | convolution fusion | flops 271597568 | bytes 4228096 | tf_op jit(solution)/shard_map/tsr,rkf->tksf/dot_general | solution.py:208
  13.2 8.7 %all-to-all-start = ((bf16[32,16,2048]{2,1,0:T(8,128)(2,1)}), bf16[32,16,2048]{2,1,0:T(8,128)(2,1)S(1)}, u32[]{:S(2)}, u32[]{:S(2)}) async-start(bf16[32,16,2048]{2,1,0:T(8,128)(2,1)} %bitcast.39), calls=%async_computation | async-start | bytes 4194304 | tf_op jit(solution)/shard_map/all_to_all | solution.py:219
  21.9 0.0 copy-start.4
  21.9 0.0 reduce-scatter.2.cloned.1.call-start
  22.0 0.3 copy.13
  22.2 0.8 copy.14
  23.1 0.2 fusion.5
  23.3 0.2 fusion.3
  23.5 18.1 %all_gather.3 = bf16[512,128]{0,1:T(8,128)(2,1)S(1)} all-gather(bf16[128,128]{0,1:T(8,128)(2,1)S(1)} %fusion.13), channel_id=1, replica_groups=mesh['trial'=8,'dp'=8,'tensor'=4] {'tensor'}, dimensions={0}, use_global_device_ids=true | all-gather | bytes 163840 | tf_op jit(solution)/shard_map/all_gather | solution.py:244
  41.5 10.7 %all-to-all-done = bf16[32,16,2048]{2,1,0:T(8,128)(2,1)S(1)} async-done(((bf16[32,16,2048]{2,1,0:T(8,128)(2,1)}), bf16[32,16,2048]{2,1,0:T(8,128)(2,1)S(1)}, u32[]{:S(2)}, u32[]{:S(2)}) %all-to-all-start) | async-done | bytes 2097184 | tf_op jit(solution)/shard_map/all_to_all | solution.py:219
  52.3 1.6 %fusion.20 = f32[128,2048]{1,0:T(8,128)} fusion(bf16[512,128]{0,1:T(8,128)(2,1)S(1)} %all_gather.3, bf16[512,2048]{1,0:T(8,128)(2,1)S(1)} %bitcast.35), kind=kOutput, calls=%fused_computation.32 | convolution fusion | flops 268435456 | bytes 3276800 | tf_op jit(solution)/shard_map/dot_general | solution.py:245
  53.9 0.0 reduce-scatter.2.cloned.1.call-update
  53.9 37.2 %shard_map.94 = (f32[128,2048]{1,0:T(8,128)}, f32[128,128]{1,0:T(8,128)}, f32[64,64]{1,0:T(8,128)}) custom-call(bf16[512,2048]{1,0:T(8,128)(2,1)} %bitcast.36, bf16[2048,2048]{1,0:T(8,128)(2,1)} %w_ref.1, bf16[2048,128]{1,0:T(8,128)(2,1)} %bitcast.43, bf16[2,1024,128]{2,1,0:T(8,128)(2,1)} %bitcast.37), custom_call_target="tpu_custom_call" | custom-call | tf_op jit(solution)/shard_map/pallas_call | solution.py:157
  91.2 1.3 %fusion.7 = f32[128,1024]{1,0:T(8,128)S(1)} fusion(bf16[64,2048]{1,0:T(8,128)(2,1)S(1)} %bitcast.46, f32[128,128]{1,0:T(8,128)} %get-tuple-element.10), kind=kOutput, calls=%fused_computation.12 | convolution fusion | flops 100663296 | bytes 720896 | tf_op jit(solution)/shard_map/dot_general | solution.py:261
  92.5 1.2 %fusion.10 = f32[128,1024]{1,0:T(8,128)S(1)} fusion(bf16[64,2048]{1,0:T(8,128)(2,1)S(1)} %bitcast.47, f32[128,128]{1,0:T(8,128)} %get-tuple-element.10), kind=kOutput, calls=%fused_computation.15 | convolution fusion | flops 100663296 | bytes 720896 | tf_op jit(solution)/shard_map/dot_general | solution.py:258
  93.7 1.1 %fusion.2 = f32[1,128,2048]{2,1,0:T(8,128)} fusion(f32[128,2048]{1,0:T(8,128)S(1)} %copy-done.2, f32[128,1024]{1,0:T(8,128)S(1)} %fusion.7, f32[128,1024]{1,0:T(8,128)S(1)} %fusion.10), kind=kLoop, calls=%fused_computation.7 | loop fusion | flops 786432 | bytes 3145728 | tf_op jit(solution)/shard_map/broadcast_in_dim | solution.py:271
  94.9 0.6 copy.22
  (20 shorter events, 0.1 us)
Async XLA Ops:
  7.2 3.9 %copy-start.1 = (bf16[128,8192]{1,0:T(8,128)(2,1)S(1)}, bf16[128,8192]{1,0:T(8,128)(2,1)}, u32[]{:S(2)}) copy-start(bf16[128,8192]{1,0:T(8,128)(2,1)} %param.7) | copy-start | bytes 6291460
  7.2 2.3 %copy-start.7 = (s32[8,512]{1,0:T(8,128)S(1)}, s32[8,512]{1,0:T(8,128)}, u32[]{:S(2)}) copy-start(s32[8,512]{1,0:T(8,128)} %param.9) | copy-start | bytes 49156
  7.2 3.8 %copy-start.5 = (f32[8192]{0:T(1024)S(1)}, f32[8192]{0:T(1024)}, u32[]{:S(2)}) copy-start(f32[8192]{0:T(1024)} %param.8) | copy-start | bytes 98308
  13.2 8.8 %copy-start.3 = (bf16[1,128,2048]{2,1,0:T(8,128)(2,1)S(1)}, bf16[1,128,2048]{2,1,0:T(8,128)(2,1)}, u32[]{:S(2)}) copy-start(bf16[1,128,2048]{2,1,0:T(8,128)(2,1)} %param.13) | copy-start | bytes 1572868
  13.2 39.1 %all-to-all-start = ((bf16[32,16,2048]{2,1,0:T(8,128)(2,1)}), bf16[32,16,2048]{2,1,0:T(8,128)(2,1)S(1)}, u32[]{:S(2)}, u32[]{:S(2)}) async-start(bf16[32,16,2048]{2,1,0:T(8,128)(2,1)} %bitcast.39), calls=%async_computation | async-start | bytes 4194304 | tf_op jit(solution)/shard_map/all_to_all | solution.py:219
  21.9 1.2 %copy-start.4 = (bf16[1,64,2048]{2,1,0:T(8,128)(2,1)S(1)}, bf16[1,64,2048]{2,1,0:T(8,128)(2,1)}, u32[]{:S(2)}) copy-start(bf16[1,64,2048]{2,1,0:T(8,128)(2,1)} %param.12) | copy-start | bytes 786436
  21.9 73.0 %reduce-scatter.2.cloned.1.call-start = ((), (), s32[]{:S(2)}) async-start(), calls=%async_computation.2 | async-start | bytes 1179648 | tf_op jit(solution)/shard_map/reduce_scatter | solution.py:268
  52.3 1.7 %copy-start = (bf16[32,16,2048]{2,1,0:T(8,128)(2,1)}, bf16[32,16,2048]{2,1,0:T(8,128)(2,1)S(1)}, u32[]{:S(2)}) copy-start(bf16[32,16,2048]{2,1,0:T(8,128)(2,1)S(1)} %all-to-all-done) | copy-start | bytes 6291460
  91.2 2.6 %copy-start.2 = (f32[128,2048]{1,0:T(8,128)S(1)}, f32[128,2048]{1,0:T(8,128)}, u32[]{:S(2)}) copy-start(f32[128,2048]{1,0:T(8,128)} %get-tuple-element.9) | copy-start | bytes 3145732
  92.5 2.3 %copy-start.6 = (f32[64,64]{1,0:T(8,128)S(1)}, f32[64,64]{1,0:T(8,128)}, u32[]{:S(2)}) copy-start(f32[64,64]{1,0:T(8,128)} %get-tuple-element.12) | copy-start | bytes 49156
Sparse Core Ops, SparseCore 0:
  54.0 37.0 reduce-scatter.1

commit v18 on v17

--- a/solution.py
+++ b/solution.py
@@ -14,7 +14,7 @@
 
 
 def _tensor_sum_kernel(
-    n1, n2, rows_ref, w_ref, dw_ref, g_ref,
+    n1, n2, rows_ref, w_ref, dw_ref, g_ref, up_ref,
     kv_out, rk_out, b_out,
     recv_kv, recv_rk, terms, recv_b1, partial, recv_b2, forward, outgoing, across_part, rk_ref, sems, kv_sems,
 ):
@@ -112,7 +112,13 @@
             across_part[rows, :] + recv_kv[1, rows, :].astype(jnp.float32)
         ).astype(forward.dtype)
         forward_copies.append(send_piece(forward, 2, p, first(across)))
-    kv_out[...] = own_part
+    xa_high = xa.astype(jnp.bfloat16)
+    xa_low = (xa - xa_high.astype(jnp.float32)).astype(jnp.bfloat16)
+    up = up_ref[...]
+    adapter = jnp.dot(xa_high, up, preferred_element_type=jnp.float32) + jnp.dot(
+        xa_low, up, preferred_element_type=jnp.float32
+    )
+    kv_out[...] = own_part + adapter_scale * adapter
     for p, copy in enumerate(own_copies):
         rows = pl.ds(p * step, step)
         copy.wait_recv()
@@ -146,7 +152,7 @@
         copy.wait_send()
 
 
-def tensor_sum(rows, w, dw, g, n1, n2, collective_id):
+def tensor_sum(rows, w, dw, g, up, n1, n2, collective_id):
     tokens = rows.shape[0] // n1
     kv_width = w.shape[1]
     quarter = n2 // 2
@@ -161,7 +167,7 @@
             jax.ShapeDtypeStruct((tokens, lanes), jnp.float32),
             jax.ShapeDtypeStruct((lanes // 2, block), jnp.float32),
         ),
-        in_specs=[vmem] * 4,
+        in_specs=[vmem] * 5,
         out_specs=(vmem, vmem, vmem),
         scratch_shapes=[
             pltpu.VMEM((n1, tokens, kv_width), jnp.bfloat16),
@@ -178,7 +184,7 @@
             pltpu.SemaphoreType.DMA((2, 3, 4)),
         ],
         compiler_params=pltpu.CompilerParams(collective_id=collective_id, has_side_effects=True),
-    )(rows, w, dw, g)
+    )(rows, w, dw, g, up)
 
 
 def shards(
@@ -246,24 +252,21 @@
         every_rank, rows, (((0,), (0,)), ((), ())), preferred_element_type=jnp.float32
     )
 
+    up_bf = adapter_up_weight[0]
+    block_up = jnp.zeros((2 * rank_index, kv_width), up_bf.dtype)
+    block_up = block_up.at[:rank_index, :keyvalue_half].set(up_bf[:, :keyvalue_half])
+    block_up = block_up.at[rank_index:, keyvalue_half:].set(up_bf[:, keyvalue_half:])
     frozen_output_local, local_rank_rows, up_block = tensor_sum(
         rows,
         keyvalue_weight,
         adapter_down_weight[0],
         grad_t,
+        block_up,
         tensors,
         dps,
         0,
     )
-    adapter_key = jnp.dot(
-        local_rank_rows[:, :rank_index], up_weight[:, :keyvalue_half], precision=highest_precision
-    )
-    adapter_value = jnp.dot(
-        local_rank_rows[:, rank_index:], up_weight[:, keyvalue_half:], precision=highest_precision
-    )
-    keyvalue_output = frozen_output_local + adapter_scale * jnp.concatenate(
-        [adapter_key, adapter_value], axis=1
-    )
+    keyvalue_output = frozen_output_local
 
     grad_a = lax.psum_scatter(grad_a_term, "dp", scatter_dimension=0, tiled=True)
 

time: 103 us -> 106 us (1.029)
  the two profiles are of different devices: /device:TPU:1 before, /device:TPU:2 now
where the time goes in v18:
time: 106 us
  Pallas kernels  37.1 us (35%)
  blocking collectives  18.8 us (18%)
  between operations  14.2 us (13%)
  waiting for transfers between devices  13.8 us (13%)
  starting transfers between devices  7.79 us (7%)
  local copies, waits for them, and re-layouts  7.2 us (7%)
  matrix products  4.12 us (4%)
  other arithmetic  2.88 us (3%)
    pallas_call x1, Pallas kernels, tensor_sum(): pl.pallas_call(functools.partial(_tensor_sum_kernel, n1, n2), out_shape=(...  37.1 us
    all_gather x1, blocking collectives, shards(): every_rank = lax.all_gather(rank_gradient, 'tensor', axis=0, tiled=True)  18.8 us
    all_to_all x1, waiting for transfers between devices, shards(): lax.all_to_all(chosen.reshape(trials * tensors, select, normed_input), ('...  8.63 us
    all_to_all x1, starting transfers between devices, shards(): lax.all_to_all(chosen.reshape(trials * tensors, select, normed_input), ('...  7.75 us
    reduce_scatter x1, waiting for transfers between devices, shards(): lax.psum_scatter(grad_a_term, 'dp', scatter_dimension=0, tiled=True)  5.17 us
    unnamed x17, local copies, waits for them, and re-layouts  3.98 us
    dot_general x1, matrix products, shards(): jnp.einsum('tsr,rkf->tksf', onehot.reshape(trials, select, pool_dev), res...  2.12 us
  transfers between devices with their start and end apart: 2, of which 2 were waited for; matrix products, arithmetic and copies ran while one was open for 1% of the time, Pallas kernels for 35%

profile of v18, /device:TPU:2, one launch (start us, length us, event | category | flops | bytes accessed | tf_op | source)
XLA Modules:
  0.0 105.8 jit_solution(11509944131006417488)
XLA Ops:
  7.2 0.0 copy-start.2
  7.2 0.9 constant_dynamic-slice_fusion
  8.1 0.1 reshape.156
  8.2 2.1 %multiply_reduce_fusion = f32[128]{0:T(128)S(1)} fusion(bf16[128,8192]{1,0:T(8,128)(2,1)} %param.11), kind=kLoop, calls=%fused_computation.2 | loop fusion | flops 3145600 | bytes 2097664 | tf_op jit(solution)/shard_map/reduce_sum | solution.py:221
  10.3 1.2 %gather_fusion = f32[128]{0:T(128)S(1)} fusion(f32[128]{0:T(128)S(1)} %add_rsqrt_fusion, s32[1024]{0:T(1024)S(1)} %pad_clamp_fusion), kind=kCustom, calls=%fused_computation | custom fusion | bytes 1536 | tf_op jit(solution)/shard_map/jit(_take)/gather | solution.py:222
  11.5 0.1 gather.7
  11.6 0.8 and_select_fusion
  12.4 2.1 %multiply_convert_fusion = bf16[8,16,4,2048]{3,1,2,0:T(8,128)(2,1)} fusion(bf16[16,4,8,2048]{3,2,1,0:T(8,128)(2,1)S(1)} %bitcast.37, f32[4,2048]{1,0:T(4,128)S(1)} %mul.40, f32[8,16]{1,0:T(8,128)S(1)} %and_select_fusion, s32[8,16]{1,0:T(8,128)S(1)} %constant_dynamic-slice_fusion), kind=kOutput, calls=%fused_computation.1 | convolution fusion | flops 271597568 | bytes 4228096 | tf_op jit(solution)/shard_map/tsr,rkf->tksf/dot_general | solution.py:214
  14.5 7.8 %all-to-all-start = ((bf16[32,16,2048]{2,1,0:T(8,128)(2,1)}), bf16[32,16,2048]{2,1,0:T(8,128)(2,1)S(1)}, u32[]{:S(2)}, u32[]{:S(2)}) async-start(bf16[32,16,2048]{2,1,0:T(8,128)(2,1)} %bitcast.38), calls=%async_computation | async-start | bytes 4194304 | tf_op jit(solution)/shard_map/all_to_all | solution.py:225
  22.3 0.0 copy-start.4
  22.3 0.0 reduce-scatter.2.cloned.1.call-start
  22.4 0.3 copy.13
  22.6 0.8 copy.14
  23.5 0.2 fusion.1
  23.7 0.2 fusion.3
  23.8 18.8 %all_gather.3 = bf16[512,128]{0,1:T(8,128)(2,1)S(1)} all-gather(bf16[128,128]{0,1:T(8,128)(2,1)S(1)} %fusion.6), channel_id=1, replica_groups=mesh['trial'=8,'dp'=8,'tensor'=4] {'tensor'}, dimensions={0}, use_global_device_ids=true | all-gather | bytes 163840 | tf_op jit(solution)/shard_map/all_gather | solution.py:250
  42.6 8.6 %all-to-all-done = bf16[32,16,2048]{2,1,0:T(8,128)(2,1)S(1)} async-done(((bf16[32,16,2048]{2,1,0:T(8,128)(2,1)}), bf16[32,16,2048]{2,1,0:T(8,128)(2,1)S(1)}, u32[]{:S(2)}, u32[]{:S(2)}) %all-to-all-start) | async-done | bytes 2097184 | tf_op jit(solution)/shard_map/all_to_all | solution.py:225
  51.3 1.7 %fusion.12 = f32[128,2048]{1,0:T(8,128)} fusion(bf16[512,128]{0,1:T(8,128)(2,1)S(1)} %all_gather.3, bf16[512,2048]{1,0:T(8,128)(2,1)S(1)} %bitcast.34), kind=kOutput, calls=%fused_computation.24 | convolution fusion | flops 268435456 | bytes 3276800 | tf_op jit(solution)/shard_map/dot_general | solution.py:251
  52.9 0.0 reduce-scatter.2.cloned.1.call-update
  53.0 0.8 copy-done.1
  53.8 37.1 %shard_map.94 = (f32[128,2048]{1,0:T(8,128)}, f32[128,128]{1,0:T(8,128)}, f32[64,64]{1,0:T(8,128)}) custom-call(bf16[512,2048]{1,0:T(8,128)(2,1)} %bitcast.35, bf16[2048,2048]{1,0:T(8,128)(2,1)} %w_ref.1, bf16[2048,128]{1,0:T(8,128)(2,1)} %bitcast.43, bf16[2,1024,128]{2,1,0:T(8,128)(2,1)} %bitcast.36, bf16[128,2048]{1,0:T(8,128)(2,1)} %copy-done.1), custom_call_target="tpu_custom_call" | custom-call | tf_op jit(solution)/shard_map/pallas_call | solution.py:163
  90.9 5.2 %reduce-scatter.2.cloned.1.call-done = f32[16,2048]{1,0:T(8,128)} async-done(((f32[128,2048]{1,0:T(8,128)}), f32[16,2048]{1,0:T(8,128)}) %reduce-scatter.2.cloned.1.call-update) | async-done | bytes 131088 | tf_op jit(solution)/shard_map/reduce_scatter | solution.py:271
  96.1 2.3 %copy.24 = f32[1,128,2048]{2,1,0:T(8,128)} copy(f32[1,128,2048]{2,1,0:T(8,128)} %bitcast.42) | data formatting | bytes 2097152
  98.4 0.6 copy.25
  (19 shorter events, 0.1 us)
Async XLA Ops:
  7.2 5.2 %copy-start.2 = (bf16[128,8192]{1,0:T(8,128)(2,1)S(1)}, bf16[128,8192]{1,0:T(8,128)(2,1)}, u32[]{:S(2)}) copy-start(bf16[128,8192]{1,0:T(8,128)(2,1)} %param.11) | copy-start | bytes 6291460
  7.2 5.2 %copy-start.5 = (f32[8192]{0:T(1024)S(1)}, f32[8192]{0:T(1024)}, u32[]{:S(2)}) copy-start(f32[8192]{0:T(1024)} %param.12) | copy-start | bytes 98308
  14.5 7.8 %copy-start.3 = (bf16[1,128,2048]{2,1,0:T(8,128)(2,1)S(1)}, bf16[1,128,2048]{2,1,0:T(8,128)(2,1)}, u32[]{:S(2)}) copy-start(bf16[1,128,2048]{2,1,0:T(8,128)(2,1)} %param.17) | copy-start | bytes 1572868
  14.5 36.7 %all-to-all-start = ((bf16[32,16,2048]{2,1,0:T(8,128)(2,1)}), bf16[32,16,2048]{2,1,0:T(8,128)(2,1)S(1)}, u32[]{:S(2)}, u32[]{:S(2)}) async-start(bf16[32,16,2048]{2,1,0:T(8,128)(2,1)} %bitcast.38), calls=%async_computation | async-start | bytes 4194304 | tf_op jit(solution)/shard_map/all_to_all | solution.py:225
  22.3 1.2 %copy-start.4 = (bf16[1,64,2048]{2,1,0:T(8,128)(2,1)S(1)}, bf16[1,64,2048]{2,1,0:T(8,128)(2,1)}, u32[]{:S(2)}) copy-start(bf16[1,64,2048]{2,1,0:T(8,128)(2,1)} %param.16) | copy-start | bytes 786436
  22.3 73.8 %reduce-scatter.2.cloned.1.call-start = ((), (), s32[]{:S(2)}) async-start(), calls=%async_computation.2 | async-start | bytes 1179648 | tf_op jit(solution)/shard_map/reduce_scatter | solution.py:271
  51.3 1.7 %copy-start = (bf16[32,16,2048]{2,1,0:T(8,128)(2,1)}, bf16[32,16,2048]{2,1,0:T(8,128)(2,1)S(1)}, u32[]{:S(2)}) copy-start(bf16[32,16,2048]{2,1,0:T(8,128)(2,1)S(1)} %all-to-all-done) | copy-start | bytes 6291460
  53.0 0.8 copy-start.1
  90.9 7.5 %copy-start.6 = (f32[64,64]{1,0:T(8,128)S(1)}, f32[64,64]{1,0:T(8,128)}, u32[]{:S(2)}) copy-start(f32[64,64]{1,0:T(8,128)} %get-tuple-element.34) | copy-start | bytes 49156
Sparse Core Ops, SparseCore 0:
  53.1 42.9 reduce-scatter.1

commit v19 on v17

--- a/solution.py
+++ b/solution.py
@@ -213,7 +213,10 @@
     )
     raw = residual_rows.astype(jnp.float32)
     row_scale = lax.rsqrt(jnp.mean(raw * raw, axis=1) + norm_eps)
-    picked_scale = jnp.take(row_scale, picks, axis=0)
+    picked_scale = jnp.sum(
+        jnp.where(picks[:, None] == jnp.arange(pool_dev, dtype=jnp.int32)[None, :], row_scale[None, :], 0.0),
+        axis=1,
+    )
     gain = input_norm_weight.reshape(1, tensors, 1, normed_input)
     chosen = (wide * picked_scale.reshape(trials, 1, select, 1) * gain).astype(jnp.bfloat16)
     arrived = lax.all_to_all(

time: 103 us -> 101 us (0.981)
  local copies, waits for them, and re-layouts: 3.25 us -> 2.03 us
    gather x2 -> x0, local copies, waits for them, and re-layouts: 1.3 us -> none  [shards(): picked_scale = jnp.take(row_scale, picks, axis=0)]
  transfers between devices with their start and end apart: 2 -> 2, of which waited for: 1 -> 1; matrix products, arithmetic and copies ran while one was open for 5% -> 5% of each run, Pallas kernels for 36% -> 37%
where the time goes in v19:
time: 101 us
  Pallas kernels  37.2 us (37%)
  blocking collectives  18.1 us (18%)
  between operations  14.2 us (14%)
  waiting for transfers between devices  10.8 us (11%)
  starting transfers between devices  8.76 us (9%)
  matrix products  6.64 us (7%)
  other arithmetic  3.52 us (3%)
  local copies, waits for them, and re-layouts  2.03 us (2%)
    pallas_call x1, Pallas kernels, tensor_sum(): pl.pallas_call(functools.partial(_tensor_sum_kernel, n1, n2), out_shape=(...  37.2 us
    all_gather x1, blocking collectives, shards(): every_rank = lax.all_gather(rank_gradient, 'tensor', axis=0, tiled=True)  18.1 us
    all_to_all x1, waiting for transfers between devices, shards(): lax.all_to_all(chosen.reshape(trials * tensors, select, normed_input), ('...  10.7 us
    all_to_all x1, starting transfers between devices, shards(): lax.all_to_all(chosen.reshape(trials * tensors, select, normed_input), ('...  8.72 us
    reduce_sum x1, other arithmetic, shards(): row_scale = lax.rsqrt(jnp.mean(raw * raw, axis=1) + norm_eps)  2.22 us
    dot_general x1, matrix products, shards(): jnp.einsum('tsr,rkf->tksf', onehot.reshape(trials, select, pool_dev), res...  2.1 us
  transfers between devices with their start and end apart: 2, of which 1 were waited for; matrix products, arithmetic and copies ran while one was open for 5% of the time, Pallas kernels for 37%

profile of v19, /device:TPU:1, one launch (start us, length us, event | category | flops | bytes accessed | tf_op | source)
XLA Modules:
  0.0 101.2 jit_solution(2697824052334190873)
XLA Ops:
  7.2 0.0 copy-start
  7.2 2.2 %multiply_reduce_fusion = f32[128]{0:T(128)S(1)} fusion(bf16[128,8192]{1,0:T(8,128)(2,1)} %param.7), kind=kLoop, calls=%fused_computation.1 | loop fusion | flops 3145600 | bytes 2097664 | tf_op jit(solution)/shard_map/reduce_sum | solution.py:215
  9.5 0.1 constant_dynamic-slice_fusion
  9.5 0.1 eq.48
  9.6 0.2 select_reduce_fusion
  9.8 0.1 mul.46
  9.9 0.0 copy-done.6
  9.9 2.1 %multiply_convert_fusion = bf16[8,16,4,2048]{3,1,2,0:T(8,128)(2,1)} fusion(bf16[16,4,8,2048]{3,2,1,0:T(8,128)(2,1)S(1)} %bitcast.36, f32[4,2048]{1,0:T(4,128)S(1)} %mul.49, f32[8,16]{1,0:T(8,128)S(1)} %mul.46, s32[8,16]{1,0:T(8,128)S(1)} %constant_dynamic-slice_fusion), kind=kOutput, calls=%fused_computation | convolution fusion | flops 271597568 | bytes 4228096 | tf_op jit(solution)/shard_map/tsr,rkf->tksf/dot_general | solution.py:208
  12.0 8.7 %all-to-all-start = ((bf16[32,16,2048]{2,1,0:T(8,128)(2,1)}), bf16[32,16,2048]{2,1,0:T(8,128)(2,1)S(1)}, u32[]{:S(2)}, u32[]{:S(2)}) async-start(bf16[32,16,2048]{2,1,0:T(8,128)(2,1)} %bitcast.37), calls=%async_computation | async-start | bytes 4194304 | tf_op jit(solution)/shard_map/all_to_all | solution.py:222
  20.7 0.0 copy-start.5
  20.8 0.0 reduce-scatter.2.cloned.1.call-start
  20.8 0.3 copy.16
  21.1 0.8 copy.17
  21.9 0.2 fusion.5
  22.1 0.2 fusion.3
  22.3 18.1 %all_gather.3 = bf16[512,128]{0,1:T(8,128)(2,1)S(1)} all-gather(bf16[128,128]{0,1:T(8,128)(2,1)S(1)} %fusion.13), channel_id=1, replica_groups=mesh['trial'=8,'dp'=8,'tensor'=4] {'tensor'}, dimensions={0}, use_global_device_ids=true | all-gather | bytes 163840 | tf_op jit(solution)/shard_map/all_gather | solution.py:247
  40.4 10.7 %all-to-all-done = bf16[32,16,2048]{2,1,0:T(8,128)(2,1)S(1)} async-done(((bf16[32,16,2048]{2,1,0:T(8,128)(2,1)}), bf16[32,16,2048]{2,1,0:T(8,128)(2,1)S(1)}, u32[]{:S(2)}, u32[]{:S(2)}) %all-to-all-start) | async-done | bytes 2097184 | tf_op jit(solution)/shard_map/all_to_all | solution.py:222
  51.1 1.7 %fusion.19 = f32[128,2048]{1,0:T(8,128)} fusion(bf16[512,128]{0,1:T(8,128)(2,1)S(1)} %all_gather.3, bf16[512,2048]{1,0:T(8,128)(2,1)S(1)} %bitcast.33), kind=kOutput, calls=%fused_computation.28 | convolution fusion | flops 268435456 | bytes 3276800 | tf_op jit(solution)/shard_map/dot_general | solution.py:248
  52.8 0.0 reduce-scatter.2.cloned.1.call-update
  52.8 37.2 %shard_map.94 = (f32[128,2048]{1,0:T(8,128)}, f32[128,128]{1,0:T(8,128)}, f32[64,64]{1,0:T(8,128)}) custom-call(bf16[512,2048]{1,0:T(8,128)(2,1)} %bitcast.34, bf16[2048,2048]{1,0:T(8,128)(2,1)} %w_ref.1, bf16[2048,128]{1,0:T(8,128)(2,1)} %bitcast.41, bf16[2,1024,128]{2,1,0:T(8,128)(2,1)} %bitcast.35), custom_call_target="tpu_custom_call" | custom-call | tf_op jit(solution)/shard_map/pallas_call | solution.py:157
  90.1 1.3 %fusion.7 = f32[128,1024]{1,0:T(8,128)S(1)} fusion(bf16[64,2048]{1,0:T(8,128)(2,1)S(1)} %bitcast.44, f32[128,128]{1,0:T(8,128)} %get-tuple-element.10), kind=kOutput, calls=%fused_computation.11 | convolution fusion | flops 100663296 | bytes 720896 | tf_op jit(solution)/shard_map/dot_general | solution.py:264
  91.4 1.2 %fusion.10 = f32[128,1024]{1,0:T(8,128)S(1)} fusion(bf16[64,2048]{1,0:T(8,128)(2,1)S(1)} %bitcast.45, f32[128,128]{1,0:T(8,128)} %get-tuple-element.10), kind=kOutput, calls=%fused_computation.14 | convolution fusion | flops 100663296 | bytes 720896 | tf_op jit(solution)/shard_map/dot_general | solution.py:261
  92.6 1.1 %fusion.2 = f32[1,128,2048]{2,1,0:T(8,128)} fusion(f32[128,2048]{1,0:T(8,128)S(1)} %copy-done.3, f32[128,1024]{1,0:T(8,128)S(1)} %fusion.7, f32[128,1024]{1,0:T(8,128)S(1)} %fusion.10), kind=kLoop, calls=%fused_computation.6 | loop fusion | flops 786432 | bytes 3145728 | tf_op jit(solution)/shard_map/broadcast_in_dim | solution.py:274
  93.7 0.6 copy.25
  (17 shorter events, 0.1 us)
Async XLA Ops:
  7.2 2.3 %copy-start = (s32[8,512]{1,0:T(8,128)S(1)}, s32[8,512]{1,0:T(8,128)}, u32[]{:S(2)}) copy-start(s32[8,512]{1,0:T(8,128)} %param.9) | copy-start | bytes 49156
  7.2 2.7 %copy-start.2 = (bf16[128,8192]{1,0:T(8,128)(2,1)S(1)}, bf16[128,8192]{1,0:T(8,128)(2,1)}, u32[]{:S(2)}) copy-start(bf16[128,8192]{1,0:T(8,128)(2,1)} %param.7) | copy-start | bytes 6291460
  7.2 2.7 %copy-start.6 = (f32[8192]{0:T(1024)S(1)}, f32[8192]{0:T(1024)}, u32[]{:S(2)}) copy-start(f32[8192]{0:T(1024)} %param.8) | copy-start | bytes 98308
  12.0 8.8 %copy-start.4 = (bf16[1,128,2048]{2,1,0:T(8,128)(2,1)S(1)}, bf16[1,128,2048]{2,1,0:T(8,128)(2,1)}, u32[]{:S(2)}) copy-start(bf16[1,128,2048]{2,1,0:T(8,128)(2,1)} %param.13) | copy-start | bytes 1572868
  12.0 39.1 %all-to-all-start = ((bf16[32,16,2048]{2,1,0:T(8,128)(2,1)}), bf16[32,16,2048]{2,1,0:T(8,128)(2,1)S(1)}, u32[]{:S(2)}, u32[]{:S(2)}) async-start(bf16[32,16,2048]{2,1,0:T(8,128)(2,1)} %bitcast.37), calls=%async_computation | async-start | bytes 4194304 | tf_op jit(solution)/shard_map/all_to_all | solution.py:222
  20.7 1.2 %copy-start.5 = (bf16[1,64,2048]{2,1,0:T(8,128)(2,1)S(1)}, bf16[1,64,2048]{2,1,0:T(8,128)(2,1)}, u32[]{:S(2)}) copy-start(bf16[1,64,2048]{2,1,0:T(8,128)(2,1)} %param.12) | copy-start | bytes 786436
  20.8 73.0 %reduce-scatter.2.cloned.1.call-start = ((), (), s32[]{:S(2)}) async-start(), calls=%async_computation.2 | async-start | bytes 1179648 | tf_op jit(solution)/shard_map/reduce_scatter | solution.py:271
  51.1 1.7 %copy-start.1 = (bf16[32,16,2048]{2,1,0:T(8,128)(2,1)}, bf16[32,16,2048]{2,1,0:T(8,128)(2,1)S(1)}, u32[]{:S(2)}) copy-start(bf16[32,16,2048]{2,1,0:T(8,128)(2,1)S(1)} %all-to-all-done) | copy-start | bytes 6291460
  90.0 2.6 %copy-start.3 = (f32[128,2048]{1,0:T(8,128)S(1)}, f32[128,2048]{1,0:T(8,128)}, u32[]{:S(2)}) copy-start(f32[128,2048]{1,0:T(8,128)} %get-tuple-element.9) | copy-start | bytes 3145732
  91.4 2.3 %copy-start.7 = (f32[64,64]{1,0:T(8,128)S(1)}, f32[64,64]{1,0:T(8,128)}, u32[]{:S(2)}) copy-start(f32[64,64]{1,0:T(8,128)} %get-tuple-element.12) | copy-start | bytes 49156
Sparse Core Ops, SparseCore 0:
  52.9 37.0 reduce-scatter.1

commit v20 on v19

--- a/solution.py
+++ b/solution.py
@@ -212,7 +212,8 @@
         preferred_element_type=jnp.float32,
     )
     raw = residual_rows.astype(jnp.float32)
-    row_scale = lax.rsqrt(jnp.mean(raw * raw, axis=1) + norm_eps)
+    lane_groups = lax.optimization_barrier((raw * raw).reshape(pool_dev, -1, 128).sum(axis=1))
+    row_scale = lax.rsqrt(lane_groups.sum(axis=1) / raw.shape[1] + norm_eps)
     picked_scale = jnp.sum(
         jnp.where(picks[:, None] == jnp.arange(pool_dev, dtype=jnp.int32)[None, :], row_scale[None, :], 0.0),
         axis=1,

time: 101 us -> 104 us (1.030)
  local copies, waits for them, and re-layouts: 2.03 us -> 4.05 us
    unnamed x0 -> x1, other arithmetic: none -> 2.04 us
    unnamed x18 -> x19, local copies, waits for them, and re-layouts: 0.92 us -> 2.95 us
    reduce_sum x1 -> x2, other arithmetic: 2.22 us -> 0.68 us  [the longest x1 0.58 us: shards(): (raw * raw).reshape(pool_dev, -1, 128).sum(axis=1)]
  transfers between devices with their start and end apart: 2 -> 2, of which waited for: 1 -> 1; matrix products, arithmetic and copies ran while one was open for 5% -> 5% of each run, Pallas kernels for 37% -> 36%
where the time goes in v20:
time: 104 us
  Pallas kernels  37.2 us (36%)
  blocking collectives  18.1 us (17%)
  between operations  14.2 us (14%)
  waiting for transfers between devices  10.8 us (10%)
  starting transfers between devices  8.76 us (8%)
  matrix products  6.63 us (6%)
  local copies, waits for them, and re-layouts  4.05 us (4%)
  other arithmetic  4.02 us (4%)
    pallas_call x1, Pallas kernels, tensor_sum(): pl.pallas_call(functools.partial(_tensor_sum_kernel, n1, n2), out_shape=(...  37.2 us
    all_gather x1, blocking collectives, shards(): every_rank = lax.all_gather(rank_gradient, 'tensor', axis=0, tiled=True)  18.1 us
    all_to_all x1, waiting for transfers between devices, shards(): lax.all_to_all(chosen.reshape(trials * tensors, select, normed_input), ('...  10.7 us
    all_to_all x1, starting transfers between devices, shards(): lax.all_to_all(chosen.reshape(trials * tensors, select, normed_input), ('...  8.72 us
    unnamed x19, local copies, waits for them, and re-layouts  2.95 us
    dot_general x1, matrix products, shards(): jnp.einsum('tsr,rkf->tksf', onehot.reshape(trials, select, pool_dev), res...  2.1 us
  transfers between devices with their start and end apart: 2, of which 1 were waited for; matrix products, arithmetic and copies ran while one was open for 5% of the time, Pallas kernels for 36%

profile of v20, /device:TPU:1, one launch (start us, length us, event | category | flops | bytes accessed | tf_op | source)
XLA Modules:
  0.0 103.7 jit_solution(2079899589445944434)
XLA Ops:
  7.2 0.7 copy-done
  7.9 0.1 constant_dynamic-slice_fusion
  8.0 0.1 eq.48
  8.0 2.0 %multiply_bitcast_fusion = f32[16,8,64,128]{3,1,2,0:T(8,128)S(1)} fusion(bf16[128,8192]{1,0:T(8,128)(2,1)} %param.7), kind=kLoop, calls=%fused_computation.2 | loop fusion | flops 2097152 | bytes 6291456
  10.1 0.7 copy.20
  10.9 0.6 bitcast_reduce_fusion
  11.4 0.1 reduce_sum.28
  11.6 0.2 select_reduce_fusion
  11.7 0.1 mul.46
  11.9 0.6 copy-done.2
  12.4 2.1 %multiply_convert_fusion = bf16[8,16,4,2048]{3,1,2,0:T(8,128)(2,1)} fusion(bf16[16,4,8,2048]{3,2,1,0:T(8,128)(2,1)S(1)} %bitcast.39, f32[4,2048]{1,0:T(4,128)S(1)} %mul.49, f32[8,16]{1,0:T(8,128)S(1)} %mul.46, s32[8,16]{1,0:T(8,128)S(1)} %constant_dynamic-slice_fusion), kind=kOutput, calls=%fused_computation.1 | convolution fusion | flops 271597568 | bytes 4228096 | tf_op jit(solution)/shard_map/tsr,rkf->tksf/dot_general | solution.py:208
  14.5 8.7 %all-to-all-start = ((bf16[32,16,2048]{2,1,0:T(8,128)(2,1)}), bf16[32,16,2048]{2,1,0:T(8,128)(2,1)S(1)}, u32[]{:S(2)}, u32[]{:S(2)}) async-start(bf16[32,16,2048]{2,1,0:T(8,128)(2,1)} %bitcast.41), calls=%async_computation | async-start | bytes 4194304 | tf_op jit(solution)/shard_map/all_to_all | solution.py:223
  23.3 0.3 copy.16
  23.6 0.8 copy.17
  24.5 0.2 fusion.3
  24.6 0.2 fusion.5
  24.8 18.1 %all_gather.3 = bf16[512,128]{0,1:T(8,128)(2,1)S(1)} all-gather(bf16[128,128]{0,1:T(8,128)(2,1)S(1)} %fusion.13), channel_id=1, replica_groups=mesh['trial'=8,'dp'=8,'tensor'=4] {'tensor'}, dimensions={0}, use_global_device_ids=true | all-gather | bytes 163840 | tf_op jit(solution)/shard_map/all_gather | solution.py:248
  42.9 10.7 %all-to-all-done = bf16[32,16,2048]{2,1,0:T(8,128)(2,1)S(1)} async-done(((bf16[32,16,2048]{2,1,0:T(8,128)(2,1)}), bf16[32,16,2048]{2,1,0:T(8,128)(2,1)S(1)}, u32[]{:S(2)}, u32[]{:S(2)}) %all-to-all-start) | async-done | bytes 2097184 | tf_op jit(solution)/shard_map/all_to_all | solution.py:223
  53.6 1.6 %fusion.19 = f32[128,2048]{1,0:T(8,128)} fusion(bf16[512,128]{0,1:T(8,128)(2,1)S(1)} %all_gather.3, bf16[512,2048]{1,0:T(8,128)(2,1)S(1)} %bitcast.37), kind=kOutput, calls=%fused_computation.29 | convolution fusion | flops 268435456 | bytes 3276800 | tf_op jit(solution)/shard_map/dot_general | solution.py:249
  55.3 37.2 %shard_map.94 = (f32[128,2048]{1,0:T(8,128)}, f32[128,128]{1,0:T(8,128)}, f32[64,64]{1,0:T(8,128)}) custom-call(bf16[512,2048]{1,0:T(8,128)(2,1)} %bitcast.38, bf16[2048,2048]{1,0:T(8,128)(2,1)} %w_ref.1, bf16[2048,128]{1,0:T(8,128)(2,1)} %bitcast.45, bf16[2,1024,128]{2,1,0:T(8,128)(2,1)} %bitcast.40), custom_call_target="tpu_custom_call" | custom-call | tf_op jit(solution)/shard_map/pallas_call | solution.py:157
  92.6 1.3 %fusion.10 = f32[128,1024]{1,0:T(8,128)S(1)} fusion(bf16[64,2048]{1,0:T(8,128)(2,1)S(1)} %bitcast.48, f32[128,128]{1,0:T(8,128)} %get-tuple-element.10), kind=kOutput, calls=%fused_computation.15 | convolution fusion | flops 100663296 | bytes 720896 | tf_op jit(solution)/shard_map/dot_general | solution.py:262
  93.9 1.3 %fusion.7 = f32[128,1024]{1,0:T(8,128)S(1)} fusion(bf16[64,2048]{1,0:T(8,128)(2,1)S(1)} %bitcast.49, f32[128,128]{1,0:T(8,128)} %get-tuple-element.10), kind=kOutput, calls=%fused_computation.12 | convolution fusion | flops 100663296 | bytes 720896 | tf_op jit(solution)/shard_map/dot_general | solution.py:265
  95.1 1.1 %fusion.2 = f32[1,128,2048]{2,1,0:T(8,128)} fusion(f32[128,2048]{1,0:T(8,128)S(1)} %copy-done.3, f32[128,1024]{1,0:T(8,128)S(1)} %fusion.7, f32[128,1024]{1,0:T(8,128)S(1)} %fusion.10), kind=kLoop, calls=%fused_computation.7 | loop fusion | flops 786432 | bytes 3145728 | tf_op jit(solution)/shard_map/broadcast_in_dim | solution.py:275
  96.2 0.6 copy.26
  (20 shorter events, 0.1 us)
Async XLA Ops:
  7.2 0.7 copy-start
  10.8 1.0 copy-start.6
  10.8 1.6 %copy-start.2 = (bf16[128,8192]{1,0:T(8,128)(2,1)S(1)}, bf16[128,8192]{1,0:T(8,128)(2,1)}, u32[]{:S(2)}) copy-start(bf16[128,8192]{1,0:T(8,128)(2,1)} %param.7) | copy-start | bytes 6291460
  14.5 8.8 %copy-start.4 = (bf16[1,128,2048]{2,1,0:T(8,128)(2,1)S(1)}, bf16[1,128,2048]{2,1,0:T(8,128)(2,1)}, u32[]{:S(2)}) copy-start(bf16[1,128,2048]{2,1,0:T(8,128)(2,1)} %param.13) | copy-start | bytes 1572868
  14.5 39.1 %all-to-all-start = ((bf16[32,16,2048]{2,1,0:T(8,128)(2,1)}), bf16[32,16,2048]{2,1,0:T(8,128)(2,1)S(1)}, u32[]{:S(2)}, u32[]{:S(2)}) async-start(bf16[32,16,2048]{2,1,0:T(8,128)(2,1)} %bitcast.41), calls=%async_computation | async-start | bytes 4194304 | tf_op jit(solution)/shard_map/all_to_all | solution.py:223
  23.3 1.2 %copy-start.5 = (bf16[1,64,2048]{2,1,0:T(8,128)(2,1)S(1)}, bf16[1,64,2048]{2,1,0:T(8,128)(2,1)}, u32[]{:S(2)}) copy-start(bf16[1,64,2048]{2,1,0:T(8,128)(2,1)} %param.12) | copy-start | bytes 786436
  23.3 73.0 %reduce-scatter.2.cloned.1.call-start = ((), (), s32[]{:S(2)}) async-start(), calls=%async_computation.2 | async-start | bytes 1179648 | tf_op jit(solution)/shard_map/reduce_scatter | solution.py:272
  53.6 1.7 %copy-start.1 = (bf16[32,16,2048]{2,1,0:T(8,128)(2,1)}, bf16[32,16,2048]{2,1,0:T(8,128)(2,1)S(1)}, u32[]{:S(2)}) copy-start(bf16[32,16,2048]{2,1,0:T(8,128)(2,1)S(1)} %all-to-all-done) | copy-start | bytes 6291460
  92.6 2.6 %copy-start.3 = (f32[128,2048]{1,0:T(8,128)S(1)}, f32[128,2048]{1,0:T(8,128)}, u32[]{:S(2)}) copy-start(f32[128,2048]{1,0:T(8,128)} %get-tuple-element.9) | copy-start | bytes 3145732
  93.8 2.4 %copy-start.7 = (f32[64,64]{1,0:T(8,128)S(1)}, f32[64,64]{1,0:T(8,128)}, u32[]{:S(2)}) copy-start(f32[64,64]{1,0:T(8,128)} %get-tuple-element.12) | copy-start | bytes 49156
Sparse Core Ops, SparseCore 0:
  55.4 37.1 reduce-scatter.1
